TPU v7x, 32 devices: a whole 2x2x4 slice. The times are simulated.
32 devices in a mesh: slab: 16 (over z, x, core), filt: 2 (over y).
Axes of the slice: x: 2, y: 2, z: 4, core: 2. Of those that a mesh axis runs over, the one named last changes fastest.
Arguments:
- volume: bfloat16 [16, 8, 64, 256], P('slab', 'filt'), may hold values from -6 to 6
- kernel_one: bfloat16 [27, 64, 64], replicated, may hold values from -0.15625 to 0.15625
- bias_one: bfloat16 [64], replicated, may hold values from -2.5 to 2.5
- kernel_two: bfloat16 [27, 128, 64], P(None, 'filt'), may hold values from -0.15625 to 0.15625
- bias_two: bfloat16 [128], P('filt'), may hold values from -2.5 to 2.5
- kernel_three: bfloat16 [27, 128, 128], P(None, 'filt'), may hold values from -0.109375 to 0.109375
- bias_three: bfloat16 [128], P('filt'), may hold values from -2.5 to 2.5
Outputs:
- skip_one: bfloat16 [16, 8, 64, 256], P('slab', 'filt')
- features_two: bfloat16 [16, 4, 128, 128], P('slab', None, 'filt')
All inputs are finite; a program needn't handle non-finite values.
Results may differ from a plain program's by a relative error of at most 0.0057.
Values may be sent and summed in bfloat16 or wider, within the bound.
No kernel may reach another device: no remote copies, remote signals or barrier semaphores. Data moves between devices by JAX's collectives and lax.ppermute only.
A program may use at most 64 MiB of HBM per device.

v0:
```python
import jax
import jax.numpy as jnp
from jax import lax
from jax.sharding import PartitionSpec as P


def extended(block, sides, width):
    for axis, dim in sides:
        count = lax.axis_size(axis)
        forward = [(i, i + 1) for i in range(count - 1)]
        backward = [(target, source) for source, target in forward]
        low = lax.ppermute(
            lax.slice_in_dim(block, block.shape[dim] - width, None, axis=dim), axis, forward
        )
        high = lax.ppermute(lax.slice_in_dim(block, 0, width, axis=dim), axis, backward)
        block = jnp.concatenate([low, block, high], axis=dim)
    return block


def pad_columns(field):
    return jnp.pad(field, ((0, 0), (0, 0), (0, 0), (1, 1)))


def accumulate(total, padded, kernel):
    planes, rows, chans, cols = total.shape
    for kd in range(3):
        for kh in range(3):
            for kw in range(3):
                tap = 9 * kd + 3 * kh + kw
                total = total + jnp.einsum(
                    "oc,dhcw->dhow",
                    kernel[tap],
                    padded[kd : kd + planes, kh : kh + rows, :, kw : kw + cols],
                    preferred_element_type=jnp.float32,
                )
    return total


def finish(total, bias):
    return jnp.maximum(total + bias.astype(jnp.float32)[None, None, :, None], 0.0).astype(
        jnp.bfloat16
    )


def per_device(volume, kernel_one, bias_one, kernel_two, bias_two, kernel_three, bias_three):
    planes, rows, chans, cols = volume.shape
    rimmed = extended(volume, (("slab", 0), ("filt", 1)), 1)
    start_one = jnp.zeros((planes, rows, kernel_one.shape[1], cols), jnp.float32)
    skip_one = finish(accumulate(start_one, pad_columns(rimmed), kernel_one), bias_one)
    pooled = jnp.max(skip_one.reshape(planes, rows // 2, 2, chans, cols // 2, 2), axis=(2, 5))
    full_rows = lax.all_gather(pooled, "filt", axis=1, tiled=True)
    planed = extended(full_rows, (("slab", 0),), 1)
    padded = jnp.pad(planed, ((0, 0), (1, 1), (0, 0), (1, 1)))
    height = full_rows.shape[1]
    width = full_rows.shape[3]
    start_two = jnp.zeros((planes, height, kernel_two.shape[1], width), jnp.float32)
    hidden = finish(accumulate(start_two, padded, kernel_two), bias_two)
    hidden_planes = extended(hidden, (("slab", 0),), 1)
    start_three = jnp.zeros((planes, height, kernel_three.shape[1], width), jnp.float32)
    piece_padded = jnp.pad(
        lax.all_gather(hidden_planes, "filt", axis=2, tiled=True), ((0, 0), (1, 1), (0, 0), (1, 1))
    )
    summed = accumulate(start_three, piece_padded, kernel_three)
    features_two = finish(summed, bias_three)
    return (skip_one, features_two)


def solution(mesh):
    return jax.shard_map(
        per_device,
        mesh=mesh,
        in_specs=(
            P("slab", "filt", None, None),
            P(),
            P(),
            P(None, "filt", None),
            P("filt"),
            P(None, "filt", None),
            P("filt"),
        ),
        out_specs=(P("slab", "filt", None, None), P("slab", None, "filt", None)),
        check_vma=False,
    )
```

profile of v0, /device:TPU:16, one launch (start us, length us, event | category | flops | bytes accessed | tf_op | source)
XLA Modules:
  0.0 69.1 jit_solution(7843316542027232377)
XLA Ops:
  0.6 2.1 %collective-permute-start = (bf16[1,4,64,256]{3,2,1,0:T(8,128)(2,1)}, bf16[1,4,64,256]{3,2,1,0:T(8,128)(2,1)S(1)}, u32[]{:S(2)}, u32[]{:S(2)}) collective-permute-start(bf16[1,4,64,256]{3,2,1,0:T(8,128)(2,1)} %param.7), channel_id=1, source_target_pairs={{0,2},{2,4},{4,6},{6,8},{8,10},{10,12},{12,14},{14,16},{16,18},{18... | collective-permute-start | bytes 393224 | tf_op jit(solution)/shard_map/ppermute | solution.py:12
  2.7 4.5 %collective-permute-start.1 = (bf16[1,4,64,256]{3,2,1,0:T(8,128)(2,1)}, bf16[1,4,64,256]{3,2,1,0:T(8,128)(2,1)S(1)}, u32[]{:S(2)}, u32[]{:S(2)}) collective-permute-start(bf16[1,4,64,256]{3,2,1,0:T(8,128)(2,1)} %param.7), channel_id=1, source_target_pairs={{2,0},{4,2},{6,4},{8,6},{10,8},{12,10},{14,12},{16,14},{18,16},{20... | collective-permute-start | bytes 393224 | tf_op jit(solution)/shard_map/ppermute | solution.py:15
  7.3 0.7 convert_element_type.24
  7.9 0.3 collective-permute-done
  8.2 0.9 %constant_dynamic-update-slice_fusion.1 = bf16[3,4,64,256]{3,2,1,0:T(8,128)(2,1)S(1)} fusion(bf16[3,4,64,256]{3,2,1,0:T(8,128)(2,1)S(1)} %constant_dynamic-update-slice_fusion.2, bf16[1,4,64,256]{3,2,1,0:T(8,128)(2,1)} %param.7), kind=kLoop, calls=%fused_computation.433 | loop fusion | bytes 262144
  9.1 1.0 %collective-permute-done.1 = bf16[1,4,64,256]{3,2,1,0:T(8,128)(2,1)S(1)} collective-permute-done((bf16[1,4,64,256]{3,2,1,0:T(8,128)(2,1)}, bf16[1,4,64,256]{3,2,1,0:T(8,128)(2,1)S(1)}, u32[]{:S(2)}, u32[]{:S(2)}) %collective-permute-start.1) | collective-permute-done | bytes 131104 | tf_op jit(solution)/shard_map/ppermute | solution.py:15
  10.1 3.4 %collective-permute-start.2 = (bf16[3,1,64,256]{3,2,1,0:T(8,128)(2,1)S(1)}, bf16[3,1,64,256]{3,2,1,0:T(8,128)(2,1)S(1)}, u32[]{:S(2)}, u32[]{:S(2)}) collective-permute-start(bf16[3,1,64,256]{3,2,1,0:T(8,128)(2,1)S(1)} %get-tuple-element.2), channel_id=1, source_target_pairs={{0,1},{2,3},{4,5},{6,7},{8,9},{10,11},{12,13},{14,15},{16,17},{18,... | collective-permute-start | bytes 294920 | tf_op jit(solution)/shard_map/ppermute | solution.py:12
  13.5 1.3 %collective-permute-start.3 = (bf16[3,1,64,256]{3,2,1,0:T(8,128)(2,1)S(1)}, bf16[3,1,64,256]{3,2,1,0:T(8,128)(2,1)S(1)}, u32[]{:S(2)}, u32[]{:S(2)}) collective-permute-start(bf16[3,1,64,256]{3,2,1,0:T(8,128)(2,1)S(1)} %get-tuple-element.3), channel_id=1, source_target_pairs={{1,0},{3,2},{5,4},{7,6},{9,8},{11,10},{13,12},{15,14},{17,16},{19,... | collective-permute-start | bytes 294920 | tf_op jit(solution)/shard_map/ppermute | solution.py:15
  15.0 1.4 %collective-permute-done.2 = bf16[3,1,64,256]{3,2,1,0:T(8,128)(2,1)S(1)} collective-permute-done((bf16[3,1,64,256]{3,2,1,0:T(8,128)(2,1)S(1)}, bf16[3,1,64,256]{3,2,1,0:T(8,128)(2,1)S(1)}, u32[]{:S(2)}, u32[]{:S(2)}) %collective-permute-start.2) | collective-permute-done | bytes 98336 | tf_op jit(solution)/shard_map/ppermute | solution.py:12
  16.5 4.1 %collective-permute-done.3 = bf16[3,1,64,256]{3,2,1,0:T(8,128)(2,1)S(1)} collective-permute-done((bf16[3,1,64,256]{3,2,1,0:T(8,128)(2,1)S(1)}, bf16[3,1,64,256]{3,2,1,0:T(8,128)(2,1)S(1)}, u32[]{:S(2)}, u32[]{:S(2)}) %collective-permute-start.3) | collective-permute-done | bytes 98336 | tf_op jit(solution)/shard_map/ppermute | solution.py:15
  20.6 0.4 fusion.60
  21.2 0.2 fusion.125
  21.4 0.2 fusion.122
  21.7 0.2 fusion.119
  21.9 0.2 convolution_bitcast_fusion
  22.4 0.2 convolution_bitcast_fusion.3
  22.8 0.2 convolution_bitcast_fusion.6
  23.2 0.2 convolution_bitcast_fusion.9
  23.6 0.2 convolution_add_fusion.10
  25.1 0.5 copy-done
  25.8 0.2 convolution_add_fusion.1
  26.5 0.3 fusion.22
  27.0 0.6 reduce_max.11
  27.7 4.6 %all-gather = bf16[4,64,128]{2,1,0:T(8,128)(2,1)S(1)} all-gather(bf16[2,64,128]{2,1,0:T(8,128)(2,1)S(1)} %copy.11), channel_id=2, replica_groups=mesh['slab'=16,'filt'=2] {'filt'}, dimensions={0}, use_global_device_ids=true | all-gather | bytes 98304 | tf_op jit(solution)/shard_map/all_gather | solution.py:51
  32.3 1.9 %collective-permute-start.4 = (bf16[1,4,64,128]{3,2,1,0:T(8,128)(2,1)S(1)}, bf16[1,4,64,128]{3,2,1,0:T(8,128)(2,1)S(1)}, u32[]{:S(2)}, u32[]{:S(2)}) collective-permute-start(bf16[1,4,64,128]{3,2,1,0:T(8,128)(2,1)S(1)} %bitcast.832), channel_id=1, source_target_pairs={{0,2},{2,4},{4,6},{6,8},{8,10},{10,12},{12,14},{14,16},{16,18},{18... | collective-permute-start | bytes 196616 | tf_op jit(solution)/shard_map/ppermute | solution.py:12
  34.2 4.5 %collective-permute-start.5 = (bf16[1,4,64,128]{3,2,1,0:T(8,128)(2,1)S(1)}, bf16[1,4,64,128]{3,2,1,0:T(8,128)(2,1)S(1)}, u32[]{:S(2)}, u32[]{:S(2)}) collective-permute-start(bf16[1,4,64,128]{3,2,1,0:T(8,128)(2,1)S(1)} %bitcast.833), channel_id=1, source_target_pairs={{2,0},{4,2},{6,4},{8,6},{10,8},{12,10},{14,12},{16,14},{18,16},{20... | collective-permute-start | bytes 196616 | tf_op jit(solution)/shard_map/ppermute | solution.py:15
  38.8 1.9 %collective-permute-done.5 = bf16[1,4,64,128]{3,2,1,0:T(8,128)(2,1)S(1)} collective-permute-done((bf16[1,4,64,128]{3,2,1,0:T(8,128)(2,1)S(1)}, bf16[1,4,64,128]{3,2,1,0:T(8,128)(2,1)S(1)}, u32[]{:S(2)}, u32[]{:S(2)}) %collective-permute-start.5) | collective-permute-done | bytes 65568 | tf_op jit(solution)/shard_map/ppermute | solution.py:15
  41.0 0.2 fusion.134
  41.4 0.2 convolution_bitcast_fusion.28
  41.7 0.2 convolution_bitcast_fusion.29
  42.0 0.2 convolution_bitcast_fusion.31
  42.3 0.2 convolution_bitcast_fusion.22
  42.5 0.2 convolution_bitcast_fusion.23
  42.9 0.2 convolution_bitcast_fusion.25
  43.1 0.2 convolution_add_fusion.40
  43.3 0.2 convolution_add_fusion.39
  44.0 0.2 convolution_add_fusion.35
  44.2 0.2 convolution_add_fusion.34
  44.6 0.2 convolution_add_fusion.32
  44.9 0.2 convolution_add_fusion.31
  45.4 0.2 convolution_add_fusion.28
  45.8 0.2 fusion.46
  46.2 1.9 %collective-permute-start.6 = (bf16[1,4,64,128]{3,2,1,0:T(8,128)(2,1)S(1)}, bf16[1,4,64,128]{3,2,1,0:T(8,128)(2,1)S(1)}, u32[]{:S(2)}, u32[]{:S(2)}) collective-permute-start(bf16[1,4,64,128]{3,2,1,0:T(8,128)(2,1)S(1)} %fusion.54), channel_id=1, source_target_pairs={{0,2},{2,4},{4,6},{6,8},{8,10},{10,12},{12,14},{14,16},{16,18},{18... | collective-permute-start | bytes 196616 | tf_op jit(solution)/shard_map/ppermute | solution.py:12
  48.2 4.6 %collective-permute-start.7 = (bf16[1,4,64,128]{3,2,1,0:T(8,128)(2,1)S(1)}, bf16[1,4,64,128]{3,2,1,0:T(8,128)(2,1)S(1)}, u32[]{:S(2)}, u32[]{:S(2)}) collective-permute-start(bf16[1,4,64,128]{3,2,1,0:T(8,128)(2,1)S(1)} %fusion.54), channel_id=1, source_target_pairs={{2,0},{4,2},{6,4},{8,6},{10,8},{12,10},{14,12},{16,14},{18,16},{20... | collective-permute-start | bytes 196616 | tf_op jit(solution)/shard_map/ppermute | solution.py:15
  52.8 1.9 %collective-permute-done.7 = bf16[1,4,64,128]{3,2,1,0:T(8,128)(2,1)S(1)} collective-permute-done((bf16[1,4,64,128]{3,2,1,0:T(8,128)(2,1)S(1)}, bf16[1,4,64,128]{3,2,1,0:T(8,128)(2,1)S(1)}, u32[]{:S(2)}, u32[]{:S(2)}) %collective-permute-start.7) | collective-permute-done | bytes 65568 | tf_op jit(solution)/shard_map/ppermute | solution.py:15
  54.7 8.1 %all_gather.7 = bf16[3,4,128,128]{3,2,1,0:T(8,128)(2,1)S(1)} all-gather(bf16[3,4,64,128]{3,2,1,0:T(8,128)(2,1)S(1)} %pad_maximum_fusion), channel_id=1, replica_groups=mesh['slab'=16,'filt'=2] {'filt'}, dimensions={2}, use_global_device_ids=true | all-gather | bytes 589824 | tf_op jit(solution)/shard_map/all_gather | solution.py:61
  62.8 0.2 fusion.132
  63.2 0.2 convolution_add_fusion.25
  63.4 0.2 convolution_add_fusion.24
  63.8 0.2 convolution_add_fusion.22
  64.1 0.2 convolution_add_fusion.21
  64.5 0.2 convolution_add_fusion.19
  64.7 0.2 convolution_add_fusion.18
  65.1 0.2 convolution_add_fusion.16
  65.3 0.2 convolution_add_fusion.15
  65.7 0.2 convolution_add_fusion.13
  66.0 0.2 fusion.35
  66.4 0.2 fusion.32
  66.6 0.2 fusion.31
  67.0 0.2 fusion.29
  67.2 0.2 fusion.28
  67.6 0.2 fusion.26
  67.9 0.2 fusion.25
  68.3 0.9 %fusion.55 = bf16[1,4,64,128]{3,2,1,0:T(8,128)(2,1)} fusion(f32[1,4,64,128]{3,2,1,0:T(8,128)S(1)} %fusion.24, bf16[3,4,128,128]{3,2,1,0:T(8,128)(2,1)S(1)} %all_gather.7, f32[64]{0:T(128)S(1)} %convert_element_type.28, bf16[27,64,128]{2,1,0:T(8,128)(2,1)S(1)} %copy-done.4), kind=kOutput, calls=%fused_computation.159 | convolution fusion | flops 8519680 | bytes 606720 | tf_op jit(solution)/shard_map/oc,dhcw->dhow/dot_general | solution.py:30
  (62 shorter events, 6.5 us)
Async XLA Ops:
  0.6 14.2 %copy-start.2 = (bf16[27,64,64]{2,1,0:T(8,128)(2,1)S(1)}, bf16[27,64,64]{2,1,0:T(8,128)(2,1)}, u32[]{:S(2)}) copy-start(bf16[27,64,64]{2,1,0:T(8,128)(2,1)} %param.8) | copy-start | bytes 663556
  0.6 7.5 %collective-permute-start = (bf16[1,4,64,256]{3,2,1,0:T(8,128)(2,1)}, bf16[1,4,64,256]{3,2,1,0:T(8,128)(2,1)S(1)}, u32[]{:S(2)}, u32[]{:S(2)}) collective-permute-start(bf16[1,4,64,256]{3,2,1,0:T(8,128)(2,1)} %param.7), channel_id=1, source_target_pairs={{0,2},{2,4},{4,6},{6,8},{8,10},{10,12},{12,14},{14,16},{16,18},{18... | collective-permute-start | bytes 393224 | tf_op jit(solution)/shard_map/ppermute | solution.py:12
  2.7 7.4 %collective-permute-start.1 = (bf16[1,4,64,256]{3,2,1,0:T(8,128)(2,1)}, bf16[1,4,64,256]{3,2,1,0:T(8,128)(2,1)S(1)}, u32[]{:S(2)}, u32[]{:S(2)}) collective-permute-start(bf16[1,4,64,256]{3,2,1,0:T(8,128)(2,1)} %param.7), channel_id=1, source_target_pairs={{2,0},{4,2},{6,4},{8,6},{10,8},{12,10},{14,12},{16,14},{18,16},{20... | collective-permute-start | bytes 393224 | tf_op jit(solution)/shard_map/ppermute | solution.py:15
  10.1 6.4 %collective-permute-start.2 = (bf16[3,1,64,256]{3,2,1,0:T(8,128)(2,1)S(1)}, bf16[3,1,64,256]{3,2,1,0:T(8,128)(2,1)S(1)}, u32[]{:S(2)}, u32[]{:S(2)}) collective-permute-start(bf16[3,1,64,256]{3,2,1,0:T(8,128)(2,1)S(1)} %get-tuple-element.2), channel_id=1, source_target_pairs={{0,1},{2,3},{4,5},{6,7},{8,9},{10,11},{12,13},{14,15},{16,17},{18,... | collective-permute-start | bytes 294920 | tf_op jit(solution)/shard_map/ppermute | solution.py:12
  13.5 7.0 %collective-permute-start.3 = (bf16[3,1,64,256]{3,2,1,0:T(8,128)(2,1)S(1)}, bf16[3,1,64,256]{3,2,1,0:T(8,128)(2,1)S(1)}, u32[]{:S(2)}, u32[]{:S(2)}) collective-permute-start(bf16[3,1,64,256]{3,2,1,0:T(8,128)(2,1)S(1)} %get-tuple-element.3), channel_id=1, source_target_pairs={{1,0},{3,2},{5,4},{7,6},{9,8},{11,10},{13,12},{15,14},{17,16},{19,... | collective-permute-start | bytes 294920 | tf_op jit(solution)/shard_map/ppermute | solution.py:15
  24.7 0.9 %copy-start = (bf16[1,4,64,256]{3,2,1,0:T(8,128)(2,1)S(1)}, bf16[1,4,64,256]{3,2,1,0:T(8,128)(2,1)}, u32[]{:S(2)}) copy-start(bf16[1,4,64,256]{3,2,1,0:T(8,128)(2,1)} %param.7) | copy-start | bytes 393220
  26.8 14.2 %copy-start.1 = (bf16[1,4,64,256]{3,2,1,0:T(8,128)(2,1)}, bf16[1,4,64,256]{3,2,1,0:T(8,128)(2,1)S(1)}, u32[]{:S(2)}) copy-start(bf16[1,4,64,256]{3,2,1,0:T(8,128)(2,1)S(1)} %fusion.22) | copy-start | bytes 393220
  26.8 12.0 %copy-start.5 = (bf16[64]{0:T(256)(128)(2,1)S(1)}, bf16[64]{0:T(256)(128)(2,1)}, u32[]{:S(2)}) copy-start(bf16[64]{0:T(256)(128)(2,1)} %param.11) | copy-start | bytes 388
  26.8 14.1 %copy-start.3 = (bf16[27,64,64]{2,1,0:T(8,128)(2,1)S(1)}, bf16[27,64,64]{2,1,0:T(8,128)(2,1)}, u32[]{:S(2)}) copy-start(bf16[27,64,64]{2,1,0:T(8,128)(2,1)} %param.10) | copy-start | bytes 663556
  32.3 6.5 %collective-permute-start.4 = (bf16[1,4,64,128]{3,2,1,0:T(8,128)(2,1)S(1)}, bf16[1,4,64,128]{3,2,1,0:T(8,128)(2,1)S(1)}, u32[]{:S(2)}, u32[]{:S(2)}) collective-permute-start(bf16[1,4,64,128]{3,2,1,0:T(8,128)(2,1)S(1)} %bitcast.832), channel_id=1, source_target_pairs={{0,2},{2,4},{4,6},{6,8},{8,10},{10,12},{12,14},{14,16},{16,18},{18... | collective-permute-start | bytes 196616 | tf_op jit(solution)/shard_map/ppermute | solution.py:12
  34.2 6.4 %collective-permute-start.5 = (bf16[1,4,64,128]{3,2,1,0:T(8,128)(2,1)S(1)}, bf16[1,4,64,128]{3,2,1,0:T(8,128)(2,1)S(1)}, u32[]{:S(2)}, u32[]{:S(2)}) collective-permute-start(bf16[1,4,64,128]{3,2,1,0:T(8,128)(2,1)S(1)} %bitcast.833), channel_id=1, source_target_pairs={{2,0},{4,2},{6,4},{8,6},{10,8},{12,10},{14,12},{16,14},{18,16},{20... | collective-permute-start | bytes 196616 | tf_op jit(solution)/shard_map/ppermute | solution.py:15
  45.8 7.0 %copy-start.6 = (bf16[64]{0:T(256)(128)(2,1)S(1)}, bf16[64]{0:T(256)(128)(2,1)}, u32[]{:S(2)}) copy-start(bf16[64]{0:T(256)(128)(2,1)} %param.13) | copy-start | bytes 388
  46.0 16.8 %copy-start.4 = (bf16[27,64,128]{2,1,0:T(8,128)(2,1)S(1)}, bf16[27,64,128]{2,1,0:T(8,128)(2,1)}, u32[]{:S(2)}) copy-start(bf16[27,64,128]{2,1,0:T(8,128)(2,1)} %param.12) | copy-start | bytes 1327108
  46.2 6.6 %collective-permute-start.6 = (bf16[1,4,64,128]{3,2,1,0:T(8,128)(2,1)S(1)}, bf16[1,4,64,128]{3,2,1,0:T(8,128)(2,1)S(1)}, u32[]{:S(2)}, u32[]{:S(2)}) collective-permute-start(bf16[1,4,64,128]{3,2,1,0:T(8,128)(2,1)S(1)} %fusion.54), channel_id=1, source_target_pairs={{0,2},{2,4},{4,6},{6,8},{8,10},{10,12},{12,14},{14,16},{16,18},{18... | collective-permute-start | bytes 196616 | tf_op jit(solution)/shard_map/ppermute | solution.py:12
  48.2 6.5 %collective-permute-start.7 = (bf16[1,4,64,128]{3,2,1,0:T(8,128)(2,1)S(1)}, bf16[1,4,64,128]{3,2,1,0:T(8,128)(2,1)S(1)}, u32[]{:S(2)}, u32[]{:S(2)}) collective-permute-start(bf16[1,4,64,128]{3,2,1,0:T(8,128)(2,1)S(1)} %fusion.54), channel_id=1, source_target_pairs={{2,0},{4,2},{6,4},{8,6},{10,8},{12,10},{14,12},{16,14},{18,16},{20... | collective-permute-start | bytes 196616 | tf_op jit(solution)/shard_map/ppermute | solution.py:15
where the time goes:
time: 69.5 us; the launch traced here: 69.1 us
  starting transfers between devices  24.3 us (35%)
  matrix products  16.7 us (24%)
  blocking collectives  12.7 us (18%)
  waiting for transfers between devices  10.5 us (15%)
  other arithmetic  1.95 us (3%)
  local copies, waits for them, and re-layouts  1.8 us (3%)
  between operations  1.19 us (2%)
    dot_general x81, matrix products, accumulate(): jnp.einsum('oc,dhcw->dhow', kernel[tap], padded[kd:kd + planes, kh:kh + r...  16.7 us
    ppermute x4, starting transfers between devices, extended(): lax.ppermute(lax.slice_in_dim(block, 0, width, axis=dim), axis, backward)  15 us
    ppermute x4, starting transfers between devices, extended(): lax.ppermute(lax.slice_in_dim(block, block.shape[dim] - width, None, axis...  9.31 us
    ppermute x4, waiting for transfers between devices, extended(): lax.ppermute(lax.slice_in_dim(block, 0, width, axis=dim), axis, backward)  8.79 us
    all_gather x1, blocking collectives, per_device(): lax.all_gather(hidden_planes, 'filt', axis=2, tiled=True)  8.14 us
    all_gather x1, blocking collectives, per_device(): full_rows = lax.all_gather(pooled, 'filt', axis=1, tiled=True)  4.58 us
    ppermute x4, waiting for transfers between devices, extended(): lax.ppermute(lax.slice_in_dim(block, block.shape[dim] - width, None, axis...  1.71 us
    unnamed x16, local copies, waits for them, and re-layouts  1.51 us
  transfers between devices with their start and end apart: 8, of which 6 were waited for; matrix products, arithmetic and copies ran while one was open for 3% of the time, Pallas kernels for 0%

commit v1 on v0

--- a/solution.py
+++ b/solution.py
@@ -1,7 +1,21 @@
+import functools
+
 import jax
 import jax.numpy as jnp
 from jax import lax
+from jax.experimental import pallas as pl
+from jax.experimental.pallas import tpu as pltpu
 from jax.sharding import PartitionSpec as P
+
+BF = jnp.bfloat16
+F32 = jnp.float32
+NT = (((1,), (1,)), ((), ()))
+NN = (((1,), (0,)), ((), ()))
+
+LAYER = 4
+RUN = 24
+FRAME = 32
+LEAD = 4
 
 
 def extended(block, sides, width):
@@ -42,7 +56,7 @@
     )
 
 
-def per_device(volume, kernel_one, bias_one, kernel_two, bias_two, kernel_three, bias_three):
+def by_planes(volume, kernel_one, bias_one, kernel_two, bias_two, kernel_three, bias_three):
     planes, rows, chans, cols = volume.shape
     rimmed = extended(volume, (("slab", 0), ("filt", 1)), 1)
     start_one = jnp.zeros((planes, rows, kernel_one.shape[1], cols), jnp.float32)
@@ -65,6 +79,301 @@
     return (skip_one, features_two)
 
 
+def dot(a, b, dims):
+    return lax.dot_general(a, b, dims, preferred_element_type=F32)
+
+
+def pack_kernel(volume, k2, k3, b23, blocks, sent):
+    count, width = blocks.shape[0] // (2 * RUN), volume.shape[1]
+    row = lax.broadcasted_iota(jnp.int32, (blocks.shape[0], width), 0)
+    col = lax.broadcasted_iota(jnp.int32, (blocks.shape[0], width), 1)
+    peer, rest = row // (2 * RUN), row % (2 * RUN)
+    wanted = (width // count) * peer + 2 * (rest % RUN - LEAD) + rest // RUN
+    chosen = jnp.where(wanted == col, 1.0, 0.0).astype(BF)
+    blocks[...] = dot(chosen, volume[...], NT).astype(BF)
+    for t in range(27):
+        sent[32 * t : 32 * t + 32, :] = jnp.concatenate([k2[t, :32, :], k2[t, 32:, :]], axis=1)
+        sent[864 + 64 * t : 928 + 64 * t, :] = k3[t]
+    sent[2592:2608, :] = b23[...]
+
+
+def banded(k_ref):
+    def pieces(dp, dw):
+        k0, k1, k2 = (k_ref(9 * dp + 3 * dr + dw) for dr in range(3))
+        none = jnp.zeros_like(k0)
+        join = lambda a, b: jnp.concatenate([a, b], axis=1)
+        return join(k1, k2), join(k0, k1), join(k2, none), join(none, k0)
+
+    return pieces
+
+
+def prep_kernel(half, k1, k2, got, w1a, w1c, w2a, w2c):
+    mine = pl.multiple_of(half[0] * 64, 64)
+    other = pl.multiple_of(64 - half[0] * 64, 64)
+    one = banded(lambda t: k1[t])
+    own = banded(lambda t: k2[t])
+
+    def received(t):
+        both = got[32 * t : 32 * t + 32, :]
+        return jnp.concatenate([both[:, :64], both[:, 64:]], axis=0)
+
+    far = banded(received)
+    zero = jnp.zeros((64, 128), BF)
+    for dp in range(3):
+        for dw in range(3):
+            t = 3 * dp + dw
+            a, b, c, d = one(dp, dw)
+            for i, (low, high) in enumerate(((a, zero), (b, c), (d, a), (zero, b))):
+                w1a[64 * i : 64 * i + 64, 256 * t : 256 * t + 128] = low
+                w1a[64 * i : 64 * i + 64, 256 * t + 128 : 256 * t + 256] = high
+            lanes = slice(128 * t, 128 * t + 128)
+            w1c[0:64, lanes] = d
+            w1c[64:128, lanes] = c
+            for at, pieces in ((mine, own), (other, far)):
+                a, b, c, d = pieces(dp, dw)
+                w2a[pl.ds(at, 64), lanes] = a
+                w2a[pl.ds(128 + at, 64), lanes] = b
+                w2c[pl.ds(at, 64), lanes] = c
+                w2c[pl.ds(128 + at, 64), lanes] = d
+
+
+def shifted(x, by):
+    return pltpu.roll(x, (-by) % x.shape[0], 0)
+
+
+def main_kernel(
+    place, low, mid, high, w1a, w1c, w2a, w2c, k3, got, b1, b2, b3, out, q, x34, pd, hd
+):
+    half, layer, group, layers = place[0], place[1], place[2], place[3]
+    planes = 3 + LAYER + 3
+    pad = jnp.zeros((FRAME - RUN, 256), F32)
+    lane = lax.broadcasted_iota(jnp.int32, (1, 128), 1)
+    left = lane < 64
+
+    for f in range(2):
+        for par in range(2):
+            runs = []
+            for v in range(planes):
+                src, at = ((low, v), (mid, v - 3), (high, v - 3 - LAYER))[
+                    (v >= 3) + (v >= 3 + LAYER)
+                ]
+                runs.append(src[2 * at + f, RUN * par : RUN * par + RUN, :].astype(F32))
+                runs.append(pad)
+            whole = jnp.concatenate(runs, axis=0)
+            q[f, 1 + par] = whole.astype(BF)
+            if par == 0:
+                q[f, 3] = shifted(whole, 1).astype(BF)
+            else:
+                q[f, 0] = shifted(whole, -1).astype(BF)
+    for a in range(4):
+        x34[a] = jnp.where(left, q[1, a, :, 0:128], q[0, a, :, 128:256])
+
+    u = LAYER + 4
+    m = u * FRAME
+    taps = [(dp, dw) for dp in range(3) for dw in range(3)]
+
+    def pick(ref, f, par):
+        parts = [ref[f, par + dw, FRAME * dp : FRAME * dp + m, :] for dp, dw in taps]
+        return jnp.concatenate(parts, axis=1)
+
+    cross = []
+    for par in range(2):
+        parts = [x34[par + dw, FRAME * dp : FRAME * dp + m, :] for dp, dw in taps]
+        cross.append(dot(jnp.concatenate(parts, axis=1), w1c[...], NT))
+    bias = b1[...].astype(F32)
+    row = lax.broadcasted_iota(jnp.int32, (m, 1), 0)
+    pooled_col = 16 * group - LEAD + row % FRAME
+    plane = LAYER * layer - 2 + row // FRAME
+    inside = (plane >= 0) & (plane < LAYER * layers) & (pooled_col >= 0) & (pooled_col < 128)
+    tiles = []
+    for f in range(2):
+        ys = []
+        for par in range(2):
+            y = dot(pick(q, f, par), w1a[...], NT)
+            if f == 0:
+                extra = jnp.where(left, 0.0, cross[par])
+                y = jnp.concatenate([y[:, :128], y[:, 128:] + extra], axis=1)
+            else:
+                extra = jnp.where(left, cross[par], 0.0)
+                y = jnp.concatenate([y[:, :128] + extra, y[:, 128:]], axis=1)
+            y = jnp.maximum(y + bias, 0.0).astype(BF).astype(F32)
+            for s in range(LAYER):
+                top = FRAME * (2 + s) + LEAD
+                out[2 * s + f, 16 * par : 16 * par + 16, :] = y[top : top + 16, :].astype(BF)
+            ys.append(y)
+        y = jnp.where(inside, jnp.maximum(ys[0], ys[1]), 0.0)
+        y0, y1 = y[:, :128], y[:, 128:]
+        y0 = jnp.maximum(y0, pltpu.roll(y0, 64, 1))
+        y1 = jnp.maximum(y1, pltpu.roll(y1, 64, 1))
+        tiles.append(jnp.where(left, y0, y1))
+    pooled = jnp.concatenate(tiles, axis=1)
+
+    for dw in range(3):
+        pd[dw] = shifted(pooled, dw - 1).astype(BF)
+    m = (LAYER + 2) * FRAME
+
+    def lanes_of(ref, n, lo, hi):
+        return [ref[dw, FRAME * dp : FRAME * dp + n, lo:hi] for dp, dw in taps]
+
+    pairs = [dot(jnp.concatenate(lanes_of(pd, m, 128 * a, 128 * a + 128), axis=1), w2a[...], NT) for a in range(2)]
+    parts = [jnp.where(left, b, a) for a, b in zip(lanes_of(pd, m, 0, 128), lanes_of(pd, m, 128, 256))]
+    mixed = dot(jnp.concatenate(parts, axis=1), w2c[...], NT)
+    row = lax.broadcasted_iota(jnp.int32, (m, 1), 0)
+    pooled_col = 16 * group - LEAD + row % FRAME
+    plane = LAYER * layer - 1 + row // FRAME
+    inside = (plane >= 0) & (plane < LAYER * layers) & (pooled_col >= 0) & (pooled_col < 128)
+    hidden = jnp.concatenate(
+        [
+            pairs[0][:, :128],
+            pairs[0][:, 128:] + mixed[:, :128],
+            pairs[1][:, :128] + mixed[:, 128:],
+            pairs[1][:, 128:],
+        ],
+        axis=1,
+    )
+    bias = jnp.concatenate([b2[...].astype(F32)] * 4, axis=1)
+    hidden = jnp.where(inside, jnp.maximum(hidden + bias, 0.0), 0.0).astype(BF).astype(F32)
+    for dw in range(3):
+        hd[dw] = shifted(hidden, dw - 1).astype(BF)
+
+    m = LAYER * FRAME
+
+    def third(t):
+        return jnp.concatenate([k3[t], got[864 + 64 * t : 928 + 64 * t, :]], axis=0)
+
+    none = jnp.zeros((128, 128), BF)
+    straight, across = [[], []], [[], []]
+    for dp, dw in taps:
+        k0, k1, k2 = (third(9 * dp + 3 * dr + dw) for dr in range(3))
+        straight[0] += [k1, k2]
+        straight[1] += [k0, k1]
+        across[0] += [none, k2]
+        across[1] += [k0, none]
+    w3a = jnp.concatenate([jnp.concatenate(rows, axis=1) for rows in straight], axis=0)
+    w3c = jnp.concatenate([jnp.concatenate(rows, axis=1) for rows in across], axis=0)
+    both = jnp.concatenate(
+        [jnp.concatenate(lanes_of(hd, m, 256 * a, 256 * a + 256), axis=1) for a in range(2)], axis=0
+    )
+    both = dot(both, w3a, NT)
+    mixed = dot(jnp.concatenate(lanes_of(hd, m, 128, 384), axis=1), w3c, NT)
+    t0, t1 = both[:m, :128], both[:m, 128:] + mixed[:, :128]
+    t2, t3 = both[m:, :128] + mixed[:, 128:], both[m:, 128:]
+    bias = b3[...].astype(F32)
+    t0, t1, t2, t3 = (jnp.maximum(t + bias, 0.0) for t in (t0, t1, t2, t3))
+    r0, r1, r2, r3 = (pltpu.roll(t, 64, 1) for t in (t0, t1, t2, t3))
+    first = jnp.concatenate([jnp.where(left, t0, r1), jnp.where(left, t2, r3)], axis=1)
+    second = jnp.concatenate([jnp.where(left, r0, t1), jnp.where(left, r2, t3)], axis=1)
+    for s in range(LAYER):
+        top = FRAME * s + LEAD
+        out[2 * s + half, 32:48, :] = first[top : top + 16, :].astype(BF)
+        out[2 * s + 1 - half, 32:48, :] = second[top : top + 16, :].astype(BF)
+
+
+def unpack_kernel(got, skip, features):
+    count = got.shape[0]
+    ones = got[:, 0:32, :].reshape(count * 32, 256)
+    twos = got[:, 32:48, :].reshape(count * 16, 256)
+    row = lax.broadcasted_iota(jnp.int32, (256, 256), 0)
+    col = lax.broadcasted_iota(jnp.int32, (256, 256), 1)
+    source = 32 * (row // 32) + 16 * (row % 2) + row % 32 // 2
+    order = jnp.where(source == col, 1.0, 0.0).astype(BF)
+    same = jnp.where(row == col, 1.0, 0.0).astype(BF)
+    by_column = dot(order, ones, NN).astype(BF)
+    skip[...] = dot(same, by_column, NT).astype(BF)
+    features[...] = dot(same, twos, NT).astype(BF)
+
+
+def vmem(count):
+    return [pl.BlockSpec(memory_space=pltpu.VMEM)] * count
+
+
+def smem(count):
+    return [pl.BlockSpec(memory_space=pltpu.SMEM)] * count
+
+
+def shape(*dims):
+    return jax.ShapeDtypeStruct(dims, BF)
+
+
+def by_columns(volume, kernel_one, bias_one, kernel_two, bias_two, kernel_three, bias_three):
+    slabs, halves = lax.axis_size("slab"), lax.axis_size("filt")
+    peers = LAYER * halves
+    slab, half = lax.axis_index("slab"), lax.axis_index("filt")
+    groups = [[peers * g + i for i in range(peers)] for g in range(slabs // LAYER)]
+    exchange = functools.partial(
+        lax.all_to_all,
+        axis_name=("slab", "filt"),
+        split_axis=0,
+        concat_axis=0,
+        axis_index_groups=groups,
+        tiled=True,
+    )
+    biases = jnp.pad(jnp.concatenate([bias_two, bias_three])[None, :], ((0, 15), (0, 0)))
+    blocks, sent = pl.pallas_call(
+        pack_kernel,
+        out_shape=(shape(peers * 2 * RUN, 256), shape(2608, 128)),
+        in_specs=vmem(4),
+        out_specs=tuple(vmem(2)),
+        name="pack",
+    )(volume.reshape(256, 256), kernel_two, kernel_three, biases)
+    got = lax.ppermute(sent, "filt", [(0, 1), (1, 0)])
+    mid = exchange(blocks.reshape(peers, 2 * RUN, 256))
+    up = [(i, i + LAYER) for i in range(slabs - LAYER)]
+    down = [(b, a) for a, b in up]
+    low = lax.ppermute(mid[2:8], "slab", up)
+    high = lax.ppermute(mid[0:6], "slab", down)
+    place = jnp.stack([half, slab // LAYER, slab % LAYER * 2 + half, slabs // LAYER]).astype(jnp.int32)
+    w1a, w1c, w2a, w2c = pl.pallas_call(
+        prep_kernel,
+        out_shape=(shape(256, 2304), shape(128, 1152), shape(256, 1152), shape(256, 1152)),
+        in_specs=smem(1) + vmem(3),
+        out_specs=tuple(vmem(4)),
+        name="prep",
+    )(place, kernel_one, kernel_two, got)
+    their = got[2592]
+    b1 = jnp.tile(bias_one, 4)[None, :]
+    first = half == 0
+    b2 = jnp.where(
+        first, jnp.concatenate([bias_two, their[:64]]), jnp.concatenate([their[:64], bias_two])
+    )[None, :]
+    b3 = jnp.concatenate([bias_three, their[64:]])[None, :]
+    frames = FRAME * (LAYER + 6)
+    out = pl.pallas_call(
+        main_kernel,
+        out_shape=shape(peers, 48, 256),
+        in_specs=smem(1) + vmem(12),
+        out_specs=vmem(1)[0],
+        scratch_shapes=[
+            pltpu.VMEM((2, 4, frames, 256), BF),
+            pltpu.VMEM((4, frames, 128), BF),
+            pltpu.VMEM((3, FRAME * (LAYER + 4), 256), BF),
+            pltpu.VMEM((3, FRAME * (LAYER + 2), 512), BF),
+        ],
+        name="sections",
+    )(place, low, mid, high, w1a, w1c, w2a, w2c, kernel_three, got, b1, b2, b3)
+    home = exchange(out)
+    skip, features = pl.pallas_call(
+        unpack_kernel,
+        out_shape=(shape(256, 256), shape(256, 128)),
+        in_specs=vmem(1),
+        out_specs=tuple(vmem(2)),
+        name="unpack",
+    )(home)
+    return skip.reshape(volume.shape), features.reshape(1, 4, 64, 128)
+
+
+def per_device(volume, kernel_one, *rest):
+    fits = (
+        volume.shape == (1, 4, 64, 256)
+        and lax.axis_size("filt") == 2
+        and lax.axis_size("slab") % LAYER == 0
+        and kernel_one.shape == (27, 64, 64)
+        and rest[1].shape == (27, 64, 64)
+        and rest[3].shape == (27, 64, 128)
+    )
+    return (by_columns if fits else by_planes)(volume, kernel_one, *rest)
+
+
 def solution(mesh):
     return jax.shard_map(
         per_device,

time: 69.5 us -> 55.1 us (0.79)
  the two profiles are of different devices: /device:TPU:16 before, /device:TPU:0 now
where the time goes in v1:
time: 55.1 us; the launch traced here: 54.6 us
  Pallas kernels  14.8 us (27%)
  waiting for transfers between devices  12.3 us (22%)
  starting transfers between devices  12.2 us (22%)
  blocking collectives  9.61 us (17%)
  other arithmetic  2.62 us (5%)
  local copies, waits for them, and re-layouts  2.21 us (4%)
  between operations  0.77 us (1%)
    all_to_all x1, waiting for transfers between devices, by_columns(): mid = exchange(blocks.reshape(peers, 2 * RUN, 256))  12.3 us
    all_to_all x1, blocking collectives, by_columns(): home = exchange(out)  9.61 us
    pallas_call x1, Pallas kernels, by_columns(): pl.pallas_call(main_kernel, out_shape=shape(peers, 48, 256), in_specs=sme...  6.64 us
    ppermute x1, starting transfers between devices, by_columns(): low = lax.ppermute(mid[2:8], 'slab', up)  4.55 us
    pallas_call x1, Pallas kernels, by_columns(): pl.pallas_call(prep_kernel, out_shape=(shape(256, 2304), shape(128, 1152)...  3.72 us
    all_to_all x1, starting transfers between devices, by_columns(): mid = exchange(blocks.reshape(peers, 2 * RUN, 256))  3.39 us
    ppermute x1, starting transfers between devices, by_columns(): got = lax.ppermute(sent, 'filt', [(0, 1), (1, 0)])  3 us
    pallas_call x1, Pallas kernels, by_columns(): pl.pallas_call(pack_kernel, out_shape=(shape(peers * 2 * RUN, 256), shape...  2.49 us
  transfers between devices with their start and end apart: 4, of which 1 were waited for; matrix products, arithmetic and copies ran while one was open for 5% of the time, Pallas kernels for 7%

profile of v1, /device:TPU:0, one launch (start us, length us, event | category | flops | bytes accessed | tf_op | source)
XLA Modules:
  0.0 54.6 jit_solution(16319591345853974798)
XLA Ops:
  0.6 0.0 copy-start.6
  0.6 0.0 copy-start.5
  0.6 0.8 %maximum_bitcast_fusion = bf16[1,128]{1,0:T(2,128)(2,1)S(1)} fusion(bf16[64]{0:T(256)(128)(2,1)} %param.13, bf16[64]{0:T(256)(128)(2,1)} %param.11), kind=kLoop, calls=%fused_computation.3 | loop fusion | flops 512 | bytes 512 | tf_op jit(solution)/shard_map/broadcast_in_dim | solution.py:311
  1.4 0.6 %pad.4.b23 = bf16[16,128]{1,0:T(8,128)(2,1)} pad(bf16[1,128]{1,0:T(2,128)(2,1)S(1)} %maximum_bitcast_fusion, bf16[]{:T(256)} %constant.39.clone.1), padding=0_15x0_0 | pad | bytes 4354 | tf_op jit(solution)/shard_map/jit(_pad)/pad | solution.py:311
  2.0 2.5 %pack.1 = (bf16[384,256]{1,0:T(8,128)(2,1)}, bf16[2608,128]{1,0:T(8,128)(2,1)}) custom-call(bf16[256,256]{1,0:T(8,128)(2,1)} %bitcast.15, bf16[27,64,64]{2,1,0:T(8,128)(2,1)} %k2.3, bf16[27,64,128]{2,1,0:T(8,128)(2,1)} %k3.3, bf16[16,128]{1,0:T(8,128)(2,1)} %pad.4.b23), custom_call_target="tpu_custom_call" | custom-call | tf_op jit(solution)/shard_map/pack/pallas_call | solution.py:312
  4.5 3.0 %collective-permute-start.2 = (bf16[2608,128]{1,0:T(8,128)(2,1)}, bf16[2608,128]{1,0:T(8,128)(2,1)S(1)}, u32[]{:S(2)}, u32[]{:S(2)}) collective-permute-start(bf16[2608,128]{1,0:T(8,128)(2,1)} %get-tuple-element.11), channel_id=1, source_target_pairs={{0,1},{1,0},{2,3},{3,2},{4,5},{5,4},{6,7},{7,6},{8,9},{9,8},{10,11... | collective-permute-start | bytes 2002952 | tf_op jit(solution)/shard_map/ppermute | solution.py:319
  7.5 3.4 %all-to-all-start = ((bf16[8,48,256]{2,1,0:T(8,128)(2,1)}), bf16[8,48,256]{2,1,0:T(8,128)(2,1)S(1)}, u32[]{:S(2)}, u32[]{:S(2)}) async-start(bf16[8,48,256]{2,1,0:T(8,128)(2,1)} %bitcast.14), calls=%async_computation | async-start | bytes 393216 | tf_op jit(solution)/shard_map/all_to_all | solution.py:320
  10.9 0.0 copy-start.4
  11.0 0.0 copy-done.5
  11.0 0.6 %broadcast_in_dim_tile.3.b1 = bf16[1,256]{1,0:T(2,128)(2,1)} reshape(bf16[4,64]{1,0:T(4,128)(2,1)S(1)} %tile.2) | data formatting | bytes 1024 | tf_op jit(solution)/shard_map/broadcast_in_dim;tile | solution.py:334
  11.6 0.6 %pad_add_fusion.half.place = s32[4]{0:T(128)} fusion(s32[1]{0:T(128)} %constant.38.clone.1, s32[1]{0:T(128)} %bitcast.2, s32[1]{0:T(128)} %bitcast.1, s32[1]{0:T(128)} %bitcast), kind=kLoop, calls=%fused_computation.2 | loop fusion | flops 12 | bytes 32 | tf_op jit(solution)/shard_map/stack | solution.py:325
  12.2 12.3 %all-to-all-done.mid = bf16[8,48,256]{2,1,0:T(8,128)(2,1)S(1)} async-done(((bf16[8,48,256]{2,1,0:T(8,128)(2,1)}), bf16[8,48,256]{2,1,0:T(8,128)(2,1)S(1)}, u32[]{:S(2)}, u32[]{:S(2)}) %all-to-all-start) | async-done | bytes 196640 | tf_op jit(solution)/shard_map/all_to_all | solution.py:320
  24.6 0.0 copy-start.1
  24.6 1.3 %collective-permute-start.1 = (bf16[6,48,256]{2,1,0:T(8,128)(2,1)S(1)}, bf16[6,48,256]{2,1,0:T(8,128)(2,1)S(1)}, u32[]{:S(2)}, u32[]{:S(2)}) collective-permute-start(bf16[6,48,256]{2,1,0:T(8,128)(2,1)S(1)} %get-tuple-element.20), channel_id=1, source_target_pairs={{8,0},{10,2},{12,4},{14,6},{16,8},{18,10},{20,12},{22,14},{24,16},... | collective-permute-start | bytes 442376 | tf_op jit(solution)/shard_map/ppermute | solution.py:324
  25.9 4.6 %collective-permute-start = (bf16[6,48,256]{2,1,0:T(8,128)(2,1)S(1)}, bf16[6,48,256]{2,1,0:T(8,128)(2,1)S(1)}, u32[]{:S(2)}, u32[]{:S(2)}) collective-permute-start(bf16[6,48,256]{2,1,0:T(8,128)(2,1)S(1)} %get-tuple-element.21), channel_id=1, source_target_pairs={{0,8},{2,10},{4,12},{6,14},{8,16},{10,18},{12,20},{14,22},{16,24},... | collective-permute-start | bytes 442376 | tf_op jit(solution)/shard_map/ppermute | solution.py:323
  30.5 0.0 collective-permute-done.2.got
  30.5 0.0 copy-start
  30.5 0.1 slice_bitcast_fusion
  30.6 0.0 copy-done.6
  30.6 0.6 %maximum_bitcast_fusion.1.b3 = bf16[1,128]{1,0:T(2,128)(2,1)} fusion(bf16[64]{0:T(256)(128)(2,1)S(1)} %get-tuple-element.18, bf16[64]{0:T(256)(128)(2,1)S(1)} %copy-done.6), kind=kLoop, calls=%fused_computation.4 | loop fusion | flops 512 | bytes 512 | tf_op jit(solution)/shard_map/broadcast_in_dim | solution.py:339
  31.2 0.1 copy-done
  31.3 3.7 %prep.1 = (bf16[256,2304]{1,0:T(8,128)(2,1)}, bf16[128,1152]{1,0:T(8,128)(2,1)}, bf16[256,1152]{1,0:T(8,128)(2,1)}, bf16[256,1152]{1,0:T(8,128)(2,1)}) custom-call(s32[4]{0:T(128)} %pad_add_fusion.half.place, bf16[27,64,64]{2,1,0:T(8,128)(2,1)} %k1.1, bf16[27,64,64]{2,1,0:T(8,128)(2,1)} %k2.3, bf16[2608,128]{1,0:T(8,128)(2,1)} %copy-done), custom_call_target="tpu_custom_call" | custom-call | tf_op jit(solution)/shard_map/prep/pallas_call | solution.py:326
  35.0 0.0 copy-done.4
  35.0 0.6 %broadcast_select_fusion.b2 = bf16[1,128]{1,0:T(2,128)(2,1)} fusion(pred[]{:T(512)S(6)} %eq.5, bf16[1,64]{1,0:T(2,128)(2,1)S(1)} %get-tuple-element.19, bf16[1,64]{1,0:T(2,128)(2,1)S(1)} %bitcast.16), kind=kLoop, calls=%fused_computation | loop fusion | flops 1152 | bytes 513 | tf_op jit(solution)/shard_map/jit(_where)/select_n | solution.py:336
  35.6 0.0 collective-permute-done.1.high
  35.6 0.0 copy-start.2
  35.6 0.0 collective-permute-done.low
  35.6 0.0 copy-start.3
  35.7 0.0 copy-done.1
  35.7 0.6 %copy-done.2 = bf16[6,48,256]{2,1,0:T(8,128)(2,1)} copy-done((bf16[6,48,256]{2,1,0:T(8,128)(2,1)}, bf16[6,48,256]{2,1,0:T(8,128)(2,1)S(1)}, u32[]{:S(2)}) %copy-start.2) | copy-done | bytes 147480
  36.3 0.1 copy-done.3
  36.4 6.6 %sections.1 = bf16[8,48,256]{2,1,0:T(8,128)(2,1)} custom-call(s32[4]{0:T(128)} %pad_add_fusion.half.place, bf16[6,48,256]{2,1,0:T(8,128)(2,1)} %copy-done.3, bf16[8,48,256]{2,1,0:T(8,128)(2,1)} %copy-done.1, bf16[6,48,256]{2,1,0:T(8,128)(2,1)} %copy-done.2, bf16[256,2304]{1,0:T(8,128)(2,1)} %get-tuple-element.12.w1a, ...), custom_call_target="tpu_custom_call" | custom-call | tf_op jit(solution)/shard_map/sections/pallas_call | solution.py:341
  43.0 9.6 %all_to_all.10.got = bf16[8,48,256]{2,1,0:T(8,128)(2,1)} all-to-all(bf16[8,48,256]{2,1,0:T(8,128)(2,1)} %sections.1), channel_id=1, replica_groups={{0,1,2,3,4,5,6,7},{8,9,10,11,12,13,14,15},{16,17,18,19,20,21,22,23},{24..., dimensions={0} | all-to-all | bytes 393216 | tf_op jit(solution)/shard_map/all_to_all | solution.py:354
  52.6 2.0 %unpack.1 = (bf16[256,256]{1,0:T(8,128)(2,1)}, bf16[256,128]{1,0:T(8,128)(2,1)}) custom-call(bf16[8,48,256]{2,1,0:T(8,128)(2,1)} %all_to_all.10.got), custom_call_target="tpu_custom_call" | custom-call | tf_op jit(solution)/shard_map/unpack/pallas_call | solution.py:355
  (2 shorter events, 0.0 us)
Async XLA Ops:
  0.6 29.9 %copy-start.6 = (bf16[64]{0:T(256)(128)(2,1)S(1)}, bf16[64]{0:T(256)(128)(2,1)}, u32[]{:S(2)}) copy-start(bf16[64]{0:T(256)(128)(2,1)} %param.13) | copy-start | bytes 388
  0.6 10.3 %copy-start.5 = (bf16[64]{0:T(256)(128)(2,1)S(1)}, bf16[64]{0:T(256)(128)(2,1)}, u32[]{:S(2)}) copy-start(bf16[64]{0:T(256)(128)(2,1)} %param.9) | copy-start | bytes 388
  4.5 25.9 %collective-permute-start.2 = (bf16[2608,128]{1,0:T(8,128)(2,1)}, bf16[2608,128]{1,0:T(8,128)(2,1)S(1)}, u32[]{:S(2)}, u32[]{:S(2)}) collective-permute-start(bf16[2608,128]{1,0:T(8,128)(2,1)} %get-tuple-element.11), channel_id=1, source_target_pairs={{0,1},{1,0},{2,3},{3,2},{4,5},{5,4},{6,7},{7,6},{8,9},{9,8},{10,11... | collective-permute-start | bytes 2002952 | tf_op jit(solution)/shard_map/ppermute | solution.py:319
  7.5 17.0 %all-to-all-start = ((bf16[8,48,256]{2,1,0:T(8,128)(2,1)}), bf16[8,48,256]{2,1,0:T(8,128)(2,1)S(1)}, u32[]{:S(2)}, u32[]{:S(2)}) async-start(bf16[8,48,256]{2,1,0:T(8,128)(2,1)} %bitcast.14), calls=%async_computation | async-start | bytes 393216 | tf_op jit(solution)/shard_map/all_to_all | solution.py:320
  10.9 24.1 %copy-start.4 = (bf16[64]{0:T(256)(128)(2,1)S(1)}, bf16[64]{0:T(256)(128)(2,1)}, u32[]{:S(2)}) copy-start(bf16[64]{0:T(256)(128)(2,1)} %param.11) | copy-start | bytes 388
  24.6 11.1 %copy-start.1 = (bf16[8,48,256]{2,1,0:T(8,128)(2,1)}, bf16[8,48,256]{2,1,0:T(8,128)(2,1)S(1)}, u32[]{:S(2)}) copy-start(bf16[8,48,256]{2,1,0:T(8,128)(2,1)S(1)} %all-to-all-done.mid) | copy-start | bytes 589828
  24.6 11.0 %collective-permute-start.1 = (bf16[6,48,256]{2,1,0:T(8,128)(2,1)S(1)}, bf16[6,48,256]{2,1,0:T(8,128)(2,1)S(1)}, u32[]{:S(2)}, u32[]{:S(2)}) collective-permute-start(bf16[6,48,256]{2,1,0:T(8,128)(2,1)S(1)} %get-tuple-element.20), channel_id=1, source_target_pairs={{8,0},{10,2},{12,4},{14,6},{16,8},{18,10},{20,12},{22,14},{24,16},... | collective-permute-start | bytes 442376 | tf_op jit(solution)/shard_map/ppermute | solution.py:324
  25.9 9.8 %collective-permute-start = (bf16[6,48,256]{2,1,0:T(8,128)(2,1)S(1)}, bf16[6,48,256]{2,1,0:T(8,128)(2,1)S(1)}, u32[]{:S(2)}, u32[]{:S(2)}) collective-permute-start(bf16[6,48,256]{2,1,0:T(8,128)(2,1)S(1)} %get-tuple-element.21), channel_id=1, source_target_pairs={{0,8},{2,10},{4,12},{6,14},{8,16},{10,18},{12,20},{14,22},{16,24},... | collective-permute-start | bytes 442376 | tf_op jit(solution)/shard_map/ppermute | solution.py:323
  30.5 0.9 %copy-start = (bf16[2608,128]{1,0:T(8,128)(2,1)}, bf16[2608,128]{1,0:T(8,128)(2,1)S(1)}, u32[]{:S(2)}) copy-start(bf16[2608,128]{1,0:T(8,128)(2,1)S(1)} %collective-permute-done.2.got) | copy-start | bytes 2002948
  35.6 0.7 %copy-start.2 = (bf16[6,48,256]{2,1,0:T(8,128)(2,1)}, bf16[6,48,256]{2,1,0:T(8,128)(2,1)S(1)}, u32[]{:S(2)}) copy-start(bf16[6,48,256]{2,1,0:T(8,128)(2,1)S(1)} %collective-permute-done.1.high) | copy-start | bytes 442372
  35.6 0.7 %copy-start.3 = (bf16[6,48,256]{2,1,0:T(8,128)(2,1)}, bf16[6,48,256]{2,1,0:T(8,128)(2,1)S(1)}, u32[]{:S(2)}) copy-start(bf16[6,48,256]{2,1,0:T(8,128)(2,1)S(1)} %collective-permute-done.low) | copy-start | bytes 442372

commit v2 on v1

--- a/solution.py
+++ b/solution.py
@@ -6,6 +6,7 @@
 from jax.experimental import pallas as pl
 from jax.experimental.pallas import tpu as pltpu
 from jax.sharding import PartitionSpec as P
+
 
 BF = jnp.bfloat16
 F32 = jnp.float32
@@ -36,7 +37,7 @@
 
 
 def accumulate(total, padded, kernel):
-    planes, rows, chans, cols = total.shape
+    planes, rows, _, cols = total.shape
     for kd in range(3):
         for kh in range(3):
             for kw in range(3):
@@ -83,18 +84,31 @@
     return lax.dot_general(a, b, dims, preferred_element_type=F32)
 
 
-def pack_kernel(volume, k2, k3, b23, blocks, sent):
-    count, width = blocks.shape[0] // (2 * RUN), volume.shape[1]
-    row = lax.broadcasted_iota(jnp.int32, (blocks.shape[0], width), 0)
-    col = lax.broadcasted_iota(jnp.int32, (blocks.shape[0], width), 1)
+def pack_kernel(volume, blocks):
+    count, width = blocks.shape[0], volume.shape[1]
+    shape = (count * 2 * RUN, width)
+    row = lax.broadcasted_iota(jnp.int32, shape, 0)
+    col = lax.broadcasted_iota(jnp.int32, shape, 1)
     peer, rest = row // (2 * RUN), row % (2 * RUN)
     wanted = (width // count) * peer + 2 * (rest % RUN - LEAD) + rest // RUN
     chosen = jnp.where(wanted == col, 1.0, 0.0).astype(BF)
-    blocks[...] = dot(chosen, volume[...], NT).astype(BF)
+    blocks[...] = dot(chosen, volume[...], NT).astype(BF).reshape(blocks.shape)
+
+
+def aligned(at, by):
+    return pl.multiple_of(at, by)
+
+
+def send_kernel(after, k2, k3, b2, b3, sent):
+    core = lax.axis_index("slab") % 2
+    top = 32 * core
     for t in range(27):
-        sent[32 * t : 32 * t + 32, :] = jnp.concatenate([k2[t, :32, :], k2[t, 32:, :]], axis=1)
-        sent[864 + 64 * t : 928 + 64 * t, :] = k3[t]
-    sent[2592:2608, :] = b23[...]
+        low = k2[t, pl.ds(aligned(top, 16), 16), :]
+        high = k2[t, pl.ds(aligned(top + 16, 16), 16), :]
+        sent[16 * t : 16 * t + 16, :] = jnp.concatenate([low, high], axis=1)
+        sent[432 + 32 * t : 464 + 32 * t, :] = k3[t, pl.ds(aligned(top, 32), 32), :]
+    both = jnp.concatenate([b2[...], b3[...]], axis=1)
+    sent[1296:1312, :] = jnp.broadcast_to(both, (16, 128))
 
 
 def banded(k_ref):
@@ -107,17 +121,8 @@
     return pieces
 
 
-def prep_kernel(half, k1, k2, got, w1a, w1c, w2a, w2c):
-    mine = pl.multiple_of(half[0] * 64, 64)
-    other = pl.multiple_of(64 - half[0] * 64, 64)
+def first_kernel(after, k1, b1, w1a, w1c, bias):
     one = banded(lambda t: k1[t])
-    own = banded(lambda t: k2[t])
-
-    def received(t):
-        both = got[32 * t : 32 * t + 32, :]
-        return jnp.concatenate([both[:, :64], both[:, 64:]], axis=0)
-
-    far = banded(received)
     zero = jnp.zeros((64, 128), BF)
     for dp in range(3):
         for dw in range(3):
@@ -129,12 +134,49 @@
             lanes = slice(128 * t, 128 * t + 128)
             w1c[0:64, lanes] = d
             w1c[64:128, lanes] = c
-            for at, pieces in ((mine, own), (other, far)):
-                a, b, c, d = pieces(dp, dw)
-                w2a[pl.ds(at, 64), lanes] = a
-                w2a[pl.ds(128 + at, 64), lanes] = b
-                w2c[pl.ds(at, 64), lanes] = c
-                w2c[pl.ds(128 + at, 64), lanes] = d
+    bias[...] = jnp.broadcast_to(jnp.concatenate([b1[...].astype(F32)] * 4, axis=1), bias.shape)
+
+
+def second_kernel(k2, k3, b2, b3, over, beside, w2a, w2c, w3, bias2, bias3):
+    half, core = lax.axis_index("filt"), lax.axis_index("slab") % 2
+    mine, other = half * 64, 64 - half * 64
+
+    def own(t):
+        return k2[t]
+
+    def piece(ref):
+        def rows(t):
+            both = ref[16 * t : 16 * t + 16, :]
+            return jnp.concatenate([both[:, :64], both[:, 64:]], axis=0)
+
+        return rows
+
+    sources = (
+        (own, mine, 64),
+        (piece(over), other + 32 * core, 32),
+        (piece(beside), other + 32 - 32 * core, 32),
+    )
+    for dp in range(3):
+        for dw in range(3):
+            t = 3 * dp + dw
+            lanes = slice(128 * t, 128 * t + 128)
+            for rows, at, size in sources:
+                a, b, c, d = banded(rows)(dp, dw)
+                w2a[pl.ds(aligned(at, 32), size), lanes] = a
+                w2a[pl.ds(aligned(128 + at, 32), size), lanes] = b
+                w2c[pl.ds(aligned(at, 32), size), lanes] = c
+                w2c[pl.ds(aligned(128 + at, 32), size), lanes] = d
+    for t in range(27):
+        w3[t, 0:64, :] = k3[t]
+        w3[t, pl.ds(aligned(64 + 32 * core, 32), 32), :] = over[432 + 32 * t : 464 + 32 * t, :]
+        w3[t, pl.ds(aligned(96 - 32 * core, 32), 32), :] = beside[432 + 32 * t : 464 + 32 * t, :]
+    theirs = over[1296:1297, :].astype(F32)
+    b2, b3 = b2[...].astype(F32), b3[...].astype(F32)
+    there2, there3 = theirs[:, :64], theirs[:, 64:]
+    low = jnp.where(half == 0, b2, there2)
+    high = jnp.where(half == 0, there2, b2)
+    bias2[...] = jnp.broadcast_to(jnp.concatenate([low, high], axis=1), bias2.shape)
+    bias3[...] = jnp.broadcast_to(jnp.concatenate([b3, there3], axis=1), bias3.shape)
 
 
 def shifted(x, by):
@@ -142,9 +184,11 @@
 
 
 def main_kernel(
-    place, low, mid, high, w1a, w1c, w2a, w2c, k3, got, b1, b2, b3, out, q, x34, pd, hd
+    low, mid, high, w1a, w1c, w2a, w2c, w3, b1, b2, b3, out, q, x34, pd, hd
 ):
-    half, layer, group, layers = place[0], place[1], place[2], place[3]
+    half, slab = lax.axis_index("filt"), lax.axis_index("slab")
+    layer, layers = slab // LAYER, lax.axis_size("slab") // LAYER
+    group = slab % LAYER * lax.axis_size("filt") + half
     planes = 3 + LAYER + 3
     pad = jnp.zeros((FRAME - RUN, 256), F32)
     lane = lax.broadcasted_iota(jnp.int32, (1, 128), 1)
@@ -180,7 +224,7 @@
     for par in range(2):
         parts = [x34[par + dw, FRAME * dp : FRAME * dp + m, :] for dp, dw in taps]
         cross.append(dot(jnp.concatenate(parts, axis=1), w1c[...], NT))
-    bias = b1[...].astype(F32)
+    bias = b1[0:1, :]
     row = lax.broadcasted_iota(jnp.int32, (m, 1), 0)
     pooled_col = 16 * group - LEAD + row % FRAME
     plane = LAYER * layer - 2 + row // FRAME
@@ -231,20 +275,17 @@
         ],
         axis=1,
     )
-    bias = jnp.concatenate([b2[...].astype(F32)] * 4, axis=1)
+    bias = jnp.concatenate([b2[0:1, :]] * 4, axis=1)
     hidden = jnp.where(inside, jnp.maximum(hidden + bias, 0.0), 0.0).astype(BF).astype(F32)
     for dw in range(3):
         hd[dw] = shifted(hidden, dw - 1).astype(BF)
 
     m = LAYER * FRAME
 
-    def third(t):
-        return jnp.concatenate([k3[t], got[864 + 64 * t : 928 + 64 * t, :]], axis=0)
-
     none = jnp.zeros((128, 128), BF)
     straight, across = [[], []], [[], []]
     for dp, dw in taps:
-        k0, k1, k2 = (third(9 * dp + 3 * dr + dw) for dr in range(3))
+        k0, k1, k2 = (w3[9 * dp + 3 * dr + dw] for dr in range(3))
         straight[0] += [k1, k2]
         straight[1] += [k0, k1]
         across[0] += [none, k2]
@@ -258,7 +299,7 @@
     mixed = dot(jnp.concatenate(lanes_of(hd, m, 128, 384), axis=1), w3c, NT)
     t0, t1 = both[:m, :128], both[:m, 128:] + mixed[:, :128]
     t2, t3 = both[m:, :128] + mixed[:, 128:], both[m:, 128:]
-    bias = b3[...].astype(F32)
+    bias = b3[0:1, :]
     t0, t1, t2, t3 = (jnp.maximum(t + bias, 0.0) for t in (t0, t1, t2, t3))
     r0, r1, r2, r3 = (pltpu.roll(t, 64, 1) for t in (t0, t1, t2, t3))
     first = jnp.concatenate([jnp.where(left, t0, r1), jnp.where(left, t2, r3)], axis=1)
@@ -283,22 +324,29 @@
     features[...] = dot(same, twos, NT).astype(BF)
 
 
-def vmem(count):
-    return [pl.BlockSpec(memory_space=pltpu.VMEM)] * count
-
-
-def smem(count):
-    return [pl.BlockSpec(memory_space=pltpu.SMEM)] * count
-
-
 def shape(*dims):
     return jax.ShapeDtypeStruct(dims, BF)
+
+
+def call(kernel, outs, *operands, scratch=(), limit=8):
+    spec = pl.BlockSpec(memory_space=pltpu.VMEM)
+    return pl.pallas_call(
+        kernel,
+        out_shape=outs,
+        in_specs=[spec] * len(operands),
+        out_specs=jax.tree.map(lambda _: spec, outs),
+        scratch_shapes=scratch,
+        compiler_params=pltpu.CompilerParams(vmem_limit_bytes=limit << 20),
+    )(*operands)
+
+
+def near(x):
+    return pltpu.with_memory_space_constraint(x, pltpu.VMEM)
 
 
 def by_columns(volume, kernel_one, bias_one, kernel_two, bias_two, kernel_three, bias_three):
     slabs, halves = lax.axis_size("slab"), lax.axis_size("filt")
     peers = LAYER * halves
-    slab, half = lax.axis_index("slab"), lax.axis_index("filt")
     groups = [[peers * g + i for i in range(peers)] for g in range(slabs // LAYER)]
     exchange = functools.partial(
         lax.all_to_all,
@@ -308,70 +356,74 @@
         axis_index_groups=groups,
         tiled=True,
     )
-    biases = jnp.pad(jnp.concatenate([bias_two, bias_three])[None, :], ((0, 15), (0, 0)))
-    blocks, sent = pl.pallas_call(
-        pack_kernel,
-        out_shape=(shape(peers * 2 * RUN, 256), shape(2608, 128)),
-        in_specs=vmem(4),
-        out_specs=tuple(vmem(2)),
-        name="pack",
-    )(volume.reshape(256, 256), kernel_two, kernel_three, biases)
-    got = lax.ppermute(sent, "filt", [(0, 1), (1, 0)])
-    mid = exchange(blocks.reshape(peers, 2 * RUN, 256))
+    b1, b2, b3 = bias_one[None, :], bias_two[None, :], bias_three[None, :]
+    blocks = call(pack_kernel, pltpu.VMEM((peers, 2 * RUN, 256), BF), volume.reshape(256, 256))
+    mid = exchange(blocks)
+    blocks = near(blocks)
+    sent = call(send_kernel, pltpu.VMEM((1312, 128), BF), blocks, kernel_two, kernel_three, b2, b3)
+    over = lax.ppermute(sent, "filt", [(0, 1), (1, 0)])
+    w1a, w1c, bias1 = call(
+        first_kernel,
+        (pltpu.VMEM((256, 2304), BF), pltpu.VMEM((128, 1152), BF), pltpu.VMEM((8, 256), F32)),
+        blocks,
+        kernel_one,
+        b1,
+    )
     up = [(i, i + LAYER) for i in range(slabs - LAYER)]
     down = [(b, a) for a, b in up]
     low = lax.ppermute(mid[2:8], "slab", up)
     high = lax.ppermute(mid[0:6], "slab", down)
-    place = jnp.stack([half, slab // LAYER, slab % LAYER * 2 + half, slabs // LAYER]).astype(jnp.int32)
-    w1a, w1c, w2a, w2c = pl.pallas_call(
-        prep_kernel,
-        out_shape=(shape(256, 2304), shape(128, 1152), shape(256, 1152), shape(256, 1152)),
-        in_specs=smem(1) + vmem(3),
-        out_specs=tuple(vmem(4)),
-        name="prep",
-    )(place, kernel_one, kernel_two, got)
-    their = got[2592]
-    b1 = jnp.tile(bias_one, 4)[None, :]
-    first = half == 0
-    b2 = jnp.where(
-        first, jnp.concatenate([bias_two, their[:64]]), jnp.concatenate([their[:64], bias_two])
-    )[None, :]
-    b3 = jnp.concatenate([bias_three, their[64:]])[None, :]
+    beside = lax.ppermute(over, "slab", [(i, i ^ 1) for i in range(slabs)])
+    w2a, w2c, w3, bias2, bias3 = call(
+        second_kernel,
+        (
+            pltpu.VMEM((256, 1152), BF),
+            pltpu.VMEM((256, 1152), BF),
+            pltpu.VMEM((27, 128, 128), BF),
+            pltpu.VMEM((8, 128), F32),
+            pltpu.VMEM((8, 128), F32),
+        ),
+        kernel_two,
+        kernel_three,
+        b2,
+        b3,
+        near(over),
+        near(beside),
+    )
     frames = FRAME * (LAYER + 6)
-    out = pl.pallas_call(
+    operands = (low, mid, high, w1a, w1c, w2a, w2c, w3, bias1, bias2, bias3)
+    out = call(
         main_kernel,
-        out_shape=shape(peers, 48, 256),
-        in_specs=smem(1) + vmem(12),
-        out_specs=vmem(1)[0],
-        scratch_shapes=[
+        pltpu.VMEM((peers, 48, 256), BF),
+        *map(near, operands),
+        scratch=[
             pltpu.VMEM((2, 4, frames, 256), BF),
             pltpu.VMEM((4, frames, 128), BF),
             pltpu.VMEM((3, FRAME * (LAYER + 4), 256), BF),
             pltpu.VMEM((3, FRAME * (LAYER + 2), 512), BF),
         ],
-        name="sections",
-    )(place, low, mid, high, w1a, w1c, w2a, w2c, kernel_three, got, b1, b2, b3)
+        limit=24,
+    )
     home = exchange(out)
-    skip, features = pl.pallas_call(
-        unpack_kernel,
-        out_shape=(shape(256, 256), shape(256, 128)),
-        in_specs=vmem(1),
-        out_specs=tuple(vmem(2)),
-        name="unpack",
-    )(home)
+    skip, features = call(unpack_kernel, (shape(256, 256), shape(256, 128)), near(home))
     return skip.reshape(volume.shape), features.reshape(1, 4, 64, 128)
 
 
-def per_device(volume, kernel_one, *rest):
-    fits = (
-        volume.shape == (1, 4, 64, 256)
-        and lax.axis_size("filt") == 2
-        and lax.axis_size("slab") % LAYER == 0
-        and kernel_one.shape == (27, 64, 64)
-        and rest[1].shape == (27, 64, 64)
-        and rest[3].shape == (27, 64, 128)
-    )
-    return (by_columns if fits else by_planes)(volume, kernel_one, *rest)
+def fits(volume, kernels, slabs, halves):
+    return (
+        volume == (1, 4, 64, 256)
+        and kernels == [(27, 64, 64), (27, 64, 64), (27, 64, 128)]
+        and halves == 2
+        and slabs % LAYER == 0
+    )
+
+
+def per_device(volume, *rest):
+    kernels = [r.shape for r in rest[::2]]
+    good = fits(volume.shape, kernels, lax.axis_size("slab"), lax.axis_size("filt"))
+    if not good:
+        return by_planes(volume, *rest)
+    return by_columns(volume, *rest)
 
 
 def solution(mesh):

time: 55.1 us -> 45.4 us (0.82)
  Pallas kernels: 14.8 us -> 9.01 us
  other arithmetic: 2.62 us -> 0 us
  local copies, waits for them, and re-layouts: 2.21 us -> 4.28 us
  waiting for transfers between devices: 12.3 us -> 10.6 us
  blocking collectives: 9.61 us -> 8.82 us
  starting transfers between devices: 12.2 us -> 11.5 us
    all_to_all x1, waiting for transfers between devices: 12.3 us -> 0.26 us  [by_columns(): mid = exchange(blocks)]
    ppermute x1 -> x2, waiting for transfers between devices: 0.01 us -> 6.07 us  [the longest x1 6.07 us: by_columns(): over = lax.ppermute(sent, 'filt', [(0, 1), (1, 0)])]
    pallas_call x4 -> x6, Pallas kernels: 14.8 us -> 9.01 us  [call(): pl.pallas_call(kernel, out_shape=outs, in_specs=[spec] * len(operands), o...]
    ppermute x1, waiting for transfers between devices: 0.01 us -> 4.12 us  [by_columns(): high = lax.ppermute(mid[0:6], 'slab', down)]
    unnamed x14 -> x22, local copies, waits for them, and re-layouts: 0.87 us -> 4.26 us
    broadcast_in_dim x2 -> x0, other arithmetic: 1.42 us -> none  [the longest x1 0.79 us: by_columns(): jnp.concatenate([bias_two, bias_three])[None, :]]
    ppermute x1, starting transfers between devices: 4.55 us -> 3.71 us  [by_columns(): low = lax.ppermute(mid[2:8], 'slab', up)]
    all_to_all x1, blocking collectives: 9.61 us -> 8.82 us  [by_columns(): home = exchange(out)]
  transfers between devices with their start and end apart: 4 -> 5, of which waited for: 1 -> 4; matrix products, arithmetic and copies ran while one was open for 5% -> 0% of each run, Pallas kernels for 7% -> 4%
where the time goes in v2:
time: 45.4 us; the launch traced here: 44.9 us
  starting transfers between devices  11.5 us (25%)
  waiting for transfers between devices  10.6 us (23%)
  Pallas kernels  9.01 us (20%)
  blocking collectives  8.82 us (19%)
  local copies, waits for them, and re-layouts  4.28 us (9%)
  between operations  0.78 us (2%)
    pallas_call x6, Pallas kernels, call(): pl.pallas_call(kernel, out_shape=outs, in_specs=[spec] * len(operands), o...  9.01 us
    all_to_all x1, blocking collectives, by_columns(): home = exchange(out)  8.82 us
    ppermute x1, waiting for transfers between devices, by_columns(): over = lax.ppermute(sent, 'filt', [(0, 1), (1, 0)])  6.07 us
    unnamed x22, local copies, waits for them, and re-layouts  4.26 us
    ppermute x1, waiting for transfers between devices, by_columns(): high = lax.ppermute(mid[0:6], 'slab', down)  4.12 us
    ppermute x1, starting transfers between devices, by_columns(): low = lax.ppermute(mid[2:8], 'slab', up)  3.71 us
    all_to_all x1, starting transfers between devices, by_columns(): mid = exchange(blocks)  3.39 us
    ppermute x1, starting transfers between devices, by_columns(): over = lax.ppermute(sent, 'filt', [(0, 1), (1, 0)])  3.06 us
  transfers between devices with their start and end apart: 5, of which 4 were waited for; matrix products, arithmetic and copies ran while one was open for 0% of the time, Pallas kernels for 4%

profile of v2, /device:TPU:0, one launch (start us, length us, event | category | flops | bytes accessed | tf_op | source)
XLA Modules:
  0.0 44.9 jit_solution(16508689134978876221)
XLA Ops:
  0.6 0.0 copy-start.5
  0.6 0.9 %copy-done.5 = bf16[1,4,64,256]{3,2,1,0:T(8,128)(2,1)S(1)} copy-done((bf16[1,4,64,256]{3,2,1,0:T(8,128)(2,1)S(1)}, bf16[1,4,64,256]{3,2,1,0:T(8,128)(2,1)}, u32[]{:S(2)}) %copy-start.5) | copy-done | bytes 131096
  1.5 1.1 %shard_map.86.after = bf16[8,48,256]{2,1,0:T(8,128)(2,1)} custom-call(bf16[256,256]{1,0:T(8,128)(2,1)S(1)} %bitcast.6), custom_call_target="tpu_custom_call" | custom-call | tf_op jit(solution)/shard_map/pallas_call | solution.py:333
  2.6 0.0 copy-start
  2.6 1.0 %copy-done = bf16[27,64,64]{2,1,0:T(8,128)(2,1)S(1)} copy-done((bf16[27,64,64]{2,1,0:T(8,128)(2,1)S(1)}, bf16[27,64,64]{2,1,0:T(8,128)(2,1)}, u32[]{:S(2)}) %copy-start) | copy-done | bytes 221208
  3.6 0.0 copy-start.2
  3.6 1.0 %copy-done.2 = bf16[27,64,128]{2,1,0:T(8,128)(2,1)S(1)} copy-done((bf16[27,64,128]{2,1,0:T(8,128)(2,1)S(1)}, bf16[27,64,128]{2,1,0:T(8,128)(2,1)}, u32[]{:S(2)}) %copy-start.2) | copy-done | bytes 442392
  4.6 0.0 copy-start.6
  4.7 0.7 %copy-done.6 = bf16[64]{0:T(256)(128)(2,1)S(1)} copy-done((bf16[64]{0:T(256)(128)(2,1)S(1)}, bf16[64]{0:T(256)(128)(2,1)}, u32[]{:S(2)}) %copy-start.6) | copy-done | bytes 152
  5.3 0.0 copy-start.8
  5.3 0.7 %copy-done.8 = bf16[64]{0:T(256)(128)(2,1)S(1)} copy-done((bf16[64]{0:T(256)(128)(2,1)S(1)}, bf16[64]{0:T(256)(128)(2,1)}, u32[]{:S(2)}) %copy-start.8) | copy-done | bytes 152
  6.0 0.0 copy-start.4
  6.0 0.0 copy-start.10
  6.0 0.0 copy-start.1
  6.0 0.0 copy-start.3
  6.0 0.0 copy-start.7
  6.0 0.0 copy-start.9
  6.0 1.1 %shard_map.88 = bf16[1312,128]{1,0:T(8,128)(2,1)S(1)} custom-call(bf16[8,48,256]{2,1,0:T(8,128)(2,1)} %shard_map.86.after, bf16[27,64,64]{2,1,0:T(8,128)(2,1)S(1)} %copy-done, bf16[27,64,128]{2,1,0:T(8,128)(2,1)S(1)} %copy-done.2, bf16[1,64]{1,0:T(2,128)(2,1)S(1)} %bitcast.7, bf16[1,64]{1,0:T(2,128)(2,1)S(1)} %bitcast.9), custom_call_target="tpu_custom_call" | custom-call | tf_op jit(solution)/shard_map/pallas_call | solution.py:333
  7.1 3.1 %collective-permute-start.2 = (bf16[1312,128]{1,0:T(8,128)(2,1)S(1)}, bf16[1312,128]{1,0:T(8,128)(2,1)S(1)}, u32[]{:S(2)}, u32[]{:S(2)}) collective-permute-start(bf16[1312,128]{1,0:T(8,128)(2,1)S(1)} %shard_map.88), channel_id=1, source_target_pairs={{0,1},{1,0},{2,3},{3,2},{4,5},{5,4},{6,7},{7,6},{8,9},{9,8},{10,11... | collective-permute-start | bytes 1007624 | tf_op jit(solution)/shard_map/ppermute | solution.py:364
  10.2 3.4 %all-to-all-start = ((bf16[8,48,256]{2,1,0:T(8,128)(2,1)}), bf16[8,48,256]{2,1,0:T(8,128)(2,1)S(1)}, u32[]{:S(2)}, u32[]{:S(2)}) async-start(bf16[8,48,256]{2,1,0:T(8,128)(2,1)} %shard_map.86.after), calls=%async_computation | async-start | bytes 393216 | tf_op jit(solution)/shard_map/all_to_all | solution.py:361
  13.6 6.1 %collective-permute-done.2.over = bf16[1312,128]{1,0:T(8,128)(2,1)S(1)} collective-permute-done((bf16[1312,128]{1,0:T(8,128)(2,1)S(1)}, bf16[1312,128]{1,0:T(8,128)(2,1)S(1)}, u32[]{:S(2)}, u32[]{:S(2)}) %collective-permute-start.2) | collective-permute-done | bytes 335904 | tf_op jit(solution)/shard_map/ppermute | solution.py:364
  19.7 0.0 collective-permute-start.3
  19.7 0.3 all-to-all-done.mid
  20.0 3.7 %collective-permute-start = (bf16[6,48,256]{2,1,0:T(8,128)(2,1)S(1)}, bf16[6,48,256]{2,1,0:T(8,128)(2,1)S(1)}, u32[]{:S(2)}, u32[]{:S(2)}) collective-permute-start(bf16[6,48,256]{2,1,0:T(8,128)(2,1)S(1)} %get-tuple-element.23), channel_id=1, source_target_pairs={{0,8},{2,10},{4,12},{6,14},{8,16},{10,18},{12,20},{14,22},{16,24},... | collective-permute-start | bytes 442376 | tf_op jit(solution)/shard_map/ppermute | solution.py:374
  23.7 1.3 %collective-permute-start.1 = (bf16[6,48,256]{2,1,0:T(8,128)(2,1)S(1)}, bf16[6,48,256]{2,1,0:T(8,128)(2,1)S(1)}, u32[]{:S(2)}, u32[]{:S(2)}) collective-permute-start(bf16[6,48,256]{2,1,0:T(8,128)(2,1)S(1)} %get-tuple-element.22), channel_id=1, source_target_pairs={{8,0},{10,2},{12,4},{14,6},{16,8},{18,10},{20,12},{22,14},{24,16},... | collective-permute-start | bytes 442376 | tf_op jit(solution)/shard_map/ppermute | solution.py:375
  25.0 0.0 copy-done.4
  25.0 0.0 copy-done.10
  25.0 1.1 %shard_map.87 = (bf16[256,2304]{1,0:T(8,128)(2,1)S(1)}, bf16[128,1152]{1,0:T(8,128)(2,1)S(1)}, f32[8,256]{1,0:T(8,128)S(1)}) custom-call(bf16[8,48,256]{2,1,0:T(8,128)(2,1)} %shard_map.86.after, bf16[27,64,64]{2,1,0:T(8,128)(2,1)S(1)} %copy-done.4, bf16[1,64]{1,0:T(2,128)(2,1)S(1)} %bitcast.11), custom_call_target="tpu_custom_call" | custom-call | tf_op jit(solution)/shard_map/pallas_call | solution.py:333
  26.1 0.0 collective-permute-done.3.beside
  26.1 0.0 copy-done.1
  26.1 0.0 copy-done.3
  26.2 0.0 copy-done.7
  26.2 0.0 copy-done.9
  26.2 0.8 %shard_map.89 = (bf16[256,1152]{1,0:T(8,128)(2,1)S(1)}, bf16[256,1152]{1,0:T(8,128)(2,1)S(1)}, bf16[27,128,128]{2,1,0:T(8,128)(2,1)S(1)}, f32[8,128]{1,0:T(8,128)S(1)}, f32[8,128]{1,0:T(8,128)S(1)}) custom-call(bf16[27,64,64]{2,1,0:T(8,128)(2,1)S(1)} %copy-done.1, bf16[27,64,128]{2,1,0:T(8,128)(2,1)S(1)} %copy-done.3, bf16[1,64]{1,0:T(2,128)(2,1)S(1)} %bitcast.8, ...), custom_call_target="tpu_custom_call" | custom-call | tf_op jit(solution)/shard_map/pallas_call | solution.py:333
  27.0 0.1 collective-permute-done.low
  27.2 4.1 %collective-permute-done.1.high = bf16[6,48,256]{2,1,0:T(8,128)(2,1)S(1)} collective-permute-done((bf16[6,48,256]{2,1,0:T(8,128)(2,1)S(1)}, bf16[6,48,256]{2,1,0:T(8,128)(2,1)S(1)}, u32[]{:S(2)}, u32[]{:S(2)}) %collective-permute-start.1) | collective-permute-done | bytes 147488 | tf_op jit(solution)/shard_map/ppermute | solution.py:375
  31.3 3.7 %shard_map.90 = bf16[8,48,256]{2,1,0:T(8,128)(2,1)S(1)} custom-call(bf16[6,48,256]{2,1,0:T(8,128)(2,1)S(1)} %collective-permute-done.low, bf16[8,48,256]{2,1,0:T(8,128)(2,1)S(1)} %all-to-all-done.mid, bf16[6,48,256]{2,1,0:T(8,128)(2,1)S(1)} %collective-permute-done.1.high, bf16[256,2304]{1,0:T(8,128)(2,1)S(1)} %get-tuple-element.12.w1a, ...), custom_call_target="tpu_custom_call" | custom-call | tf_op jit(solution)/shard_map/pallas_call | solution.py:333
  35.0 8.8 %all_to_all.10.got = bf16[8,48,256]{2,1,0:T(8,128)(2,1)S(1)} all-to-all(bf16[8,48,256]{2,1,0:T(8,128)(2,1)S(1)} %shard_map.90), channel_id=1, replica_groups={{0,1,2,3,4,5,6,7},{8,9,10,11,12,13,14,15},{16,17,18,19,20,21,22,23},{24..., dimensions={0} | all-to-all | bytes 393216 | tf_op jit(solution)/shard_map/all_to_all | solution.py:407
  43.8 1.1 %shard_map.91 = (bf16[256,256]{1,0:T(8,128)(2,1)}, bf16[256,128]{1,0:T(8,128)(2,1)}) custom-call(bf16[8,48,256]{2,1,0:T(8,128)(2,1)S(1)} %all_to_all.10.got), custom_call_target="tpu_custom_call" | custom-call | tf_op jit(solution)/shard_map/pallas_call | solution.py:333
  (1 shorter events, 0.0 us)
Async XLA Ops:
  0.6 0.9 %copy-start.5 = (bf16[1,4,64,256]{3,2,1,0:T(8,128)(2,1)S(1)}, bf16[1,4,64,256]{3,2,1,0:T(8,128)(2,1)}, u32[]{:S(2)}) copy-start(bf16[1,4,64,256]{3,2,1,0:T(8,128)(2,1)} %param.7) | copy-start | bytes 393220
  2.6 1.0 %copy-start = (bf16[27,64,64]{2,1,0:T(8,128)(2,1)S(1)}, bf16[27,64,64]{2,1,0:T(8,128)(2,1)}, u32[]{:S(2)}) copy-start(bf16[27,64,64]{2,1,0:T(8,128)(2,1)} %k2.3) | copy-start | bytes 663556
  3.6 1.0 %copy-start.2 = (bf16[27,64,128]{2,1,0:T(8,128)(2,1)S(1)}, bf16[27,64,128]{2,1,0:T(8,128)(2,1)}, u32[]{:S(2)}) copy-start(bf16[27,64,128]{2,1,0:T(8,128)(2,1)} %k3.3) | copy-start | bytes 1327108
  4.6 0.7 %copy-start.6 = (bf16[64]{0:T(256)(128)(2,1)S(1)}, bf16[64]{0:T(256)(128)(2,1)}, u32[]{:S(2)}) copy-start(bf16[64]{0:T(256)(128)(2,1)} %param.11) | copy-start | bytes 388
  5.3 0.7 %copy-start.8 = (bf16[64]{0:T(256)(128)(2,1)S(1)}, bf16[64]{0:T(256)(128)(2,1)}, u32[]{:S(2)}) copy-start(bf16[64]{0:T(256)(128)(2,1)} %param.13) | copy-start | bytes 388
  6.0 19.0 %copy-start.4 = (bf16[27,64,64]{2,1,0:T(8,128)(2,1)S(1)}, bf16[27,64,64]{2,1,0:T(8,128)(2,1)}, u32[]{:S(2)}) copy-start(bf16[27,64,64]{2,1,0:T(8,128)(2,1)} %k1.1) | copy-start | bytes 663556
  6.0 19.0 %copy-start.10 = (bf16[64]{0:T(256)(128)(2,1)S(1)}, bf16[64]{0:T(256)(128)(2,1)}, u32[]{:S(2)}) copy-start(bf16[64]{0:T(256)(128)(2,1)} %param.9) | copy-start | bytes 388
  6.0 20.2 %copy-start.1 = (bf16[27,64,64]{2,1,0:T(8,128)(2,1)S(1)}, bf16[27,64,64]{2,1,0:T(8,128)(2,1)}, u32[]{:S(2)}) copy-start(bf16[27,64,64]{2,1,0:T(8,128)(2,1)} %k2.3) | copy-start | bytes 663556
  6.0 20.2 %copy-start.3 = (bf16[27,64,128]{2,1,0:T(8,128)(2,1)S(1)}, bf16[27,64,128]{2,1,0:T(8,128)(2,1)}, u32[]{:S(2)}) copy-start(bf16[27,64,128]{2,1,0:T(8,128)(2,1)} %k3.3) | copy-start | bytes 1327108
  6.0 20.2 %copy-start.7 = (bf16[64]{0:T(256)(128)(2,1)S(1)}, bf16[64]{0:T(256)(128)(2,1)}, u32[]{:S(2)}) copy-start(bf16[64]{0:T(256)(128)(2,1)} %param.11) | copy-start | bytes 388
  6.0 20.2 %copy-start.9 = (bf16[64]{0:T(256)(128)(2,1)S(1)}, bf16[64]{0:T(256)(128)(2,1)}, u32[]{:S(2)}) copy-start(bf16[64]{0:T(256)(128)(2,1)} %param.13) | copy-start | bytes 388
  7.1 12.5 %collective-permute-start.2 = (bf16[1312,128]{1,0:T(8,128)(2,1)S(1)}, bf16[1312,128]{1,0:T(8,128)(2,1)S(1)}, u32[]{:S(2)}, u32[]{:S(2)}) collective-permute-start(bf16[1312,128]{1,0:T(8,128)(2,1)S(1)} %shard_map.88), channel_id=1, source_target_pairs={{0,1},{1,0},{2,3},{3,2},{4,5},{5,4},{6,7},{7,6},{8,9},{9,8},{10,11... | collective-permute-start | bytes 1007624 | tf_op jit(solution)/shard_map/ppermute | solution.py:364
  10.2 9.7 %all-to-all-start = ((bf16[8,48,256]{2,1,0:T(8,128)(2,1)}), bf16[8,48,256]{2,1,0:T(8,128)(2,1)S(1)}, u32[]{:S(2)}, u32[]{:S(2)}) async-start(bf16[8,48,256]{2,1,0:T(8,128)(2,1)} %shard_map.86.after), calls=%async_computation | async-start | bytes 393216 | tf_op jit(solution)/shard_map/all_to_all | solution.py:361
  19.7 6.5 %collective-permute-start.3 = (bf16[1312,128]{1,0:T(8,128)(2,1)S(1)}, bf16[1312,128]{1,0:T(8,128)(2,1)S(1)}, u32[]{:S(2)}, u32[]{:S(2)}) collective-permute-start(bf16[1312,128]{1,0:T(8,128)(2,1)S(1)} %collective-permute-done.2.over), channel_id=1, source_target_pairs={{0,2},{2,0},{4,6},{6,4},{8,10},{10,8},{12,14},{14,12},{16,18},{18,... | collective-permute-start | bytes 1007624 | tf_op jit(solution)/shard_map/ppermute | solution.py:376
  20.0 7.2 %collective-permute-start = (bf16[6,48,256]{2,1,0:T(8,128)(2,1)S(1)}, bf16[6,48,256]{2,1,0:T(8,128)(2,1)S(1)}, u32[]{:S(2)}, u32[]{:S(2)}) collective-permute-start(bf16[6,48,256]{2,1,0:T(8,128)(2,1)S(1)} %get-tuple-element.23), channel_id=1, source_target_pairs={{0,8},{2,10},{4,12},{6,14},{8,16},{10,18},{12,20},{14,22},{16,24},... | collective-permute-start | bytes 442376 | tf_op jit(solution)/shard_map/ppermute | solution.py:374
  23.7 7.6 %collective-permute-start.1 = (bf16[6,48,256]{2,1,0:T(8,128)(2,1)S(1)}, bf16[6,48,256]{2,1,0:T(8,128)(2,1)S(1)}, u32[]{:S(2)}, u32[]{:S(2)}) collective-permute-start(bf16[6,48,256]{2,1,0:T(8,128)(2,1)S(1)} %get-tuple-element.22), channel_id=1, source_target_pairs={{8,0},{10,2},{12,4},{14,6},{16,8},{18,10},{20,12},{22,14},{24,16},... | collective-permute-start | bytes 442376 | tf_op jit(solution)/shard_map/ppermute | solution.py:375

commit v3 on v2

--- a/solution.py
+++ b/solution.py
@@ -15,7 +15,7 @@
 
 LAYER = 4
 RUN = 24
-FRAME = 32
+FRAME = RUN
 LEAD = 4
 
 
@@ -84,7 +84,9 @@
     return lax.dot_general(a, b, dims, preferred_element_type=F32)
 
 
-def pack_kernel(volume, blocks):
+def pack_kernel(far, blocks, volume, sem):
+    copy = pltpu.make_async_copy(far, volume, sem)
+    copy.start()
     count, width = blocks.shape[0], volume.shape[1]
     shape = (count * 2 * RUN, width)
     row = lax.broadcasted_iota(jnp.int32, shape, 0)
@@ -92,6 +94,7 @@
     peer, rest = row // (2 * RUN), row % (2 * RUN)
     wanted = (width // count) * peer + 2 * (rest % RUN - LEAD) + rest // RUN
     chosen = jnp.where(wanted == col, 1.0, 0.0).astype(BF)
+    copy.wait()
     blocks[...] = dot(chosen, volume[...], NT).astype(BF).reshape(blocks.shape)
 
 
@@ -99,14 +102,22 @@
     return pl.multiple_of(at, by)
 
 
-def send_kernel(after, k2, k3, b2, b3, sent):
-    core = lax.axis_index("slab") % 2
-    top = 32 * core
+def send_kernel(far2, far3, far_b2, far_b3, sent, k2, k3, b2, b3, sems):
+    top = aligned(32 * (lax.axis_index("slab") % 2), 32)
+    half = pl.ds(top, 32)
+    copies = [
+        pltpu.make_async_copy(far, near, sems.at[i])
+        for i, (far, near) in enumerate(
+            ((far_b2, b2), (far_b3, b3), (far2.at[:, half, :], k2), (far3.at[:, half, :], k3))
+        )
+    ]
+    for copy in copies:
+        copy.start()
+    for copy in copies:
+        copy.wait()
     for t in range(27):
-        low = k2[t, pl.ds(aligned(top, 16), 16), :]
-        high = k2[t, pl.ds(aligned(top + 16, 16), 16), :]
-        sent[16 * t : 16 * t + 16, :] = jnp.concatenate([low, high], axis=1)
-        sent[432 + 32 * t : 464 + 32 * t, :] = k3[t, pl.ds(aligned(top, 32), 32), :]
+        sent[16 * t : 16 * t + 16, :] = jnp.concatenate([k2[t, :16, :], k2[t, 16:, :]], axis=1)
+        sent[432 + 32 * t : 464 + 32 * t, :] = k3[t]
     both = jnp.concatenate([b2[...], b3[...]], axis=1)
     sent[1296:1312, :] = jnp.broadcast_to(both, (16, 128))
 
@@ -121,7 +132,14 @@
     return pieces
 
 
-def first_kernel(after, k1, b1, w1a, w1c, bias):
+def rim_kernel(mid, to_first, to_second):
+    odd = lax.axis_index("slab") // LAYER % 2
+    n = to_first.shape[0]
+    to_first[...] = mid[pl.ds(2 - 2 * odd, n)]
+    to_second[...] = mid[pl.ds(2 * odd, n)]
+
+
+def first_kernel(k1, b1, w1a, w1c, bias):
     one = banded(lambda t: k1[t])
     zero = jnp.zeros((64, 128), BF)
     for dp in range(3):
@@ -184,13 +202,13 @@
 
 
 def main_kernel(
-    low, mid, high, w1a, w1c, w2a, w2c, w3, b1, b2, b3, out, q, x34, pd, hd
+    rim_a, mid, rim_b, w1a, w1c, w2a, w2c, w3, b1, b2, b3, out, q, x34, pd, hd
 ):
     half, slab = lax.axis_index("filt"), lax.axis_index("slab")
     layer, layers = slab // LAYER, lax.axis_size("slab") // LAYER
     group = slab % LAYER * lax.axis_size("filt") + half
     planes = 3 + LAYER + 3
-    pad = jnp.zeros((FRAME - RUN, 256), F32)
+    odd = layer % 2 == 1
     lane = lax.broadcasted_iota(jnp.int32, (1, 128), 1)
     left = lane < 64
 
@@ -198,11 +216,13 @@
         for par in range(2):
             runs = []
             for v in range(planes):
-                src, at = ((low, v), (mid, v - 3), (high, v - 3 - LAYER))[
-                    (v >= 3) + (v >= 3 + LAYER)
-                ]
-                runs.append(src[2 * at + f, RUN * par : RUN * par + RUN, :].astype(F32))
-                runs.append(pad)
+                rows = slice(RUN * par, RUN * par + RUN)
+                if 3 <= v < 3 + LAYER:
+                    run = mid[2 * (v - 3) + f, rows, :]
+                else:
+                    at = 2 * (v if v < 3 else v - 3 - LAYER) + f
+                    run = jnp.where(odd == (v < 3), rim_a[at, rows, :], rim_b[at, rows, :])
+                runs.append(run.astype(F32))
             whole = jnp.concatenate(runs, axis=0)
             q[f, 1 + par] = whole.astype(BF)
             if par == 0:
@@ -220,10 +240,19 @@
         parts = [ref[f, par + dw, FRAME * dp : FRAME * dp + m, :] for dp, dw in taps]
         return jnp.concatenate(parts, axis=1)
 
-    cross = []
-    for par in range(2):
+    def pick34(par):
         parts = [x34[par + dw, FRAME * dp : FRAME * dp + m, :] for dp, dw in taps]
-        cross.append(dot(jnp.concatenate(parts, axis=1), w1c[...], NT))
+        return jnp.concatenate(parts, axis=1)
+
+    def pair(parts, weights):
+        n = parts[0].shape[0]
+        all_rows = dot(jnp.concatenate(parts, axis=0), weights, NT)
+        return [all_rows[n * i : n * i + n] for i in range(len(parts))]
+
+    cross = pair([pick34(0), pick34(1)], w1c[...])
+    sums = []
+    for f in range(2):
+        sums += pair([pick(q, f, par) for par in range(2)], w1a[...])
     bias = b1[0:1, :]
     row = lax.broadcasted_iota(jnp.int32, (m, 1), 0)
     pooled_col = 16 * group - LEAD + row % FRAME
@@ -233,7 +262,7 @@
     for f in range(2):
         ys = []
         for par in range(2):
-            y = dot(pick(q, f, par), w1a[...], NT)
+            y = sums[2 * f + par]
             if f == 0:
                 extra = jnp.where(left, 0.0, cross[par])
                 y = jnp.concatenate([y[:, :128], y[:, 128:] + extra], axis=1)
@@ -259,7 +288,10 @@
     def lanes_of(ref, n, lo, hi):
         return [ref[dw, FRAME * dp : FRAME * dp + n, lo:hi] for dp, dw in taps]
 
-    pairs = [dot(jnp.concatenate(lanes_of(pd, m, 128 * a, 128 * a + 128), axis=1), w2a[...], NT) for a in range(2)]
+    pairs = pair(
+        [jnp.concatenate(lanes_of(pd, m, 128 * a, 128 * a + 128), axis=1) for a in range(2)],
+        w2a[...],
+    )
     parts = [jnp.where(left, b, a) for a, b in zip(lanes_of(pd, m, 0, 128), lanes_of(pd, m, 128, 256))]
     mixed = dot(jnp.concatenate(parts, axis=1), w2c[...], NT)
     row = lax.broadcasted_iota(jnp.int32, (m, 1), 0)
@@ -328,12 +360,14 @@
     return jax.ShapeDtypeStruct(dims, BF)
 
 
-def call(kernel, outs, *operands, scratch=(), limit=8):
+def call(kernel, outs, *operands, scratch=(), limit=8, far=False):
     spec = pl.BlockSpec(memory_space=pltpu.VMEM)
+    if far:
+        operands = [pltpu.with_memory_space_constraint(x, pltpu.HBM) for x in operands]
     return pl.pallas_call(
         kernel,
         out_shape=outs,
-        in_specs=[spec] * len(operands),
+        in_specs=[pl.BlockSpec(memory_space=pltpu.HBM) if far else spec] * len(operands),
         out_specs=jax.tree.map(lambda _: spec, outs),
         scratch_shapes=scratch,
         compiler_params=pltpu.CompilerParams(vmem_limit_bytes=limit << 20),
@@ -357,22 +391,46 @@
         tiled=True,
     )
     b1, b2, b3 = bias_one[None, :], bias_two[None, :], bias_three[None, :]
-    blocks = call(pack_kernel, pltpu.VMEM((peers, 2 * RUN, 256), BF), volume.reshape(256, 256))
+    blocks = call(
+        pack_kernel,
+        pltpu.VMEM((peers, 2 * RUN, 256), BF),
+        volume.reshape(256, 256),
+        scratch=[pltpu.VMEM((256, 256), BF), pltpu.SemaphoreType.DMA],
+        far=True,
+    )
     mid = exchange(blocks)
-    blocks = near(blocks)
-    sent = call(send_kernel, pltpu.VMEM((1312, 128), BF), blocks, kernel_two, kernel_three, b2, b3)
+    sent = call(
+        send_kernel,
+        pltpu.VMEM((1312, 128), BF),
+        kernel_two,
+        kernel_three,
+        b2,
+        b3,
+        scratch=[
+            pltpu.VMEM((27, 32, 64), BF),
+            pltpu.VMEM((27, 32, 128), BF),
+            pltpu.VMEM((1, 64), BF),
+            pltpu.VMEM((1, 64), BF),
+            pltpu.SemaphoreType.DMA((4,)),
+        ],
+        far=True,
+    )
     over = lax.ppermute(sent, "filt", [(0, 1), (1, 0)])
     w1a, w1c, bias1 = call(
         first_kernel,
         (pltpu.VMEM((256, 2304), BF), pltpu.VMEM((128, 1152), BF), pltpu.VMEM((8, 256), F32)),
-        blocks,
         kernel_one,
         b1,
     )
-    up = [(i, i + LAYER) for i in range(slabs - LAYER)]
-    down = [(b, a) for a, b in up]
-    low = lax.ppermute(mid[2:8], "slab", up)
-    high = lax.ppermute(mid[0:6], "slab", down)
+    planes = pltpu.VMEM((2 * (LAYER - 1), 2 * RUN, 256), BF)
+    to_first, to_second = call(rim_kernel, (planes, planes), near(mid))
+
+    def swaps(start):
+        up = [(i, i + LAYER) for i in range(slabs - LAYER) if i // LAYER % 2 == start]
+        return up + [(b, a) for a, b in up]
+
+    rim_a = lax.ppermute(to_first, "slab", swaps(0))
+    rim_b = lax.ppermute(to_second, "slab", swaps(1))
     beside = lax.ppermute(over, "slab", [(i, i ^ 1) for i in range(slabs)])
     w2a, w2c, w3, bias2, bias3 = call(
         second_kernel,
@@ -391,7 +449,7 @@
         near(beside),
     )
     frames = FRAME * (LAYER + 6)
-    operands = (low, mid, high, w1a, w1c, w2a, w2c, w3, bias1, bias2, bias3)
+    operands = (rim_a, mid, rim_b, w1a, w1c, w2a, w2c, w3, bias1, bias2, bias3)
     out = call(
         main_kernel,
         pltpu.VMEM((peers, 48, 256), BF),

time: 45.4 us -> 43.9 us (0.967)
  the two profiles are of different devices: /device:TPU:0 before, /device:TPU:16 now
where the time goes in v3:
time: 43.9 us; the launch traced here: 43 us
  blocking collectives  16.6 us (38%)
  waiting for transfers between devices  12.9 us (29%)
  Pallas kernels  7.6 us (17%)
  starting transfers between devices  5.14 us (12%)
  between operations  0.79 us (2%)
    all_to_all x1, blocking collectives, by_columns(): mid = exchange(blocks)  8.93 us
    ppermute x1, waiting for transfers between devices, by_columns(): over = lax.ppermute(sent, 'filt', [(0, 1), (1, 0)])  8.11 us
    all_to_all x1, blocking collectives, by_columns(): home = exchange(out)  7.7 us
    pallas_call x7, Pallas kernels, call(): pl.pallas_call(kernel, out_shape=outs, in_specs=[pl.BlockSpec(memory_spac...  7.6 us
    ppermute x1, waiting for transfers between devices, by_columns(): rim_b = lax.ppermute(to_second, 'slab', swaps(1))  3.18 us
    ppermute x1, starting transfers between devices, by_columns(): rim_b = lax.ppermute(to_second, 'slab', swaps(1))  1.91 us
    ppermute x1, starting transfers between devices, by_columns(): rim_a = lax.ppermute(to_first, 'slab', swaps(0))  1.64 us
    ppermute x1, starting transfers between devices, by_columns(): over = lax.ppermute(sent, 'filt', [(0, 1), (1, 0)])  1.58 us
  transfers between devices with their start and end apart: 4, of which 3 were waited for; matrix products, arithmetic and copies ran while one was open for 0% of the time, Pallas kernels for 5%

profile of v3, /device:TPU:16, one launch (start us, length us, event | category | flops | bytes accessed | tf_op | source)
XLA Modules:
  0.0 43.0 jit_solution(16651212315602724149)
XLA Ops:
  0.6 0.0 copy-start.5
  0.6 0.0 copy-start.2
  0.7 0.0 copy-start
  0.7 0.0 copy-start.1
  0.7 0.0 copy-start.3
  0.7 0.0 copy-start.4
  0.7 1.3 %shard_map.89 = bf16[1312,128]{1,0:T(8,128)(2,1)S(1)} custom-call(bf16[27,64,64]{2,1,0:T(8,128)(2,1)} %k2.1, bf16[27,64,128]{2,1,0:T(8,128)(2,1)} %k3.1, bf16[1,64]{1,0:T(2,128)(2,1)} %bitcast.6, bf16[1,64]{1,0:T(2,128)(2,1)} %bitcast.8), custom_call_target="tpu_custom_call" | custom-call | tf_op jit(solution)/shard_map/pallas_call | solution.py:367
  2.0 1.6 %collective-permute-start.2 = (bf16[1312,128]{1,0:T(8,128)(2,1)S(1)}, bf16[1312,128]{1,0:T(8,128)(2,1)S(1)}, u32[]{:S(2)}, u32[]{:S(2)}) collective-permute-start(bf16[1312,128]{1,0:T(8,128)(2,1)S(1)} %shard_map.89), channel_id=1, source_target_pairs={{0,1},{1,0},{2,3},{3,2},{4,5},{5,4},{6,7},{7,6},{8,9},{9,8},{10,11... | collective-permute-start | bytes 1007624 | tf_op jit(solution)/shard_map/ppermute | solution.py:418
  3.6 8.1 %collective-permute-done.2.over = bf16[1312,128]{1,0:T(8,128)(2,1)S(1)} collective-permute-done((bf16[1312,128]{1,0:T(8,128)(2,1)S(1)}, bf16[1312,128]{1,0:T(8,128)(2,1)S(1)}, u32[]{:S(2)}, u32[]{:S(2)}) %collective-permute-start.2) | collective-permute-done | bytes 335904 | tf_op jit(solution)/shard_map/ppermute | solution.py:418
  11.7 0.0 collective-permute-start.3
  11.7 1.2 %shard_map.86 = bf16[8,48,256]{2,1,0:T(8,128)(2,1)S(1)} custom-call(bf16[256,256]{1,0:T(8,128)(2,1)} %bitcast.11), custom_call_target="tpu_custom_call" | custom-call | tf_op jit(solution)/shard_map/pallas_call | solution.py:367
  12.9 8.9 %all_to_all.10.mid = bf16[8,48,256]{2,1,0:T(8,128)(2,1)S(1)} all-to-all(bf16[8,48,256]{2,1,0:T(8,128)(2,1)S(1)} %shard_map.86), channel_id=1, replica_groups={{0,1,2,3,4,5,6,7},{8,9,10,11,12,13,14,15},{16,17,18,19,20,21,22,23},{24..., dimensions={0} | all-to-all | bytes 393216 | tf_op jit(solution)/shard_map/all_to_all | solution.py:401
  21.8 1.6 %collective-permute-start = (bf16[6,48,256]{2,1,0:T(8,128)(2,1)S(1)}, bf16[6,48,256]{2,1,0:T(8,128)(2,1)S(1)}, u32[]{:S(2)}, u32[]{:S(2)}) collective-permute-start(bf16[6,48,256]{2,1,0:T(8,128)(2,1)S(1)} %get-tuple-element.14), channel_id=1, source_target_pairs={{0,8},{2,10},{4,12},{6,14},{16,24},{18,26},{20,28},{22,30},{8,0},{... | collective-permute-start | bytes 442376 | tf_op jit(solution)/shard_map/ppermute | solution.py:432
  23.5 1.9 %collective-permute-start.1 = (bf16[6,48,256]{2,1,0:T(8,128)(2,1)S(1)}, bf16[6,48,256]{2,1,0:T(8,128)(2,1)S(1)}, u32[]{:S(2)}, u32[]{:S(2)}) collective-permute-start(bf16[6,48,256]{2,1,0:T(8,128)(2,1)S(1)} %get-tuple-element.15), channel_id=1, source_target_pairs={{8,16},{10,18},{12,20},{14,22},{16,8},{18,10},{20,12},{22,14},{9,1... | collective-permute-start | bytes 442376 | tf_op jit(solution)/shard_map/ppermute | solution.py:433
  25.4 0.0 copy-done.5
  25.4 0.0 copy-done.2
  25.4 0.2 shard_map.88
  25.6 0.0 collective-permute-done.3.beside
  25.7 0.0 copy-done
  25.7 0.0 copy-done.1
  25.7 0.0 copy-done.3
  25.7 0.0 copy-done.4
  25.7 0.8 %shard_map.90 = (bf16[256,1152]{1,0:T(8,128)(2,1)S(1)}, bf16[256,1152]{1,0:T(8,128)(2,1)S(1)}, bf16[27,128,128]{2,1,0:T(8,128)(2,1)S(1)}, f32[8,128]{1,0:T(8,128)S(1)}, f32[8,128]{1,0:T(8,128)S(1)}) custom-call(bf16[27,64,64]{2,1,0:T(8,128)(2,1)S(1)} %copy-done, bf16[27,64,128]{2,1,0:T(8,128)(2,1)S(1)} %copy-done.1, bf16[1,64]{1,0:T(2,128)(2,1)S(1)} %bitcast.7, ...), custom_call_target="tpu_custom_call" | custom-call | tf_op jit(solution)/shard_map/pallas_call | solution.py:367
  26.5 1.6 %collective-permute-done.rim_a = bf16[6,48,256]{2,1,0:T(8,128)(2,1)S(1)} collective-permute-done((bf16[6,48,256]{2,1,0:T(8,128)(2,1)S(1)}, bf16[6,48,256]{2,1,0:T(8,128)(2,1)S(1)}, u32[]{:S(2)}, u32[]{:S(2)}) %collective-permute-start) | collective-permute-done | bytes 147488 | tf_op jit(solution)/shard_map/ppermute | solution.py:432
  28.1 3.2 %collective-permute-done.1.rim_b = bf16[6,48,256]{2,1,0:T(8,128)(2,1)S(1)} collective-permute-done((bf16[6,48,256]{2,1,0:T(8,128)(2,1)S(1)}, bf16[6,48,256]{2,1,0:T(8,128)(2,1)S(1)}, u32[]{:S(2)}, u32[]{:S(2)}) %collective-permute-start.1) | collective-permute-done | bytes 147488 | tf_op jit(solution)/shard_map/ppermute | solution.py:433
  31.3 3.0 %shard_map.91 = bf16[8,48,256]{2,1,0:T(8,128)(2,1)S(1)} custom-call(bf16[6,48,256]{2,1,0:T(8,128)(2,1)S(1)} %collective-permute-done.rim_a, bf16[8,48,256]{2,1,0:T(8,128)(2,1)S(1)} %all_to_all.10.mid, bf16[6,48,256]{2,1,0:T(8,128)(2,1)S(1)} %collective-permute-done.1.rim_b, bf16[256,2304]{1,0:T(8,128)(2,1)S(1)} %get-tuple-element.16.w1a, ...), custom_call_target="tpu_custom_call" | custom-call | tf_op jit(solution)/shard_map/pallas_call | solution.py:367
  34.3 7.7 %all_to_all.11.got = bf16[8,48,256]{2,1,0:T(8,128)(2,1)S(1)} all-to-all(bf16[8,48,256]{2,1,0:T(8,128)(2,1)S(1)} %shard_map.91), channel_id=1, replica_groups={{0,1,2,3,4,5,6,7},{8,9,10,11,12,13,14,15},{16,17,18,19,20,21,22,23},{24..., dimensions={0} | all-to-all | bytes 393216 | tf_op jit(solution)/shard_map/all_to_all | solution.py:465
  42.0 1.1 %shard_map.92 = (bf16[256,256]{1,0:T(8,128)(2,1)}, bf16[256,128]{1,0:T(8,128)(2,1)}) custom-call(bf16[8,48,256]{2,1,0:T(8,128)(2,1)S(1)} %all_to_all.11.got), custom_call_target="tpu_custom_call" | custom-call | tf_op jit(solution)/shard_map/pallas_call | solution.py:367
  (1 shorter events, 0.0 us)
Async XLA Ops:
  0.6 24.8 %copy-start.5 = (bf16[64]{0:T(256)(128)(2,1)S(1)}, bf16[64]{0:T(256)(128)(2,1)}, u32[]{:S(2)}) copy-start(bf16[64]{0:T(256)(128)(2,1)} %param.9) | copy-start | bytes 388
  0.6 24.8 %copy-start.2 = (bf16[27,64,64]{2,1,0:T(8,128)(2,1)S(1)}, bf16[27,64,64]{2,1,0:T(8,128)(2,1)}, u32[]{:S(2)}) copy-start(bf16[27,64,64]{2,1,0:T(8,128)(2,1)} %k1.1) | copy-start | bytes 663556
  0.7 25.0 %copy-start = (bf16[27,64,64]{2,1,0:T(8,128)(2,1)S(1)}, bf16[27,64,64]{2,1,0:T(8,128)(2,1)}, u32[]{:S(2)}) copy-start(bf16[27,64,64]{2,1,0:T(8,128)(2,1)} %k2.1) | copy-start | bytes 663556
  0.7 25.0 %copy-start.1 = (bf16[27,64,128]{2,1,0:T(8,128)(2,1)S(1)}, bf16[27,64,128]{2,1,0:T(8,128)(2,1)}, u32[]{:S(2)}) copy-start(bf16[27,64,128]{2,1,0:T(8,128)(2,1)} %k3.1) | copy-start | bytes 1327108
  0.7 25.0 %copy-start.3 = (bf16[64]{0:T(256)(128)(2,1)S(1)}, bf16[64]{0:T(256)(128)(2,1)}, u32[]{:S(2)}) copy-start(bf16[64]{0:T(256)(128)(2,1)} %param.11) | copy-start | bytes 388
  0.7 25.0 %copy-start.4 = (bf16[64]{0:T(256)(128)(2,1)S(1)}, bf16[64]{0:T(256)(128)(2,1)}, u32[]{:S(2)}) copy-start(bf16[64]{0:T(256)(128)(2,1)} %param.13) | copy-start | bytes 388
  2.0 9.7 %collective-permute-start.2 = (bf16[1312,128]{1,0:T(8,128)(2,1)S(1)}, bf16[1312,128]{1,0:T(8,128)(2,1)S(1)}, u32[]{:S(2)}, u32[]{:S(2)}) collective-permute-start(bf16[1312,128]{1,0:T(8,128)(2,1)S(1)} %shard_map.89), channel_id=1, source_target_pairs={{0,1},{1,0},{2,3},{3,2},{4,5},{5,4},{6,7},{7,6},{8,9},{9,8},{10,11... | collective-permute-start | bytes 1007624 | tf_op jit(solution)/shard_map/ppermute | solution.py:418
  11.7 13.9 %collective-permute-start.3 = (bf16[1312,128]{1,0:T(8,128)(2,1)S(1)}, bf16[1312,128]{1,0:T(8,128)(2,1)S(1)}, u32[]{:S(2)}, u32[]{:S(2)}) collective-permute-start(bf16[1312,128]{1,0:T(8,128)(2,1)S(1)} %collective-permute-done.2.over), channel_id=1, source_target_pairs={{0,2},{2,0},{4,6},{6,4},{8,10},{10,8},{12,14},{14,12},{16,18},{18,... | collective-permute-start | bytes 1007624 | tf_op jit(solution)/shard_map/ppermute | solution.py:434
  21.8 6.3 %collective-permute-start = (bf16[6,48,256]{2,1,0:T(8,128)(2,1)S(1)}, bf16[6,48,256]{2,1,0:T(8,128)(2,1)S(1)}, u32[]{:S(2)}, u32[]{:S(2)}) collective-permute-start(bf16[6,48,256]{2,1,0:T(8,128)(2,1)S(1)} %get-tuple-element.14), channel_id=1, source_target_pairs={{0,8},{2,10},{4,12},{6,14},{16,24},{18,26},{20,28},{22,30},{8,0},{... | collective-permute-start | bytes 442376 | tf_op jit(solution)/shard_map/ppermute | solution.py:432
  23.5 7.8 %collective-permute-start.1 = (bf16[6,48,256]{2,1,0:T(8,128)(2,1)S(1)}, bf16[6,48,256]{2,1,0:T(8,128)(2,1)S(1)}, u32[]{:S(2)}, u32[]{:S(2)}) collective-permute-start(bf16[6,48,256]{2,1,0:T(8,128)(2,1)S(1)} %get-tuple-element.15), channel_id=1, source_target_pairs={{8,16},{10,18},{12,20},{14,22},{16,8},{18,10},{20,12},{22,14},{9,1... | collective-permute-start | bytes 442376 | tf_op jit(solution)/shard_map/ppermute | solution.py:433

commit v4 on v3

--- a/solution.py
+++ b/solution.py
@@ -139,8 +139,9 @@
     to_second[...] = mid[pl.ds(2 * odd, n)]
 
 
-def first_kernel(k1, b1, w1a, w1c, bias):
+def first_kernel(k1, k2, b1, w1a, w1c, v2a, v2c, bias):
     one = banded(lambda t: k1[t])
+    two = banded(lambda t: k2[t])
     zero = jnp.zeros((64, 128), BF)
     for dp in range(3):
         for dw in range(3):
@@ -152,78 +153,47 @@
             lanes = slice(128 * t, 128 * t + 128)
             w1c[0:64, lanes] = d
             w1c[64:128, lanes] = c
+            a, b, c, d = two(dp, dw)
+            v2a[0:64, lanes] = a
+            v2a[64:128, lanes] = b
+            v2c[0:64, lanes] = c
+            v2c[64:128, lanes] = d
     bias[...] = jnp.broadcast_to(jnp.concatenate([b1[...].astype(F32)] * 4, axis=1), bias.shape)
-
-
-def second_kernel(k2, k3, b2, b3, over, beside, w2a, w2c, w3, bias2, bias3):
-    half, core = lax.axis_index("filt"), lax.axis_index("slab") % 2
-    mine, other = half * 64, 64 - half * 64
-
-    def own(t):
-        return k2[t]
-
-    def piece(ref):
-        def rows(t):
-            both = ref[16 * t : 16 * t + 16, :]
-            return jnp.concatenate([both[:, :64], both[:, 64:]], axis=0)
-
-        return rows
-
-    sources = (
-        (own, mine, 64),
-        (piece(over), other + 32 * core, 32),
-        (piece(beside), other + 32 - 32 * core, 32),
-    )
-    for dp in range(3):
-        for dw in range(3):
-            t = 3 * dp + dw
-            lanes = slice(128 * t, 128 * t + 128)
-            for rows, at, size in sources:
-                a, b, c, d = banded(rows)(dp, dw)
-                w2a[pl.ds(aligned(at, 32), size), lanes] = a
-                w2a[pl.ds(aligned(128 + at, 32), size), lanes] = b
-                w2c[pl.ds(aligned(at, 32), size), lanes] = c
-                w2c[pl.ds(aligned(128 + at, 32), size), lanes] = d
-    for t in range(27):
-        w3[t, 0:64, :] = k3[t]
-        w3[t, pl.ds(aligned(64 + 32 * core, 32), 32), :] = over[432 + 32 * t : 464 + 32 * t, :]
-        w3[t, pl.ds(aligned(96 - 32 * core, 32), 32), :] = beside[432 + 32 * t : 464 + 32 * t, :]
-    theirs = over[1296:1297, :].astype(F32)
-    b2, b3 = b2[...].astype(F32), b3[...].astype(F32)
-    there2, there3 = theirs[:, :64], theirs[:, 64:]
-    low = jnp.where(half == 0, b2, there2)
-    high = jnp.where(half == 0, there2, b2)
-    bias2[...] = jnp.broadcast_to(jnp.concatenate([low, high], axis=1), bias2.shape)
-    bias3[...] = jnp.broadcast_to(jnp.concatenate([b3, there3], axis=1), bias3.shape)
 
 
 def shifted(x, by):
     return pltpu.roll(x, (-by) % x.shape[0], 0)
 
 
-def main_kernel(
-    rim_a, mid, rim_b, w1a, w1c, w2a, w2c, w3, b1, b2, b3, out, q, x34, pd, hd
-):
+TAPS = [(dp, dw) for dp in range(3) for dw in range(3)]
+
+
+def inside(first, planes):
     half, slab = lax.axis_index("filt"), lax.axis_index("slab")
     layer, layers = slab // LAYER, lax.axis_size("slab") // LAYER
     group = slab % LAYER * lax.axis_size("filt") + half
-    planes = 3 + LAYER + 3
-    odd = layer % 2 == 1
-    lane = lax.broadcasted_iota(jnp.int32, (1, 128), 1)
-    left = lane < 64
-
+    row = lax.broadcasted_iota(jnp.int32, (planes * FRAME, 1), 0)
+    col = 16 * group - LEAD + row % FRAME
+    plane = LAYER * layer + first + row // FRAME
+    return (plane >= 0) & (plane < LAYER * layers) & (col >= 0) & (col < 128)
+
+
+def pair(parts, weights):
+    n = parts[0].shape[0]
+    all_rows = dot(jnp.concatenate(parts, axis=0), weights, NT)
+    return [all_rows[n * i : n * i + n] for i in range(len(parts))]
+
+
+def lanes_of(ref, n, lo, hi):
+    return [ref[dw, FRAME * dp : FRAME * dp + n, lo:hi] for dp, dw in TAPS]
+
+
+def spread_runs(run, planes, q, x34):
+    left = lax.broadcasted_iota(jnp.int32, (1, 128), 1) < 64
     for f in range(2):
         for par in range(2):
-            runs = []
-            for v in range(planes):
-                rows = slice(RUN * par, RUN * par + RUN)
-                if 3 <= v < 3 + LAYER:
-                    run = mid[2 * (v - 3) + f, rows, :]
-                else:
-                    at = 2 * (v if v < 3 else v - 3 - LAYER) + f
-                    run = jnp.where(odd == (v < 3), rim_a[at, rows, :], rim_b[at, rows, :])
-                runs.append(run.astype(F32))
-            whole = jnp.concatenate(runs, axis=0)
+            rows = slice(RUN * par, RUN * par + RUN)
+            whole = jnp.concatenate([run(v, f, rows).astype(F32) for v in planes], axis=0)
             q[f, 1 + par] = whole.astype(BF)
             if par == 0:
                 q[f, 3] = shifted(whole, 1).astype(BF)
@@ -232,72 +202,141 @@
     for a in range(4):
         x34[a] = jnp.where(left, q[1, a, :, 0:128], q[0, a, :, 128:256])
 
+
+def products(q, x34, w1a, w1c, step):
+    left = lax.broadcasted_iota(jnp.int32, (1, 128), 1) < 64
+    n = LAYER * FRAME
+    out = []
+    for dp in range(3):
+        rows = slice(FRAME * step * dp, FRAME * step * dp + n)
+
+        def pick(ref, par):
+            return jnp.concatenate([ref[par + dw, rows, :] for dw in range(3)], axis=1)
+
+        cross = pair([pick(x34, par) for par in range(2)], w1c[:, 384 * dp : 384 * dp + 384])
+        sums = []
+        for f in range(2):
+            ys = pair([pick(q.at[f], par) for par in range(2)], w1a[:, 768 * dp : 768 * dp + 768])
+            for par in range(2):
+                low, high = ys[par][:, :128], ys[par][:, 128:]
+                if f == 0:
+                    high = high + jnp.where(left, 0.0, cross[par])
+                else:
+                    low = low + jnp.where(left, cross[par], 0.0)
+                ys[par] = jnp.concatenate([low, high], axis=1)
+            sums.append(ys)
+        out.append(sums)
+    return out
+
+
+def frame(x, i):
+    return x[FRAME * i : FRAME * i + FRAME]
+
+
+def add(terms):
+    return functools.reduce(jnp.add, terms)
+
+
+def inner_kernel(mid, w1a, w1c, acc, q, x34):
+    spread_runs(lambda v, f, rows: mid[2 * v + f, rows, :], range(LAYER), q, x34)
+    sums = products(q, x34, w1a, w1c, 0)
+    for f in range(2):
+        for par in range(2):
+            for e in range(LAYER + 2):
+                terms = [
+                    frame(sums[dp][f][par], e - 2 + dp)
+                    for dp in range(3)
+                    if 0 <= e - 2 + dp < LAYER
+                ]
+                acc[f, par, FRAME * e : FRAME * e + FRAME, :] = add(terms)
+
+
+def one_kernel(rim_a, rim_b, w1a, w1c, b1, acc, skips, pd, q, x34):
+    odd = lax.axis_index("slab") // LAYER % 2 == 1
+    left = lax.broadcasted_iota(jnp.int32, (1, 128), 1) < 64
+
+    def run(v, f, rows):
+        at = 2 * (v % 3) + f
+        return jnp.where(odd == (v < 3), rim_a[at, rows, :], rim_b[at, rows, :])
+
+    spread_runs(run, range(6), q, x34)
+    sums = products(q, x34, w1a, w1c, 1)
     u = LAYER + 4
-    m = u * FRAME
-    taps = [(dp, dw) for dp in range(3) for dw in range(3)]
-
-    def pick(ref, f, par):
-        parts = [ref[f, par + dw, FRAME * dp : FRAME * dp + m, :] for dp, dw in taps]
-        return jnp.concatenate(parts, axis=1)
-
-    def pick34(par):
-        parts = [x34[par + dw, FRAME * dp : FRAME * dp + m, :] for dp, dw in taps]
-        return jnp.concatenate(parts, axis=1)
-
-    def pair(parts, weights):
-        n = parts[0].shape[0]
-        all_rows = dot(jnp.concatenate(parts, axis=0), weights, NT)
-        return [all_rows[n * i : n * i + n] for i in range(len(parts))]
-
-    cross = pair([pick34(0), pick34(1)], w1c[...])
-    sums = []
-    for f in range(2):
-        sums += pair([pick(q, f, par) for par in range(2)], w1a[...])
+    targets = ((0, 1, 2, u - 1), (0, 1, u - 2, u - 1), (0, u - 3, u - 2, u - 1))
     bias = b1[0:1, :]
-    row = lax.broadcasted_iota(jnp.int32, (m, 1), 0)
-    pooled_col = 16 * group - LEAD + row % FRAME
-    plane = LAYER * layer - 2 + row // FRAME
-    inside = (plane >= 0) & (plane < LAYER * layers) & (pooled_col >= 0) & (pooled_col < 128)
+    within = inside(-2, u)
     tiles = []
     for f in range(2):
         ys = []
         for par in range(2):
-            y = sums[2 * f + par]
-            if f == 0:
-                extra = jnp.where(left, 0.0, cross[par])
-                y = jnp.concatenate([y[:, :128], y[:, 128:] + extra], axis=1)
-            else:
-                extra = jnp.where(left, cross[par], 0.0)
-                y = jnp.concatenate([y[:, :128] + extra, y[:, 128:]], axis=1)
-            y = jnp.maximum(y + bias, 0.0).astype(BF).astype(F32)
+            planes = []
+            for plane in range(u):
+                terms = [
+                    frame(sums[dp][f][par], targets[dp].index(plane))
+                    for dp in range(3)
+                    if plane in targets[dp]
+                ]
+                if 1 <= plane <= u - 2:
+                    terms.append(acc[f, par, FRAME * (plane - 1) : FRAME * plane, :])
+                planes.append(add(terms))
             for s in range(LAYER):
-                top = FRAME * (2 + s) + LEAD
-                out[2 * s + f, 16 * par : 16 * par + 16, :] = y[top : top + 16, :].astype(BF)
-            ys.append(y)
-        y = jnp.where(inside, jnp.maximum(ys[0], ys[1]), 0.0)
+                kept = planes[2 + s][LEAD : LEAD + 16, :]
+                kept = jnp.maximum(kept + bias, 0.0).astype(BF)
+                skips[2 * s + f, 16 * par : 16 * par + 16, :] = kept
+            ys.append(jnp.concatenate(planes, axis=0))
+        y = jnp.maximum(ys[0], ys[1])
         y0, y1 = y[:, :128], y[:, 128:]
         y0 = jnp.maximum(y0, pltpu.roll(y0, 64, 1))
         y1 = jnp.maximum(y1, pltpu.roll(y1, 64, 1))
-        tiles.append(jnp.where(left, y0, y1))
+        y = jnp.maximum(jnp.where(left, y0, y1) + bias[:, :128], 0.0)
+        tiles.append(jnp.where(within, y, 0.0))
     pooled = jnp.concatenate(tiles, axis=1)
-
     for dw in range(3):
         pd[dw] = shifted(pooled, dw - 1).astype(BF)
+
+
+def two_kernel(pd, v2a, v2c, k3, over, beside, b2, b3, skips, out, w2a, w2c, hd):
+    half, core = lax.axis_index("filt"), lax.axis_index("slab") % 2
+    lane = lax.broadcasted_iota(jnp.int32, (1, 128), 1)
+    left = lane < 64
+    out[:, 0:32, :] = skips[...]
+
+    mine, other = half * 64, 64 - half * 64
+    for row in range(2):
+        w2a[pl.ds(aligned(128 * row + mine, 64), 64), :] = v2a[64 * row : 64 * row + 64, :]
+        w2c[pl.ds(aligned(128 * row + mine, 64), 64), :] = v2c[64 * row : 64 * row + 64, :]
+
+    def piece(ref):
+        def rows(t):
+            both = ref[16 * t : 16 * t + 16, :]
+            return jnp.concatenate([both[:, :64], both[:, 64:]], axis=0)
+
+        return banded(rows)
+
+    for rows, at in ((piece(over), other + 32 * core), (piece(beside), other + 32 - 32 * core)):
+        for dp, dw in TAPS:
+            lanes = slice(128 * (3 * dp + dw), 128 * (3 * dp + dw) + 128)
+            a, b, c, d = rows(dp, dw)
+            w2a[pl.ds(aligned(at, 32), 32), lanes] = a
+            w2a[pl.ds(aligned(128 + at, 32), 32), lanes] = b
+            w2c[pl.ds(aligned(at, 32), 32), lanes] = c
+            w2c[pl.ds(aligned(128 + at, 32), 32), lanes] = d
+    theirs = over[1296:1297, :].astype(F32)
+    here2, here3 = b2[...].astype(F32), b3[...].astype(F32)
+    there2, there3 = theirs[:, :64], theirs[:, 64:]
+    low = jnp.where(half == 0, here2, there2)
+    high = jnp.where(half == 0, there2, here2)
+    bias2 = jnp.concatenate([low, high], axis=1)
+    turned = jnp.concatenate([there3[:, 32:], there3[:, :32]], axis=1)
+    bias3 = jnp.concatenate([here3, jnp.where(core == 1, turned, there3)], axis=1)
+
     m = (LAYER + 2) * FRAME
-
-    def lanes_of(ref, n, lo, hi):
-        return [ref[dw, FRAME * dp : FRAME * dp + n, lo:hi] for dp, dw in taps]
-
     pairs = pair(
         [jnp.concatenate(lanes_of(pd, m, 128 * a, 128 * a + 128), axis=1) for a in range(2)],
         w2a[...],
     )
     parts = [jnp.where(left, b, a) for a, b in zip(lanes_of(pd, m, 0, 128), lanes_of(pd, m, 128, 256))]
     mixed = dot(jnp.concatenate(parts, axis=1), w2c[...], NT)
-    row = lax.broadcasted_iota(jnp.int32, (m, 1), 0)
-    pooled_col = 16 * group - LEAD + row % FRAME
-    plane = LAYER * layer - 1 + row // FRAME
-    inside = (plane >= 0) & (plane < LAYER * layers) & (pooled_col >= 0) & (pooled_col < 128)
     hidden = jnp.concatenate(
         [
             pairs[0][:, :128],
@@ -307,17 +346,21 @@
         ],
         axis=1,
     )
-    bias = jnp.concatenate([b2[0:1, :]] * 4, axis=1)
-    hidden = jnp.where(inside, jnp.maximum(hidden + bias, 0.0), 0.0).astype(BF).astype(F32)
+    bias = jnp.concatenate([bias2] * 4, axis=1)
+    hidden = jnp.where(inside(-1, LAYER + 2), jnp.maximum(hidden + bias, 0.0), 0.0).astype(BF).astype(F32)
     for dw in range(3):
         hd[dw] = shifted(hidden, dw - 1).astype(BF)
 
     m = LAYER * FRAME
 
+    def third(t):
+        rows = slice(432 + 32 * t, 464 + 32 * t)
+        return jnp.concatenate([k3[t], over[rows, :], beside[rows, :]], axis=0)
+
     none = jnp.zeros((128, 128), BF)
     straight, across = [[], []], [[], []]
-    for dp, dw in taps:
-        k0, k1, k2 = (w3[9 * dp + 3 * dr + dw] for dr in range(3))
+    for dp, dw in TAPS:
+        k0, k1, k2 = (third(9 * dp + 3 * dr + dw) for dr in range(3))
         straight[0] += [k1, k2]
         straight[1] += [k0, k1]
         across[0] += [none, k2]
@@ -331,11 +374,13 @@
     mixed = dot(jnp.concatenate(lanes_of(hd, m, 128, 384), axis=1), w3c, NT)
     t0, t1 = both[:m, :128], both[:m, 128:] + mixed[:, :128]
     t2, t3 = both[m:, :128] + mixed[:, 128:], both[m:, 128:]
-    bias = b3[0:1, :]
-    t0, t1, t2, t3 = (jnp.maximum(t + bias, 0.0) for t in (t0, t1, t2, t3))
+    t0, t1, t2, t3 = (jnp.maximum(t + bias3, 0.0) for t in (t0, t1, t2, t3))
     r0, r1, r2, r3 = (pltpu.roll(t, 64, 1) for t in (t0, t1, t2, t3))
     first = jnp.concatenate([jnp.where(left, t0, r1), jnp.where(left, t2, r3)], axis=1)
     second = jnp.concatenate([jnp.where(left, r0, t1), jnp.where(left, r2, t3)], axis=1)
+    lane = lax.broadcasted_iota(jnp.int32, (1, 256), 1)
+    swapped = jnp.where(lane % 64 < 32, pltpu.roll(second, 224, 1), pltpu.roll(second, 32, 1))
+    second = jnp.where(core == 1, swapped, second)
     for s in range(LAYER):
         top = FRAME * s + LEAD
         out[2 * s + half, 32:48, :] = first[top : top + 16, :].astype(BF)
@@ -416,10 +461,17 @@
         far=True,
     )
     over = lax.ppermute(sent, "filt", [(0, 1), (1, 0)])
-    w1a, w1c, bias1 = call(
+    w1a, w1c, v2a, v2c, bias1 = call(
         first_kernel,
-        (pltpu.VMEM((256, 2304), BF), pltpu.VMEM((128, 1152), BF), pltpu.VMEM((8, 256), F32)),
+        (
+            pltpu.VMEM((256, 2304), BF),
+            pltpu.VMEM((128, 1152), BF),
+            pltpu.VMEM((128, 1152), BF),
+            pltpu.VMEM((128, 1152), BF),
+            pltpu.VMEM((8, 256), F32),
+        ),
         kernel_one,
+        kernel_two,
         b1,
     )
     planes = pltpu.VMEM((2 * (LAYER - 1), 2 * RUN, 256), BF)
@@ -432,32 +484,32 @@
     rim_a = lax.ppermute(to_first, "slab", swaps(0))
     rim_b = lax.ppermute(to_second, "slab", swaps(1))
     beside = lax.ppermute(over, "slab", [(i, i ^ 1) for i in range(slabs)])
-    w2a, w2c, w3, bias2, bias3 = call(
-        second_kernel,
-        (
+
+    def space(planes):
+        rows = FRAME * planes
+        return [pltpu.VMEM((2, 4, rows, 256), BF), pltpu.VMEM((4, rows, 128), BF)]
+
+    acc = call(
+        inner_kernel,
+        pltpu.VMEM((2, 2, FRAME * (LAYER + 2), 256), F32),
+        *map(near, (mid, w1a, w1c)),
+        scratch=space(LAYER),
+        limit=24,
+    )
+    skips, pooled = call(
+        one_kernel,
+        (pltpu.VMEM((peers, 32, 256), BF), pltpu.VMEM((3, FRAME * (LAYER + 4), 256), BF)),
+        *map(near, (rim_a, rim_b, w1a, w1c, bias1, acc)),
+        scratch=space(6),
+        limit=24,
+    )
+    out = call(
+        two_kernel,
+        pltpu.VMEM((peers, 48, 256), BF),
+        *map(near, (pooled, v2a, v2c, kernel_three, over, beside, b2, b3, skips)),
+        scratch=[
             pltpu.VMEM((256, 1152), BF),
             pltpu.VMEM((256, 1152), BF),
-            pltpu.VMEM((27, 128, 128), BF),
-            pltpu.VMEM((8, 128), F32),
-            pltpu.VMEM((8, 128), F32),
-        ),
-        kernel_two,
-        kernel_three,
-        b2,
-        b3,
-        near(over),
-        near(beside),
-    )
-    frames = FRAME * (LAYER + 6)
-    operands = (rim_a, mid, rim_b, w1a, w1c, w2a, w2c, w3, bias1, bias2, bias3)
-    out = call(
-        main_kernel,
-        pltpu.VMEM((peers, 48, 256), BF),
-        *map(near, operands),
-        scratch=[
-            pltpu.VMEM((2, 4, frames, 256), BF),
-            pltpu.VMEM((4, frames, 128), BF),
-            pltpu.VMEM((3, FRAME * (LAYER + 4), 256), BF),
             pltpu.VMEM((3, FRAME * (LAYER + 2), 512), BF),
         ],
         limit=24,

time: 43.9 us -> 43.8 us (level)
    pallas_call x7 -> x8, Pallas kernels: 7.6 us -> 7.84 us  [call(): pl.pallas_call(kernel, out_shape=outs, in_specs=[pl.BlockSpec(memory_spac...]
  transfers between devices with their start and end apart: 4 -> 4, of which waited for: 3 -> 3; matrix products, arithmetic and copies ran while one was open for 0% -> 0% of each run, Pallas kernels for 5% -> 9%
where the time goes in v4:
time: 43.8 us; the launch traced here: 42.9 us
  blocking collectives  16.6 us (38%)
  waiting for transfers between devices  12.5 us (29%)
  Pallas kernels  7.84 us (18%)
  starting transfers between devices  5.14 us (12%)
  between operations  0.77 us (2%)
    all_to_all x1, blocking collectives, by_columns(): mid = exchange(blocks)  8.93 us
    ppermute x1, waiting for transfers between devices, by_columns(): over = lax.ppermute(sent, 'filt', [(0, 1), (1, 0)])  8.11 us
    pallas_call x8, Pallas kernels, call(): pl.pallas_call(kernel, out_shape=outs, in_specs=[pl.BlockSpec(memory_spac...  7.84 us
    all_to_all x1, blocking collectives, by_columns(): home = exchange(out)  7.7 us
    ppermute x1, waiting for transfers between devices, by_columns(): rim_b = lax.ppermute(to_second, 'slab', swaps(1))  3.18 us
    ppermute x1, starting transfers between devices, by_columns(): rim_b = lax.ppermute(to_second, 'slab', swaps(1))  1.91 us
    ppermute x1, starting transfers between devices, by_columns(): rim_a = lax.ppermute(to_first, 'slab', swaps(0))  1.64 us
    ppermute x1, starting transfers between devices, by_columns(): over = lax.ppermute(sent, 'filt', [(0, 1), (1, 0)])  1.58 us
  transfers between devices with their start and end apart: 4, of which 3 were waited for; matrix products, arithmetic and copies ran while one was open for 0% of the time, Pallas kernels for 9%

profile of v4, /device:TPU:16, one launch (start us, length us, event | category | flops | bytes accessed | tf_op | source)
XLA Modules:
  0.0 42.9 jit_solution(8376763037491384261)
XLA Ops:
  0.6 0.0 copy-start
  0.6 0.0 copy-start.5
  0.7 0.0 copy-start.2
  0.7 1.3 %shard_map.91 = bf16[1312,128]{1,0:T(8,128)(2,1)S(1)} custom-call(bf16[27,64,64]{2,1,0:T(8,128)(2,1)} %far2.1, bf16[27,64,128]{2,1,0:T(8,128)(2,1)} %k3.1, bf16[1,64]{1,0:T(2,128)(2,1)} %bitcast.6, bf16[1,64]{1,0:T(2,128)(2,1)} %bitcast.8), custom_call_target="tpu_custom_call" | custom-call | tf_op jit(solution)/shard_map/pallas_call | solution.py:412
  2.0 1.6 %collective-permute-start.2 = (bf16[1312,128]{1,0:T(8,128)(2,1)S(1)}, bf16[1312,128]{1,0:T(8,128)(2,1)S(1)}, u32[]{:S(2)}, u32[]{:S(2)}) collective-permute-start(bf16[1312,128]{1,0:T(8,128)(2,1)S(1)} %shard_map.91), channel_id=1, source_target_pairs={{0,1},{1,0},{2,3},{3,2},{4,5},{5,4},{6,7},{7,6},{8,9},{9,8},{10,11... | collective-permute-start | bytes 1007624 | tf_op jit(solution)/shard_map/ppermute | solution.py:463
  3.6 8.1 %collective-permute-done.2.over = bf16[1312,128]{1,0:T(8,128)(2,1)S(1)} collective-permute-done((bf16[1312,128]{1,0:T(8,128)(2,1)S(1)}, bf16[1312,128]{1,0:T(8,128)(2,1)S(1)}, u32[]{:S(2)}, u32[]{:S(2)}) %collective-permute-start.2) | collective-permute-done | bytes 335904 | tf_op jit(solution)/shard_map/ppermute | solution.py:463
  11.7 0.0 collective-permute-start.3
  11.7 1.2 %shard_map.86 = bf16[8,48,256]{2,1,0:T(8,128)(2,1)S(1)} custom-call(bf16[256,256]{1,0:T(8,128)(2,1)} %bitcast.11), custom_call_target="tpu_custom_call" | custom-call | tf_op jit(solution)/shard_map/pallas_call | solution.py:412
  12.8 8.9 %all_to_all.10.mid = bf16[8,48,256]{2,1,0:T(8,128)(2,1)S(1)} all-to-all(bf16[8,48,256]{2,1,0:T(8,128)(2,1)S(1)} %shard_map.86), channel_id=1, replica_groups={{0,1,2,3,4,5,6,7},{8,9,10,11,12,13,14,15},{16,17,18,19,20,21,22,23},{24..., dimensions={0} | all-to-all | bytes 393216 | tf_op jit(solution)/shard_map/all_to_all | solution.py:446
  21.8 1.6 %collective-permute-start = (bf16[6,48,256]{2,1,0:T(8,128)(2,1)S(1)}, bf16[6,48,256]{2,1,0:T(8,128)(2,1)S(1)}, u32[]{:S(2)}, u32[]{:S(2)}) collective-permute-start(bf16[6,48,256]{2,1,0:T(8,128)(2,1)S(1)} %get-tuple-element.13), channel_id=1, source_target_pairs={{0,8},{2,10},{4,12},{6,14},{16,24},{18,26},{20,28},{22,30},{8,0},{... | collective-permute-start | bytes 442376 | tf_op jit(solution)/shard_map/ppermute | solution.py:484
  23.4 1.9 %collective-permute-start.1 = (bf16[6,48,256]{2,1,0:T(8,128)(2,1)S(1)}, bf16[6,48,256]{2,1,0:T(8,128)(2,1)S(1)}, u32[]{:S(2)}, u32[]{:S(2)}) collective-permute-start(bf16[6,48,256]{2,1,0:T(8,128)(2,1)S(1)} %get-tuple-element.14), channel_id=1, source_target_pairs={{8,16},{10,18},{12,20},{14,22},{16,8},{18,10},{20,12},{22,14},{9,1... | collective-permute-start | bytes 442376 | tf_op jit(solution)/shard_map/ppermute | solution.py:485
  25.3 0.0 copy-done
  25.4 0.0 copy-done.5
  25.4 0.0 copy-done.2
  25.4 0.3 shard_map.88
  25.7 1.1 %shard_map.89.acc = f32[2,2,144,256]{3,2,1,0:T(8,128)S(1)} custom-call(bf16[8,48,256]{2,1,0:T(8,128)(2,1)S(1)} %all_to_all.10.mid, bf16[256,2304]{1,0:T(8,128)(2,1)S(1)} %get-tuple-element.15.w1a, bf16[128,1152]{1,0:T(8,128)(2,1)S(1)} %get-tuple-element.16.w1c), custom_call_target="tpu_custom_call" | custom-call | tf_op jit(solution)/shard_map/pallas_call | solution.py:412
  26.8 1.3 %collective-permute-done.rim_a = bf16[6,48,256]{2,1,0:T(8,128)(2,1)S(1)} collective-permute-done((bf16[6,48,256]{2,1,0:T(8,128)(2,1)S(1)}, bf16[6,48,256]{2,1,0:T(8,128)(2,1)S(1)}, u32[]{:S(2)}, u32[]{:S(2)}) %collective-permute-start) | collective-permute-done | bytes 147488 | tf_op jit(solution)/shard_map/ppermute | solution.py:484
  28.1 3.2 %collective-permute-done.1.rim_b = bf16[6,48,256]{2,1,0:T(8,128)(2,1)S(1)} collective-permute-done((bf16[6,48,256]{2,1,0:T(8,128)(2,1)S(1)}, bf16[6,48,256]{2,1,0:T(8,128)(2,1)S(1)}, u32[]{:S(2)}, u32[]{:S(2)}) %collective-permute-start.1) | collective-permute-done | bytes 147488 | tf_op jit(solution)/shard_map/ppermute | solution.py:485
  31.2 0.0 copy-start.1
  31.2 0.0 copy-start.3
  31.2 0.0 copy-start.4
  31.2 1.2 %shard_map.90 = (bf16[8,32,256]{2,1,0:T(8,128)(2,1)S(1)}, bf16[3,192,256]{2,1,0:T(8,128)(2,1)S(1)}) custom-call(bf16[6,48,256]{2,1,0:T(8,128)(2,1)S(1)} %collective-permute-done.rim_a, bf16[6,48,256]{2,1,0:T(8,128)(2,1)S(1)} %collective-permute-done.1.rim_b, bf16[256,2304]{1,0:T(8,128)(2,1)S(1)} %get-tuple-element.15.w1a, ...), custom_call_target="tpu_custom_call" | custom-call | tf_op jit(solution)/shard_map/pallas_call | solution.py:412
  32.5 0.0 collective-permute-done.3.beside
  32.5 0.0 copy-done.1
  32.5 0.0 copy-done.3
  32.5 0.0 copy-done.4
  32.5 1.7 %shard_map.92 = bf16[8,48,256]{2,1,0:T(8,128)(2,1)S(1)} custom-call(bf16[3,192,256]{2,1,0:T(8,128)(2,1)S(1)} %get-tuple-element.18.pd, bf16[128,1152]{1,0:T(8,128)(2,1)S(1)} %get-tuple-element.19.v2a, bf16[128,1152]{1,0:T(8,128)(2,1)S(1)} %get-tuple-element.20.v2c, bf16[27,64,128]{2,1,0:T(8,128)(2,1)S(1)} %copy-done.1, ...), custom_call_target="tpu_custom_call" | custom-call | tf_op jit(solution)/shard_map/pallas_call | solution.py:412
  34.2 7.7 %all_to_all.11.got = bf16[8,48,256]{2,1,0:T(8,128)(2,1)S(1)} all-to-all(bf16[8,48,256]{2,1,0:T(8,128)(2,1)S(1)} %shard_map.92), channel_id=1, replica_groups={{0,1,2,3,4,5,6,7},{8,9,10,11,12,13,14,15},{16,17,18,19,20,21,22,23},{24..., dimensions={0} | all-to-all | bytes 393216 | tf_op jit(solution)/shard_map/all_to_all | solution.py:517
  41.9 1.1 %shard_map.93 = (bf16[256,256]{1,0:T(8,128)(2,1)}, bf16[256,128]{1,0:T(8,128)(2,1)}) custom-call(bf16[8,48,256]{2,1,0:T(8,128)(2,1)S(1)} %all_to_all.11.got), custom_call_target="tpu_custom_call" | custom-call | tf_op jit(solution)/shard_map/pallas_call | solution.py:412
  (1 shorter events, 0.0 us)
Async XLA Ops:
  0.6 24.7 %copy-start = (bf16[27,64,64]{2,1,0:T(8,128)(2,1)S(1)}, bf16[27,64,64]{2,1,0:T(8,128)(2,1)}, u32[]{:S(2)}) copy-start(bf16[27,64,64]{2,1,0:T(8,128)(2,1)} %far2.1) | copy-start | bytes 663556
  0.6 24.7 %copy-start.5 = (bf16[64]{0:T(256)(128)(2,1)S(1)}, bf16[64]{0:T(256)(128)(2,1)}, u32[]{:S(2)}) copy-start(bf16[64]{0:T(256)(128)(2,1)} %param.9) | copy-start | bytes 388
  0.7 24.7 %copy-start.2 = (bf16[27,64,64]{2,1,0:T(8,128)(2,1)S(1)}, bf16[27,64,64]{2,1,0:T(8,128)(2,1)}, u32[]{:S(2)}) copy-start(bf16[27,64,64]{2,1,0:T(8,128)(2,1)} %k1.1) | copy-start | bytes 663556
  2.0 9.7 %collective-permute-start.2 = (bf16[1312,128]{1,0:T(8,128)(2,1)S(1)}, bf16[1312,128]{1,0:T(8,128)(2,1)S(1)}, u32[]{:S(2)}, u32[]{:S(2)}) collective-permute-start(bf16[1312,128]{1,0:T(8,128)(2,1)S(1)} %shard_map.91), channel_id=1, source_target_pairs={{0,1},{1,0},{2,3},{3,2},{4,5},{5,4},{6,7},{7,6},{8,9},{9,8},{10,11... | collective-permute-start | bytes 1007624 | tf_op jit(solution)/shard_map/ppermute | solution.py:463
  11.7 20.8 %collective-permute-start.3 = (bf16[1312,128]{1,0:T(8,128)(2,1)S(1)}, bf16[1312,128]{1,0:T(8,128)(2,1)S(1)}, u32[]{:S(2)}, u32[]{:S(2)}) collective-permute-start(bf16[1312,128]{1,0:T(8,128)(2,1)S(1)} %collective-permute-done.2.over), channel_id=1, source_target_pairs={{0,2},{2,0},{4,6},{6,4},{8,10},{10,8},{12,14},{14,12},{16,18},{18,... | collective-permute-start | bytes 1007624 | tf_op jit(solution)/shard_map/ppermute | solution.py:486
  21.8 6.3 %collective-permute-start = (bf16[6,48,256]{2,1,0:T(8,128)(2,1)S(1)}, bf16[6,48,256]{2,1,0:T(8,128)(2,1)S(1)}, u32[]{:S(2)}, u32[]{:S(2)}) collective-permute-start(bf16[6,48,256]{2,1,0:T(8,128)(2,1)S(1)} %get-tuple-element.13), channel_id=1, source_target_pairs={{0,8},{2,10},{4,12},{6,14},{16,24},{18,26},{20,28},{22,30},{8,0},{... | collective-permute-start | bytes 442376 | tf_op jit(solution)/shard_map/ppermute | solution.py:484
  23.4 7.8 %collective-permute-start.1 = (bf16[6,48,256]{2,1,0:T(8,128)(2,1)S(1)}, bf16[6,48,256]{2,1,0:T(8,128)(2,1)S(1)}, u32[]{:S(2)}, u32[]{:S(2)}) collective-permute-start(bf16[6,48,256]{2,1,0:T(8,128)(2,1)S(1)} %get-tuple-element.14), channel_id=1, source_target_pairs={{8,16},{10,18},{12,20},{14,22},{16,8},{18,10},{20,12},{22,14},{9,1... | collective-permute-start | bytes 442376 | tf_op jit(solution)/shard_map/ppermute | solution.py:485
  31.2 1.2 %copy-start.1 = (bf16[27,64,128]{2,1,0:T(8,128)(2,1)S(1)}, bf16[27,64,128]{2,1,0:T(8,128)(2,1)}, u32[]{:S(2)}) copy-start(bf16[27,64,128]{2,1,0:T(8,128)(2,1)} %k3.1) | copy-start | bytes 1327108
  31.2 1.2 %copy-start.3 = (bf16[64]{0:T(256)(128)(2,1)S(1)}, bf16[64]{0:T(256)(128)(2,1)}, u32[]{:S(2)}) copy-start(bf16[64]{0:T(256)(128)(2,1)} %param.11) | copy-start | bytes 388
  31.2 1.2 %copy-start.4 = (bf16[64]{0:T(256)(128)(2,1)S(1)}, bf16[64]{0:T(256)(128)(2,1)}, u32[]{:S(2)}) copy-start(bf16[64]{0:T(256)(128)(2,1)} %param.13) | copy-start | bytes 388

commit v5 on v4

--- a/solution.py
+++ b/solution.py
@@ -84,9 +84,18 @@
     return lax.dot_general(a, b, dims, preferred_element_type=F32)
 
 
-def pack_kernel(far, blocks, volume, sem):
-    copy = pltpu.make_async_copy(far, volume, sem)
-    copy.start()
+def pack_kernel(far, far2, far3, far_b2, far_b3, blocks, k2, k3, b2, b3, volume, sems):
+    half = pl.ds(aligned(32 * (lax.axis_index("slab") % 2), 32), 32)
+    pairs = (
+        (far, volume),
+        (far2.at[:, half, :], k2),
+        (far3.at[:, half, :], k3),
+        (far_b2, b2),
+        (far_b3, b3),
+    )
+    copies = [pltpu.make_async_copy(*ends, sems.at[i]) for i, ends in enumerate(pairs)]
+    for copy in copies:
+        copy.start()
     count, width = blocks.shape[0], volume.shape[1]
     shape = (count * 2 * RUN, width)
     row = lax.broadcasted_iota(jnp.int32, shape, 0)
@@ -94,27 +103,17 @@
     peer, rest = row // (2 * RUN), row % (2 * RUN)
     wanted = (width // count) * peer + 2 * (rest % RUN - LEAD) + rest // RUN
     chosen = jnp.where(wanted == col, 1.0, 0.0).astype(BF)
-    copy.wait()
+    copies[0].wait()
     blocks[...] = dot(chosen, volume[...], NT).astype(BF).reshape(blocks.shape)
+    for copy in copies[1:]:
+        copy.wait()
 
 
 def aligned(at, by):
     return pl.multiple_of(at, by)
 
 
-def send_kernel(far2, far3, far_b2, far_b3, sent, k2, k3, b2, b3, sems):
-    top = aligned(32 * (lax.axis_index("slab") % 2), 32)
-    half = pl.ds(top, 32)
-    copies = [
-        pltpu.make_async_copy(far, near, sems.at[i])
-        for i, (far, near) in enumerate(
-            ((far_b2, b2), (far_b3, b3), (far2.at[:, half, :], k2), (far3.at[:, half, :], k3))
-        )
-    ]
-    for copy in copies:
-        copy.start()
-    for copy in copies:
-        copy.wait()
+def send_kernel(k2, k3, b2, b3, sent):
     for t in range(27):
         sent[16 * t : 16 * t + 16, :] = jnp.concatenate([k2[t, :16, :], k2[t, 16:, :]], axis=1)
         sent[432 + 32 * t : 464 + 32 * t, :] = k3[t]
@@ -252,12 +251,15 @@
 
 
 def one_kernel(rim_a, rim_b, w1a, w1c, b1, acc, skips, pd, q, x34):
-    odd = lax.axis_index("slab") // LAYER % 2 == 1
+    layer, layers = lax.axis_index("slab") // LAYER, lax.axis_size("slab") // LAYER
+    odd = layer % 2 == 1
     left = lax.broadcasted_iota(jnp.int32, (1, 128), 1) < 64
 
     def run(v, f, rows):
         at = 2 * (v % 3) + f
-        return jnp.where(odd == (v < 3), rim_a[at, rows, :], rim_b[at, rows, :])
+        got = jnp.where(odd == (v < 3), rim_a[at, rows, :], rim_b[at, rows, :])
+        outside = layer == (0 if v < 3 else layers - 1)
+        return jnp.where(outside, jnp.zeros_like(got), got)
 
     spread_runs(run, range(6), q, x34)
     sums = products(q, x34, w1a, w1c, 1)
@@ -436,30 +438,25 @@
         tiled=True,
     )
     b1, b2, b3 = bias_one[None, :], bias_two[None, :], bias_three[None, :]
-    blocks = call(
+    blocks, *mine = call(
         pack_kernel,
-        pltpu.VMEM((peers, 2 * RUN, 256), BF),
+        (
+            pltpu.VMEM((peers, 2 * RUN, 256), BF),
+            pltpu.VMEM((27, 32, 64), BF),
+            pltpu.VMEM((27, 32, 128), BF),
+            pltpu.VMEM((1, 64), BF),
+            pltpu.VMEM((1, 64), BF),
+        ),
         volume.reshape(256, 256),
-        scratch=[pltpu.VMEM((256, 256), BF), pltpu.SemaphoreType.DMA],
-        far=True,
-    )
-    mid = exchange(blocks)
-    sent = call(
-        send_kernel,
-        pltpu.VMEM((1312, 128), BF),
         kernel_two,
         kernel_three,
         b2,
         b3,
-        scratch=[
-            pltpu.VMEM((27, 32, 64), BF),
-            pltpu.VMEM((27, 32, 128), BF),
-            pltpu.VMEM((1, 64), BF),
-            pltpu.VMEM((1, 64), BF),
-            pltpu.SemaphoreType.DMA((4,)),
-        ],
+        scratch=[pltpu.VMEM((256, 256), BF), pltpu.SemaphoreType.DMA((5,))],
         far=True,
     )
+    mid = exchange(blocks)
+    sent = call(send_kernel, pltpu.VMEM((1312, 128), BF), *map(near, mine))
     over = lax.ppermute(sent, "filt", [(0, 1), (1, 0)])
     w1a, w1c, v2a, v2c, bias1 = call(
         first_kernel,
@@ -479,7 +476,8 @@
 
     def swaps(start):
         up = [(i, i + LAYER) for i in range(slabs - LAYER) if i // LAYER % 2 == start]
-        return up + [(b, a) for a, b in up]
+        both = dict(up + [(b, a) for a, b in up])
+        return [(i, both.get(i, i ^ 1)) for i in range(slabs)]
 
     rim_a = lax.ppermute(to_first, "slab", swaps(0))
     rim_b = lax.ppermute(to_second, "slab", swaps(1))

time: 43.8 us -> 40.8 us (0.932)
  the two profiles are of different devices: /device:TPU:16 before, /device:TPU:17 now
where the time goes in v5:
time: 40.8 us; the launch traced here: 40.6 us
  blocking collectives  17.7 us (43%)
  waiting for transfers between devices  11.2 us (27%)
  Pallas kernels  6.76 us (17%)
  starting transfers between devices  4.2 us (10%)
  between operations  0.74 us (2%)
    all_to_all x1, blocking collectives, by_columns(): mid = exchange(blocks)  8.87 us
    all_to_all x1, blocking collectives, by_columns(): home = exchange(out)  8.84 us
    ppermute x1, waiting for transfers between devices, by_columns(): over = lax.ppermute(sent, 'filt', [(0, 1), (1, 0)])  7.53 us
    pallas_call x8, Pallas kernels, call(): pl.pallas_call(kernel, out_shape=outs, in_specs=[pl.BlockSpec(memory_spac...  6.76 us
    ppermute x1, waiting for transfers between devices, by_columns(): rim_a = lax.ppermute(to_first, 'slab', swaps(0))  2.6 us
    ppermute x1, starting transfers between devices, by_columns(): beside = lax.ppermute(over, 'slab', [(i, i ^ 1) for i in range(slabs)])  1.53 us
    ppermute x1, starting transfers between devices, by_columns(): rim_a = lax.ppermute(to_first, 'slab', swaps(0))  1.36 us
    ppermute x1, starting transfers between devices, by_columns(): over = lax.ppermute(sent, 'filt', [(0, 1), (1, 0)])  1.3 us
  transfers between devices with their start and end apart: 4, of which 3 were waited for; matrix products, arithmetic and copies ran while one was open for 0% of the time, Pallas kernels for 6%

profile of v5, /device:TPU:17, one launch (start us, length us, event | category | flops | bytes accessed | tf_op | source)
XLA Modules:
  0.0 40.6 jit_solution(10124884324255778727)
XLA Ops:
  0.6 0.0 copy-start
  0.6 0.0 copy-start.2
  0.7 0.0 copy-start.5
  0.7 1.3 %shard_map.86 = (bf16[8,48,256]{2,1,0:T(8,128)(2,1)S(1)}, bf16[27,32,64]{2,1,0:T(8,128)(2,1)S(1)}, bf16[27,32,128]{2,1,0:T(8,128)(2,1)S(1)}, bf16[1,64]{1,0:T(2,128)(2,1)S(1)}, bf16[1,64]{1,0:T(2,128)(2,1)S(1)}) custom-call(bf16[256,256]{1,0:T(8,128)(2,1)} %bitcast.11, bf16[27,64,64]{2,1,0:T(8,128)(2,1)} %k2.1, bf16[27,64,128]{2,1,0:T(8,128)(2,1)} %k3.1, ...), custom_call_target="tpu_custom_call" | custom-call | tf_op jit(solution)/shard_map/pallas_call | solution.py:414
  1.9 0.1 shard_map.91
  2.1 1.3 %collective-permute-start.2 = (bf16[1312,128]{1,0:T(8,128)(2,1)S(1)}, bf16[1312,128]{1,0:T(8,128)(2,1)S(1)}, u32[]{:S(2)}, u32[]{:S(2)}) collective-permute-start(bf16[1312,128]{1,0:T(8,128)(2,1)S(1)} %shard_map.91), channel_id=1, source_target_pairs={{0,1},{1,0},{2,3},{3,2},{4,5},{5,4},{6,7},{7,6},{8,9},{9,8},{10,11... | collective-permute-start | bytes 1007624 | tf_op jit(solution)/shard_map/ppermute | solution.py:460
  3.4 7.5 %collective-permute-done.2.over = bf16[1312,128]{1,0:T(8,128)(2,1)S(1)} collective-permute-done((bf16[1312,128]{1,0:T(8,128)(2,1)S(1)}, bf16[1312,128]{1,0:T(8,128)(2,1)S(1)}, u32[]{:S(2)}, u32[]{:S(2)}) %collective-permute-start.2) | collective-permute-done | bytes 335904 | tf_op jit(solution)/shard_map/ppermute | solution.py:460
  10.9 1.5 %collective-permute-start.3 = (bf16[1312,128]{1,0:T(8,128)(2,1)S(1)}, bf16[1312,128]{1,0:T(8,128)(2,1)S(1)}, u32[]{:S(2)}, u32[]{:S(2)}) collective-permute-start(bf16[1312,128]{1,0:T(8,128)(2,1)S(1)} %collective-permute-done.2.over), channel_id=1, source_target_pairs={{0,2},{2,0},{4,6},{6,4},{8,10},{10,8},{12,14},{14,12},{16,18},{18,... | collective-permute-start | bytes 1007624 | tf_op jit(solution)/shard_map/ppermute | solution.py:484
  12.4 8.9 %all_to_all.10.mid = bf16[8,48,256]{2,1,0:T(8,128)(2,1)S(1)} all-to-all(bf16[8,48,256]{2,1,0:T(8,128)(2,1)S(1)} %get-tuple-element.18), channel_id=1, replica_groups={{0,1,2,3,4,5,6,7},{8,9,10,11,12,13,14,15},{16,17,18,19,20,21,22,23},{24..., dimensions={0} | all-to-all | bytes 393216 | tf_op jit(solution)/shard_map/all_to_all | solution.py:458
  21.3 1.4 %collective-permute-start = (bf16[6,48,256]{2,1,0:T(8,128)(2,1)S(1)}, bf16[6,48,256]{2,1,0:T(8,128)(2,1)S(1)}, u32[]{:S(2)}, u32[]{:S(2)}) collective-permute-start(bf16[6,48,256]{2,1,0:T(8,128)(2,1)S(1)} %get-tuple-element.19), channel_id=1, source_target_pairs={{0,8},{2,10},{4,12},{6,14},{8,0},{10,2},{12,4},{14,6},{16,24},{18,... | collective-permute-start | bytes 442376 | tf_op jit(solution)/shard_map/ppermute | solution.py:482
  22.7 0.0 collective-permute-start.1
  22.7 0.0 copy-done
  22.7 0.0 copy-done.2
  22.7 0.0 copy-done.5
  22.7 0.3 shard_map.88
  23.0 1.1 %shard_map.89.acc = f32[2,2,144,256]{3,2,1,0:T(8,128)S(1)} custom-call(bf16[8,48,256]{2,1,0:T(8,128)(2,1)S(1)} %all_to_all.10.mid, bf16[256,2304]{1,0:T(8,128)(2,1)S(1)} %get-tuple-element.21.w1a, bf16[128,1152]{1,0:T(8,128)(2,1)S(1)} %get-tuple-element.22.w1c), custom_call_target="tpu_custom_call" | custom-call | tf_op jit(solution)/shard_map/pallas_call | solution.py:414
  24.1 2.6 %collective-permute-done.rim_a = bf16[6,48,256]{2,1,0:T(8,128)(2,1)S(1)} collective-permute-done((bf16[6,48,256]{2,1,0:T(8,128)(2,1)S(1)}, bf16[6,48,256]{2,1,0:T(8,128)(2,1)S(1)}, u32[]{:S(2)}, u32[]{:S(2)}) %collective-permute-start) | collective-permute-done | bytes 147488 | tf_op jit(solution)/shard_map/ppermute | solution.py:482
  26.7 1.0 %collective-permute-done.1.rim_b = bf16[6,48,256]{2,1,0:T(8,128)(2,1)S(1)} collective-permute-done((bf16[6,48,256]{2,1,0:T(8,128)(2,1)S(1)}, bf16[6,48,256]{2,1,0:T(8,128)(2,1)S(1)}, u32[]{:S(2)}, u32[]{:S(2)}) %collective-permute-start.1) | collective-permute-done | bytes 147488 | tf_op jit(solution)/shard_map/ppermute | solution.py:483
  27.8 0.0 copy-start.1
  27.8 0.0 copy-start.3
  27.8 0.0 copy-start.4
  27.8 1.2 %shard_map.90 = (bf16[8,32,256]{2,1,0:T(8,128)(2,1)S(1)}, bf16[3,192,256]{2,1,0:T(8,128)(2,1)S(1)}) custom-call(bf16[6,48,256]{2,1,0:T(8,128)(2,1)S(1)} %collective-permute-done.rim_a, bf16[6,48,256]{2,1,0:T(8,128)(2,1)S(1)} %collective-permute-done.1.rim_b, bf16[256,2304]{1,0:T(8,128)(2,1)S(1)} %get-tuple-element.21.w1a, ...), custom_call_target="tpu_custom_call" | custom-call | tf_op jit(solution)/shard_map/pallas_call | solution.py:414
  29.0 0.0 collective-permute-done.3.beside
  29.0 0.0 copy-done.1
  29.0 0.0 copy-done.3
  29.0 0.0 copy-done.4
  29.0 1.7 %shard_map.92 = bf16[8,48,256]{2,1,0:T(8,128)(2,1)S(1)} custom-call(bf16[3,192,256]{2,1,0:T(8,128)(2,1)S(1)} %get-tuple-element.24.pd, bf16[128,1152]{1,0:T(8,128)(2,1)S(1)} %get-tuple-element.25.v2a, bf16[128,1152]{1,0:T(8,128)(2,1)S(1)} %get-tuple-element.26.v2c, bf16[27,64,128]{2,1,0:T(8,128)(2,1)S(1)} %copy-done.1, ...), custom_call_target="tpu_custom_call" | custom-call | tf_op jit(solution)/shard_map/pallas_call | solution.py:414
  30.7 8.8 %all_to_all.11.got = bf16[8,48,256]{2,1,0:T(8,128)(2,1)S(1)} all-to-all(bf16[8,48,256]{2,1,0:T(8,128)(2,1)S(1)} %shard_map.92), channel_id=1, replica_groups={{0,1,2,3,4,5,6,7},{8,9,10,11,12,13,14,15},{16,17,18,19,20,21,22,23},{24..., dimensions={0} | all-to-all | bytes 393216 | tf_op jit(solution)/shard_map/all_to_all | solution.py:515
  39.5 1.1 %shard_map.93 = (bf16[256,256]{1,0:T(8,128)(2,1)}, bf16[256,128]{1,0:T(8,128)(2,1)}) custom-call(bf16[8,48,256]{2,1,0:T(8,128)(2,1)S(1)} %all_to_all.11.got), custom_call_target="tpu_custom_call" | custom-call | tf_op jit(solution)/shard_map/pallas_call | solution.py:414
  (1 shorter events, 0.0 us)
Async XLA Ops:
  0.6 22.1 %copy-start = (bf16[27,64,64]{2,1,0:T(8,128)(2,1)S(1)}, bf16[27,64,64]{2,1,0:T(8,128)(2,1)}, u32[]{:S(2)}) copy-start(bf16[27,64,64]{2,1,0:T(8,128)(2,1)} %k2.1) | copy-start | bytes 663556
  0.6 22.0 %copy-start.2 = (bf16[27,64,64]{2,1,0:T(8,128)(2,1)S(1)}, bf16[27,64,64]{2,1,0:T(8,128)(2,1)}, u32[]{:S(2)}) copy-start(bf16[27,64,64]{2,1,0:T(8,128)(2,1)} %k1.1) | copy-start | bytes 663556
  0.7 22.0 %copy-start.5 = (bf16[64]{0:T(256)(128)(2,1)S(1)}, bf16[64]{0:T(256)(128)(2,1)}, u32[]{:S(2)}) copy-start(bf16[64]{0:T(256)(128)(2,1)} %param.9) | copy-start | bytes 388
  2.1 8.8 %collective-permute-start.2 = (bf16[1312,128]{1,0:T(8,128)(2,1)S(1)}, bf16[1312,128]{1,0:T(8,128)(2,1)S(1)}, u32[]{:S(2)}, u32[]{:S(2)}) collective-permute-start(bf16[1312,128]{1,0:T(8,128)(2,1)S(1)} %shard_map.91), channel_id=1, source_target_pairs={{0,1},{1,0},{2,3},{3,2},{4,5},{5,4},{6,7},{7,6},{8,9},{9,8},{10,11... | collective-permute-start | bytes 1007624 | tf_op jit(solution)/shard_map/ppermute | solution.py:460
  10.9 18.1 %collective-permute-start.3 = (bf16[1312,128]{1,0:T(8,128)(2,1)S(1)}, bf16[1312,128]{1,0:T(8,128)(2,1)S(1)}, u32[]{:S(2)}, u32[]{:S(2)}) collective-permute-start(bf16[1312,128]{1,0:T(8,128)(2,1)S(1)} %collective-permute-done.2.over), channel_id=1, source_target_pairs={{0,2},{2,0},{4,6},{6,4},{8,10},{10,8},{12,14},{14,12},{16,18},{18,... | collective-permute-start | bytes 1007624 | tf_op jit(solution)/shard_map/ppermute | solution.py:484
  21.3 5.4 %collective-permute-start = (bf16[6,48,256]{2,1,0:T(8,128)(2,1)S(1)}, bf16[6,48,256]{2,1,0:T(8,128)(2,1)S(1)}, u32[]{:S(2)}, u32[]{:S(2)}) collective-permute-start(bf16[6,48,256]{2,1,0:T(8,128)(2,1)S(1)} %get-tuple-element.19), channel_id=1, source_target_pairs={{0,8},{2,10},{4,12},{6,14},{8,0},{10,2},{12,4},{14,6},{16,24},{18,... | collective-permute-start | bytes 442376 | tf_op jit(solution)/shard_map/ppermute | solution.py:482
  22.7 5.1 %collective-permute-start.1 = (bf16[6,48,256]{2,1,0:T(8,128)(2,1)S(1)}, bf16[6,48,256]{2,1,0:T(8,128)(2,1)S(1)}, u32[]{:S(2)}, u32[]{:S(2)}) collective-permute-start(bf16[6,48,256]{2,1,0:T(8,128)(2,1)S(1)} %get-tuple-element.20), channel_id=1, source_target_pairs={{0,2},{2,0},{4,6},{6,4},{8,16},{10,18},{12,20},{14,22},{16,8},{18,... | collective-permute-start | bytes 442376 | tf_op jit(solution)/shard_map/ppermute | solution.py:483
  27.8 1.2 %copy-start.1 = (bf16[27,64,128]{2,1,0:T(8,128)(2,1)S(1)}, bf16[27,64,128]{2,1,0:T(8,128)(2,1)}, u32[]{:S(2)}) copy-start(bf16[27,64,128]{2,1,0:T(8,128)(2,1)} %k3.1) | copy-start | bytes 1327108
  27.8 1.2 %copy-start.3 = (bf16[64]{0:T(256)(128)(2,1)S(1)}, bf16[64]{0:T(256)(128)(2,1)}, u32[]{:S(2)}) copy-start(bf16[64]{0:T(256)(128)(2,1)} %param.11) | copy-start | bytes 388
  27.8 1.2 %copy-start.4 = (bf16[64]{0:T(256)(128)(2,1)S(1)}, bf16[64]{0:T(256)(128)(2,1)}, u32[]{:S(2)}) copy-start(bf16[64]{0:T(256)(128)(2,1)} %param.13) | copy-start | bytes 388

commit v6 on v5

--- a/solution.py
+++ b/solution.py
@@ -113,12 +113,12 @@
     return pl.multiple_of(at, by)
 
 
-def send_kernel(k2, k3, b2, b3, sent):
+def send_kernel(k2, k3, b2, b3, sent2, sent3):
     for t in range(27):
-        sent[16 * t : 16 * t + 16, :] = jnp.concatenate([k2[t, :16, :], k2[t, 16:, :]], axis=1)
-        sent[432 + 32 * t : 464 + 32 * t, :] = k3[t]
+        sent2[16 * t : 16 * t + 16, :] = jnp.concatenate([k2[t, :16, :], k2[t, 16:, :]], axis=1)
+        sent3[32 * t : 32 * t + 32, :] = k3[t]
     both = jnp.concatenate([b2[...], b3[...]], axis=1)
-    sent[1296:1312, :] = jnp.broadcast_to(both, (16, 128))
+    sent2[432:448, :] = jnp.broadcast_to(both, (16, 128))
 
 
 def banded(k_ref):
@@ -138,7 +138,14 @@
     to_second[...] = mid[pl.ds(2 * odd, n)]
 
 
-def first_kernel(k1, k2, b1, w1a, w1c, v2a, v2c, bias):
+def first_kernel(far3, k1, k2, b1, w1a, w1c, v2a, v2c, bias, k3, order, same, sem):
+    copy = pltpu.make_async_copy(far3, k3, sem)
+    copy.start()
+    row = lax.broadcasted_iota(jnp.int32, order.shape, 0)
+    col = lax.broadcasted_iota(jnp.int32, order.shape, 1)
+    source = 32 * (row // 32) + 16 * (row % 2) + row % 32 // 2
+    order[...] = jnp.where(source == col, 1.0, 0.0).astype(BF)
+    same[...] = jnp.where(row == col, 1.0, 0.0).astype(BF)
     one = banded(lambda t: k1[t])
     two = banded(lambda t: k2[t])
     zero = jnp.zeros((64, 128), BF)
@@ -158,6 +165,7 @@
             v2c[0:64, lanes] = c
             v2c[64:128, lanes] = d
     bias[...] = jnp.broadcast_to(jnp.concatenate([b1[...].astype(F32)] * 4, axis=1), bias.shape)
+    copy.wait()
 
 
 def shifted(x, by):
@@ -297,12 +305,8 @@
         pd[dw] = shifted(pooled, dw - 1).astype(BF)
 
 
-def two_kernel(pd, v2a, v2c, k3, over, beside, b2, b3, skips, out, w2a, w2c, hd):
+def second_kernel(v2a, v2c, over, beside, b2, b3, w2a, w2c, bias2, bias3):
     half, core = lax.axis_index("filt"), lax.axis_index("slab") % 2
-    lane = lax.broadcasted_iota(jnp.int32, (1, 128), 1)
-    left = lane < 64
-    out[:, 0:32, :] = skips[...]
-
     mine, other = half * 64, 64 - half * 64
     for row in range(2):
         w2a[pl.ds(aligned(128 * row + mine, 64), 64), :] = v2a[64 * row : 64 * row + 64, :]
@@ -323,15 +327,19 @@
             w2a[pl.ds(aligned(128 + at, 32), 32), lanes] = b
             w2c[pl.ds(aligned(at, 32), 32), lanes] = c
             w2c[pl.ds(aligned(128 + at, 32), 32), lanes] = d
-    theirs = over[1296:1297, :].astype(F32)
+    theirs = over[432:433, :].astype(F32)
     here2, here3 = b2[...].astype(F32), b3[...].astype(F32)
     there2, there3 = theirs[:, :64], theirs[:, 64:]
     low = jnp.where(half == 0, here2, there2)
     high = jnp.where(half == 0, there2, here2)
-    bias2 = jnp.concatenate([low, high], axis=1)
+    bias2[...] = jnp.broadcast_to(jnp.concatenate([low, high], axis=1), bias2.shape)
     turned = jnp.concatenate([there3[:, 32:], there3[:, :32]], axis=1)
-    bias3 = jnp.concatenate([here3, jnp.where(core == 1, turned, there3)], axis=1)
-
+    order3 = jnp.concatenate([here3, jnp.where(core == 1, turned, there3)], axis=1)
+    bias3[...] = jnp.broadcast_to(order3, bias3.shape)
+
+
+def two_kernel(pd, w2a, w2c, b2, hd):
+    left = lax.broadcasted_iota(jnp.int32, (1, 128), 1) < 64
     m = (LAYER + 2) * FRAME
     pairs = pair(
         [jnp.concatenate(lanes_of(pd, m, 128 * a, 128 * a + 128), axis=1) for a in range(2)],
@@ -348,15 +356,21 @@
         ],
         axis=1,
     )
-    bias = jnp.concatenate([bias2] * 4, axis=1)
+    bias = jnp.concatenate([b2[0:1, :]] * 4, axis=1)
     hidden = jnp.where(inside(-1, LAYER + 2), jnp.maximum(hidden + bias, 0.0), 0.0).astype(BF).astype(F32)
     for dw in range(3):
         hd[dw] = shifted(hidden, dw - 1).astype(BF)
 
+
+def three_kernel(hd, k3, over, beside, b3, skips, out):
+    half, core = lax.axis_index("filt"), lax.axis_index("slab") % 2
+    lane = lax.broadcasted_iota(jnp.int32, (1, 128), 1)
+    left = lane < 64
+    out[:, 0:32, :] = skips[...]
     m = LAYER * FRAME
 
     def third(t):
-        rows = slice(432 + 32 * t, 464 + 32 * t)
+        rows = slice(32 * t, 32 * t + 32)
         return jnp.concatenate([k3[t], over[rows, :], beside[rows, :]], axis=0)
 
     none = jnp.zeros((128, 128), BF)
@@ -376,7 +390,7 @@
     mixed = dot(jnp.concatenate(lanes_of(hd, m, 128, 384), axis=1), w3c, NT)
     t0, t1 = both[:m, :128], both[:m, 128:] + mixed[:, :128]
     t2, t3 = both[m:, :128] + mixed[:, 128:], both[m:, 128:]
-    t0, t1, t2, t3 = (jnp.maximum(t + bias3, 0.0) for t in (t0, t1, t2, t3))
+    t0, t1, t2, t3 = (jnp.maximum(t + b3[0:1, :], 0.0) for t in (t0, t1, t2, t3))
     r0, r1, r2, r3 = (pltpu.roll(t, 64, 1) for t in (t0, t1, t2, t3))
     first = jnp.concatenate([jnp.where(left, t0, r1), jnp.where(left, t2, r3)], axis=1)
     second = jnp.concatenate([jnp.where(left, r0, t1), jnp.where(left, r2, t3)], axis=1)
@@ -389,32 +403,28 @@
         out[2 * s + 1 - half, 32:48, :] = second[top : top + 16, :].astype(BF)
 
 
-def unpack_kernel(got, skip, features):
+def unpack_kernel(got, order, same, skip, features):
     count = got.shape[0]
     ones = got[:, 0:32, :].reshape(count * 32, 256)
     twos = got[:, 32:48, :].reshape(count * 16, 256)
-    row = lax.broadcasted_iota(jnp.int32, (256, 256), 0)
-    col = lax.broadcasted_iota(jnp.int32, (256, 256), 1)
-    source = 32 * (row // 32) + 16 * (row % 2) + row % 32 // 2
-    order = jnp.where(source == col, 1.0, 0.0).astype(BF)
-    same = jnp.where(row == col, 1.0, 0.0).astype(BF)
-    by_column = dot(order, ones, NN).astype(BF)
-    skip[...] = dot(same, by_column, NT).astype(BF)
-    features[...] = dot(same, twos, NT).astype(BF)
+    by_column = dot(order[...], ones, NN).astype(BF)
+    skip[...] = dot(same[...], by_column, NT).astype(BF)
+    features[...] = dot(same[...], twos, NT).astype(BF)
 
 
 def shape(*dims):
     return jax.ShapeDtypeStruct(dims, BF)
 
 
-def call(kernel, outs, *operands, scratch=(), limit=8, far=False):
+def call(kernel, outs, *operands, scratch=(), limit=8, far=0):
     spec = pl.BlockSpec(memory_space=pltpu.VMEM)
-    if far:
-        operands = [pltpu.with_memory_space_constraint(x, pltpu.HBM) for x in operands]
+    hbm = pl.BlockSpec(memory_space=pltpu.HBM)
+    there = [pltpu.with_memory_space_constraint(x, pltpu.HBM) for x in operands[:far]]
+    operands = [*there, *operands[far:]]
     return pl.pallas_call(
         kernel,
         out_shape=outs,
-        in_specs=[pl.BlockSpec(memory_space=pltpu.HBM) if far else spec] * len(operands),
+        in_specs=[hbm] * far + [spec] * (len(operands) - far),
         out_specs=jax.tree.map(lambda _: spec, outs),
         scratch_shapes=scratch,
         compiler_params=pltpu.CompilerParams(vmem_limit_bytes=limit << 20),
@@ -453,12 +463,14 @@
         b2,
         b3,
         scratch=[pltpu.VMEM((256, 256), BF), pltpu.SemaphoreType.DMA((5,))],
-        far=True,
+        far=5,
     )
     mid = exchange(blocks)
-    sent = call(send_kernel, pltpu.VMEM((1312, 128), BF), *map(near, mine))
-    over = lax.ppermute(sent, "filt", [(0, 1), (1, 0)])
-    w1a, w1c, v2a, v2c, bias1 = call(
+    halves_sent = (pltpu.VMEM((448, 128), BF), pltpu.VMEM((864, 128), BF))
+    sent2, sent3 = call(send_kernel, halves_sent, *map(near, mine))
+    over2 = lax.ppermute(sent2, "filt", [(0, 1), (1, 0)])
+    over3 = lax.ppermute(sent3, "filt", [(0, 1), (1, 0)])
+    w1a, w1c, v2a, v2c, bias1, k3, order, same = call(
         first_kernel,
         (
             pltpu.VMEM((256, 2304), BF),
@@ -466,10 +478,16 @@
             pltpu.VMEM((128, 1152), BF),
             pltpu.VMEM((128, 1152), BF),
             pltpu.VMEM((8, 256), F32),
+            pltpu.VMEM(kernel_three.shape, BF),
+            pltpu.VMEM((256, 256), BF),
+            pltpu.VMEM((256, 256), BF),
         ),
+        kernel_three,
         kernel_one,
         kernel_two,
         b1,
+        scratch=[pltpu.SemaphoreType.DMA],
+        far=1,
     )
     planes = pltpu.VMEM((2 * (LAYER - 1), 2 * RUN, 256), BF)
     to_first, to_second = call(rim_kernel, (planes, planes), near(mid))
@@ -481,7 +499,19 @@
 
     rim_a = lax.ppermute(to_first, "slab", swaps(0))
     rim_b = lax.ppermute(to_second, "slab", swaps(1))
-    beside = lax.ppermute(over, "slab", [(i, i ^ 1) for i in range(slabs)])
+    other_core = [(i, i ^ 1) for i in range(slabs)]
+    beside2 = lax.ppermute(over2, "slab", other_core)
+    beside3 = lax.ppermute(over3, "slab", other_core)
+    w2a, w2c, bias2, bias3 = call(
+        second_kernel,
+        (
+            pltpu.VMEM((256, 1152), BF),
+            pltpu.VMEM((256, 1152), BF),
+            pltpu.VMEM((8, 128), F32),
+            pltpu.VMEM((8, 128), F32),
+        ),
+        *map(near, (v2a, v2c, over2, beside2, b2, b3)),
+    )
 
     def space(planes):
         rows = FRAME * planes
@@ -501,19 +531,21 @@
         scratch=space(6),
         limit=24,
     )
+    hidden = call(
+        two_kernel,
+        pltpu.VMEM((3, FRAME * (LAYER + 2), 512), BF),
+        *map(near, (pooled, w2a, w2c, bias2)),
+        limit=24,
+    )
     out = call(
-        two_kernel,
+        three_kernel,
         pltpu.VMEM((peers, 48, 256), BF),
-        *map(near, (pooled, v2a, v2c, kernel_three, over, beside, b2, b3, skips)),
-        scratch=[
-            pltpu.VMEM((256, 1152), BF),
-            pltpu.VMEM((256, 1152), BF),
-            pltpu.VMEM((3, FRAME * (LAYER + 2), 512), BF),
-        ],
+        *map(near, (hidden, k3, over3, beside3, bias3, skips)),
         limit=24,
     )
     home = exchange(out)
-    skip, features = call(unpack_kernel, (shape(256, 256), shape(256, 128)), near(home))
+    outs = (shape(256, 256), shape(256, 128))
+    skip, features = call(unpack_kernel, outs, *map(near, (home, order, same)))
     return skip.reshape(volume.shape), features.reshape(1, 4, 64, 128)
 
 

time: 40.8 us -> 33.2 us (0.81)
  blocking collectives: 17.7 us -> 8.74 us
  waiting for transfers between devices: 11.2 us -> 4.83 us
  starting transfers between devices: 4.2 us -> 10.2 us
  Pallas kernels: 6.76 us -> 8.26 us
    all_to_all x1 -> x0, blocking collectives: 8.87 us -> none  [by_columns(): mid = exchange(blocks)]
    ppermute x2 -> x4, waiting for transfers between devices: 7.53 us -> 0.04 us  [the longest x1 0.03 us: by_columns(): over2 = lax.ppermute(sent2, 'filt', [(0, 1), (1, 0)])]
    all_to_all x0 -> x1, starting transfers between devices: none -> 4.25 us  [by_columns(): mid = exchange(blocks)]
    all_to_all x0 -> x1, waiting for transfers between devices: none -> 3.03 us  [by_columns(): mid = exchange(blocks)]
    ppermute x1, waiting for transfers between devices: 2.6 us -> 0.74 us  [by_columns(): rim_a = lax.ppermute(to_first, 'slab', swaps(0))]
    ppermute x2 -> x4, starting transfers between devices: 2.83 us -> 4.61 us  [the longest x1 1.36 us: by_columns(): over2 = lax.ppermute(sent2, 'filt', [(0, 1), (1, 0)])]
    pallas_call x8 -> x10, Pallas kernels: 6.76 us -> 8.26 us  [call(): pl.pallas_call(kernel, out_shape=outs, in_specs=[hbm] * far + [spec] * (l...]
  transfers between devices with their start and end apart: 4 -> 7, of which waited for: 3 -> 3; matrix products, arithmetic and copies ran while one was open for 0% -> 0% of each run, Pallas kernels for 6% -> 13%
where the time goes in v6:
time: 33.2 us; the launch traced here: 32.8 us
  starting transfers between devices  10.2 us (31%)
  blocking collectives  8.74 us (26%)
  Pallas kernels  8.26 us (25%)
  waiting for transfers between devices  4.83 us (15%)
  between operations  0.76 us (2%)
    all_to_all x1, blocking collectives, by_columns(): home = exchange(out)  8.74 us
    pallas_call x10, Pallas kernels, call(): pl.pallas_call(kernel, out_shape=outs, in_specs=[hbm] * far + [spec] * (l...  8.26 us
    all_to_all x1, starting transfers between devices, by_columns(): mid = exchange(blocks)  4.25 us
    all_to_all x1, waiting for transfers between devices, by_columns(): mid = exchange(blocks)  3.03 us
    ppermute x1, starting transfers between devices, by_columns(): rim_a = lax.ppermute(to_first, 'slab', swaps(0))  1.36 us
    ppermute x1, starting transfers between devices, by_columns(): over2 = lax.ppermute(sent2, 'filt', [(0, 1), (1, 0)])  1.36 us
    ppermute x1, starting transfers between devices, by_columns(): over3 = lax.ppermute(sent3, 'filt', [(0, 1), (1, 0)])  1.3 us
    ppermute x1, waiting for transfers between devices, by_columns(): rim_b = lax.ppermute(to_second, 'slab', swaps(1))  1.02 us
  transfers between devices with their start and end apart: 7, of which 3 were waited for; matrix products, arithmetic and copies ran while one was open for 0% of the time, Pallas kernels for 13%

profile of v6, /device:TPU:17, one launch (start us, length us, event | category | flops | bytes accessed | tf_op | source)
XLA Modules:
  0.0 32.8 jit_solution(5146834240822430031)
XLA Ops:
  0.6 0.0 copy-start
  0.6 0.0 copy-start.1
  0.7 0.0 copy-start.4
  0.7 2.0 %shard_map.86 = (bf16[8,48,256]{2,1,0:T(8,128)(2,1)}, bf16[27,32,64]{2,1,0:T(8,128)(2,1)S(1)}, bf16[27,32,128]{2,1,0:T(8,128)(2,1)S(1)}, bf16[1,64]{1,0:T(2,128)(2,1)S(1)}, bf16[1,64]{1,0:T(2,128)(2,1)S(1)}) custom-call(bf16[256,256]{1,0:T(8,128)(2,1)} %bitcast.11, bf16[27,64,64]{2,1,0:T(8,128)(2,1)} %k2.1, bf16[27,64,128]{2,1,0:T(8,128)(2,1)} %far3.3, ...), custom_call_target="tpu_custom_call" | custom-call | tf_op jit(solution)/shard_map/pallas_call | solution.py:424
  2.6 0.1 shard_map.91
  2.7 1.3 %collective-permute-start.4 = (bf16[864,128]{1,0:T(8,128)(2,1)S(1)}, bf16[864,128]{1,0:T(8,128)(2,1)S(1)}, u32[]{:S(2)}, u32[]{:S(2)}) collective-permute-start(bf16[864,128]{1,0:T(8,128)(2,1)S(1)} %get-tuple-element.45), channel_id=1, source_target_pairs={{0,1},{1,0},{2,3},{3,2},{4,5},{5,4},{6,7},{7,6},{8,9},{9,8},{10,11... | collective-permute-start | bytes 663560 | tf_op jit(solution)/shard_map/ppermute | solution.py:472
  4.0 4.3 %all-to-all-start = ((bf16[8,48,256]{2,1,0:T(8,128)(2,1)}), bf16[8,48,256]{2,1,0:T(8,128)(2,1)S(1)}, u32[]{:S(2)}, u32[]{:S(2)}) async-start(bf16[8,48,256]{2,1,0:T(8,128)(2,1)} %get-tuple-element.27), calls=%async_computation | async-start | bytes 393216 | tf_op jit(solution)/shard_map/all_to_all | solution.py:468
  8.3 1.4 %collective-permute-start.2 = (bf16[448,128]{1,0:T(8,128)(2,1)S(1)}, bf16[448,128]{1,0:T(8,128)(2,1)S(1)}, u32[]{:S(2)}, u32[]{:S(2)}) collective-permute-start(bf16[448,128]{1,0:T(8,128)(2,1)S(1)} %get-tuple-element.40), channel_id=1, source_target_pairs={{0,1},{1,0},{2,3},{3,2},{4,5},{5,4},{6,7},{7,6},{8,9},{9,8},{10,11... | collective-permute-start | bytes 344072 | tf_op jit(solution)/shard_map/ppermute | solution.py:471
  9.6 0.0 collective-permute-done.4.over
  9.6 1.0 %collective-permute-start.5 = (bf16[864,128]{1,0:T(8,128)(2,1)S(1)}, bf16[864,128]{1,0:T(8,128)(2,1)S(1)}, u32[]{:S(2)}, u32[]{:S(2)}) collective-permute-start(bf16[864,128]{1,0:T(8,128)(2,1)S(1)} %collective-permute-done.4.over), channel_id=1, source_target_pairs={{0,2},{2,0},{4,6},{6,4},{8,10},{10,8},{12,14},{14,12},{16,18},{18,... | collective-permute-start | bytes 663560 | tf_op jit(solution)/shard_map/ppermute | solution.py:504
  10.6 3.0 %all-to-all-done.mid = bf16[8,48,256]{2,1,0:T(8,128)(2,1)S(1)} async-done(((bf16[8,48,256]{2,1,0:T(8,128)(2,1)}), bf16[8,48,256]{2,1,0:T(8,128)(2,1)S(1)}, u32[]{:S(2)}, u32[]{:S(2)}) %all-to-all-start) | async-done | bytes 196640 | tf_op jit(solution)/shard_map/all_to_all | solution.py:468
  13.7 1.4 %collective-permute-start = (bf16[6,48,256]{2,1,0:T(8,128)(2,1)S(1)}, bf16[6,48,256]{2,1,0:T(8,128)(2,1)S(1)}, u32[]{:S(2)}, u32[]{:S(2)}) collective-permute-start(bf16[6,48,256]{2,1,0:T(8,128)(2,1)S(1)} %get-tuple-element.28), channel_id=1, source_target_pairs={{0,8},{2,10},{4,12},{6,14},{8,0},{10,2},{12,4},{14,6},{16,24},{18,... | collective-permute-start | bytes 442376 | tf_op jit(solution)/shard_map/ppermute | solution.py:500
  15.0 0.0 collective-permute-start.1
  15.1 0.0 collective-permute-done.2.over
  15.1 1.0 %collective-permute-start.3 = (bf16[448,128]{1,0:T(8,128)(2,1)S(1)}, bf16[448,128]{1,0:T(8,128)(2,1)S(1)}, u32[]{:S(2)}, u32[]{:S(2)}) collective-permute-start(bf16[448,128]{1,0:T(8,128)(2,1)S(1)} %collective-permute-done.2.over), channel_id=1, source_target_pairs={{0,2},{2,0},{4,6},{6,4},{8,10},{10,8},{12,14},{14,12},{16,18},{18,... | collective-permute-start | bytes 344072 | tf_op jit(solution)/shard_map/ppermute | solution.py:503
  16.0 0.0 copy-done
  16.0 0.0 copy-done.1
  16.1 0.0 copy-done.4
  16.1 1.0 %shard_map.88 = (bf16[256,2304]{1,0:T(8,128)(2,1)S(1)}, bf16[128,1152]{1,0:T(8,128)(2,1)S(1)}, bf16[128,1152]{1,0:T(8,128)(2,1)S(1)}, bf16[128,1152]{1,0:T(8,128...) custom-call(bf16[27,64,128]{2,1,0:T(8,128)(2,1)} %far3.3, ...), custom_call_target="tpu_custom_call" | custom-call | tf_op jit(solution)/shard_map/pallas_call | solution.py:424
  17.1 0.0 copy-start.2
  17.1 0.0 copy-start.3
  17.1 1.1 %shard_map.89.acc = f32[2,2,144,256]{3,2,1,0:T(8,128)S(1)} custom-call(bf16[8,48,256]{2,1,0:T(8,128)(2,1)S(1)} %all-to-all-done.mid, bf16[256,2304]{1,0:T(8,128)(2,1)S(1)} %get-tuple-element.30.w1a, bf16[128,1152]{1,0:T(8,128)(2,1)S(1)} %get-tuple-element.31.w1c), custom_call_target="tpu_custom_call" | custom-call | tf_op jit(solution)/shard_map/pallas_call | solution.py:424
  18.2 0.0 collective-permute-done.3.beside
  18.2 0.0 copy-done.2
  18.2 0.0 copy-done.3
  18.2 0.2 shard_map.92
  18.5 0.7 %collective-permute-done.rim_a = bf16[6,48,256]{2,1,0:T(8,128)(2,1)S(1)} collective-permute-done((bf16[6,48,256]{2,1,0:T(8,128)(2,1)S(1)}, bf16[6,48,256]{2,1,0:T(8,128)(2,1)S(1)}, u32[]{:S(2)}, u32[]{:S(2)}) %collective-permute-start) | collective-permute-done | bytes 147488 | tf_op jit(solution)/shard_map/ppermute | solution.py:500
  19.2 1.0 %collective-permute-done.1.rim_b = bf16[6,48,256]{2,1,0:T(8,128)(2,1)S(1)} collective-permute-done((bf16[6,48,256]{2,1,0:T(8,128)(2,1)S(1)}, bf16[6,48,256]{2,1,0:T(8,128)(2,1)S(1)}, u32[]{:S(2)}, u32[]{:S(2)}) %collective-permute-start.1) | collective-permute-done | bytes 147488 | tf_op jit(solution)/shard_map/ppermute | solution.py:501
  20.2 1.2 %shard_map.90 = (bf16[8,32,256]{2,1,0:T(8,128)(2,1)S(1)}, bf16[3,192,256]{2,1,0:T(8,128)(2,1)S(1)}) custom-call(bf16[6,48,256]{2,1,0:T(8,128)(2,1)S(1)} %collective-permute-done.rim_a, bf16[6,48,256]{2,1,0:T(8,128)(2,1)S(1)} %collective-permute-done.1.rim_b, bf16[256,2304]{1,0:T(8,128)(2,1)S(1)} %get-tuple-element.30.w1a, ...), custom_call_target="tpu_custom_call" | custom-call | tf_op jit(solution)/shard_map/pallas_call | solution.py:424
  21.4 0.6 %shard_map.93.hd = bf16[3,144,512]{2,1,0:T(8,128)(2,1)S(1)} custom-call(bf16[3,192,256]{2,1,0:T(8,128)(2,1)S(1)} %get-tuple-element.33.pd, bf16[256,1152]{1,0:T(8,128)(2,1)S(1)} %get-tuple-element.41.w2a, bf16[256,1152]{1,0:T(8,128)(2,1)S(1)} %get-tuple-element.42.w2c, f32[8,128]{1,0:T(8,128)S(1)} %get-tuple-element.43.b2), custom_call_target="tpu_custom_call" | custom-call | tf_op jit(solution)/shard_map/pallas_call | solution.py:424
  22.0 0.0 collective-permute-done.5.beside
  22.0 1.0 %shard_map.94 = bf16[8,48,256]{2,1,0:T(8,128)(2,1)S(1)} custom-call(bf16[3,144,512]{2,1,0:T(8,128)(2,1)S(1)} %shard_map.93.hd, bf16[27,64,128]{2,1,0:T(8,128)(2,1)S(1)} %get-tuple-element.44.k3, bf16[864,128]{1,0:T(8,128)(2,1)S(1)} %collective-permute-done.4.over, bf16[864,128]{1,0:T(8,128)(2,1)S(1)} %collective-permute-done.5.beside, ...), custom_call_target="tpu_custom_call" | custom-call | tf_op jit(solution)/shard_map/pallas_call | solution.py:424
  23.0 8.7 %all_to_all.10.got = bf16[8,48,256]{2,1,0:T(8,128)(2,1)S(1)} all-to-all(bf16[8,48,256]{2,1,0:T(8,128)(2,1)S(1)} %shard_map.94), channel_id=1, replica_groups={{0,1,2,3,4,5,6,7},{8,9,10,11,12,13,14,15},{16,17,18,19,20,21,22,23},{24..., dimensions={0} | all-to-all | bytes 393216 | tf_op jit(solution)/shard_map/all_to_all | solution.py:546
  31.8 1.1 %shard_map.95 = (bf16[256,256]{1,0:T(8,128)(2,1)}, bf16[256,128]{1,0:T(8,128)(2,1)}) custom-call(bf16[8,48,256]{2,1,0:T(8,128)(2,1)S(1)} %all_to_all.10.got, bf16[256,256]{1,0:T(8,128)(2,1)S(1)} %get-tuple-element.48.order, bf16[256,256]{1,0:T(8,128)(2,1)S(1)} %get-tuple-element.49.same), custom_call_target="tpu_custom_call" | custom-call | tf_op jit(solution)/shard_map/pallas_call | solution.py:424
  (1 shorter events, 0.0 us)
Async XLA Ops:
  0.6 15.4 %copy-start = (bf16[27,64,64]{2,1,0:T(8,128)(2,1)S(1)}, bf16[27,64,64]{2,1,0:T(8,128)(2,1)}, u32[]{:S(2)}) copy-start(bf16[27,64,64]{2,1,0:T(8,128)(2,1)} %k2.1) | copy-start | bytes 663556
  0.6 15.4 %copy-start.1 = (bf16[27,64,64]{2,1,0:T(8,128)(2,1)S(1)}, bf16[27,64,64]{2,1,0:T(8,128)(2,1)}, u32[]{:S(2)}) copy-start(bf16[27,64,64]{2,1,0:T(8,128)(2,1)} %k1.1) | copy-start | bytes 663556
  0.7 15.4 %copy-start.4 = (bf16[64]{0:T(256)(128)(2,1)S(1)}, bf16[64]{0:T(256)(128)(2,1)}, u32[]{:S(2)}) copy-start(bf16[64]{0:T(256)(128)(2,1)} %param.9) | copy-start | bytes 388
  2.7 6.9 %collective-permute-start.4 = (bf16[864,128]{1,0:T(8,128)(2,1)S(1)}, bf16[864,128]{1,0:T(8,128)(2,1)S(1)}, u32[]{:S(2)}, u32[]{:S(2)}) collective-permute-start(bf16[864,128]{1,0:T(8,128)(2,1)S(1)} %get-tuple-element.45), channel_id=1, source_target_pairs={{0,1},{1,0},{2,3},{3,2},{4,5},{5,4},{6,7},{7,6},{8,9},{9,8},{10,11... | collective-permute-start | bytes 663560 | tf_op jit(solution)/shard_map/ppermute | solution.py:472
  4.0 9.6 %all-to-all-start = ((bf16[8,48,256]{2,1,0:T(8,128)(2,1)}), bf16[8,48,256]{2,1,0:T(8,128)(2,1)S(1)}, u32[]{:S(2)}, u32[]{:S(2)}) async-start(bf16[8,48,256]{2,1,0:T(8,128)(2,1)} %get-tuple-element.27), calls=%async_computation | async-start | bytes 393216 | tf_op jit(solution)/shard_map/all_to_all | solution.py:468
  8.3 6.8 %collective-permute-start.2 = (bf16[448,128]{1,0:T(8,128)(2,1)S(1)}, bf16[448,128]{1,0:T(8,128)(2,1)S(1)}, u32[]{:S(2)}, u32[]{:S(2)}) collective-permute-start(bf16[448,128]{1,0:T(8,128)(2,1)S(1)} %get-tuple-element.40), channel_id=1, source_target_pairs={{0,1},{1,0},{2,3},{3,2},{4,5},{5,4},{6,7},{7,6},{8,9},{9,8},{10,11... | collective-permute-start | bytes 344072 | tf_op jit(solution)/shard_map/ppermute | solution.py:471
  9.6 12.3 %collective-permute-start.5 = (bf16[864,128]{1,0:T(8,128)(2,1)S(1)}, bf16[864,128]{1,0:T(8,128)(2,1)S(1)}, u32[]{:S(2)}, u32[]{:S(2)}) collective-permute-start(bf16[864,128]{1,0:T(8,128)(2,1)S(1)} %collective-permute-done.4.over), channel_id=1, source_target_pairs={{0,2},{2,0},{4,6},{6,4},{8,10},{10,8},{12,14},{14,12},{16,18},{18,... | collective-permute-start | bytes 663560 | tf_op jit(solution)/shard_map/ppermute | solution.py:504
  13.7 5.5 %collective-permute-start = (bf16[6,48,256]{2,1,0:T(8,128)(2,1)S(1)}, bf16[6,48,256]{2,1,0:T(8,128)(2,1)S(1)}, u32[]{:S(2)}, u32[]{:S(2)}) collective-permute-start(bf16[6,48,256]{2,1,0:T(8,128)(2,1)S(1)} %get-tuple-element.28), channel_id=1, source_target_pairs={{0,8},{2,10},{4,12},{6,14},{8,0},{10,2},{12,4},{14,6},{16,24},{18,... | collective-permute-start | bytes 442376 | tf_op jit(solution)/shard_map/ppermute | solution.py:500
  15.0 5.2 %collective-permute-start.1 = (bf16[6,48,256]{2,1,0:T(8,128)(2,1)S(1)}, bf16[6,48,256]{2,1,0:T(8,128)(2,1)S(1)}, u32[]{:S(2)}, u32[]{:S(2)}) collective-permute-start(bf16[6,48,256]{2,1,0:T(8,128)(2,1)S(1)} %get-tuple-element.29), channel_id=1, source_target_pairs={{0,2},{2,0},{4,6},{6,4},{8,16},{10,18},{12,20},{14,22},{16,8},{18,... | collective-permute-start | bytes 442376 | tf_op jit(solution)/shard_map/ppermute | solution.py:501
  15.1 3.1 %collective-permute-start.3 = (bf16[448,128]{1,0:T(8,128)(2,1)S(1)}, bf16[448,128]{1,0:T(8,128)(2,1)S(1)}, u32[]{:S(2)}, u32[]{:S(2)}) collective-permute-start(bf16[448,128]{1,0:T(8,128)(2,1)S(1)} %collective-permute-done.2.over), channel_id=1, source_target_pairs={{0,2},{2,0},{4,6},{6,4},{8,10},{10,8},{12,14},{14,12},{16,18},{18,... | collective-permute-start | bytes 344072 | tf_op jit(solution)/shard_map/ppermute | solution.py:503
  17.1 1.1 %copy-start.2 = (bf16[64]{0:T(256)(128)(2,1)S(1)}, bf16[64]{0:T(256)(128)(2,1)}, u32[]{:S(2)}) copy-start(bf16[64]{0:T(256)(128)(2,1)} %param.11) | copy-start | bytes 388
  17.1 1.1 %copy-start.3 = (bf16[64]{0:T(256)(128)(2,1)S(1)}, bf16[64]{0:T(256)(128)(2,1)}, u32[]{:S(2)}) copy-start(bf16[64]{0:T(256)(128)(2,1)} %param.13) | copy-start | bytes 388

commit v7 on v6

--- a/solution.py
+++ b/solution.py
@@ -89,7 +89,7 @@
     pairs = (
         (far, volume),
         (far2.at[:, half, :], k2),
-        (far3.at[:, half, :], k3),
+        (far3, k3),
         (far_b2, b2),
         (far_b3, b3),
     )
@@ -114,9 +114,10 @@
 
 
 def send_kernel(k2, k3, b2, b3, sent2, sent3):
+    half = pl.ds(aligned(32 * (lax.axis_index("slab") % 2), 32), 32)
     for t in range(27):
         sent2[16 * t : 16 * t + 16, :] = jnp.concatenate([k2[t, :16, :], k2[t, 16:, :]], axis=1)
-        sent3[32 * t : 32 * t + 32, :] = k3[t]
+        sent3[32 * t : 32 * t + 32, :] = k3[t, half, :]
     both = jnp.concatenate([b2[...], b3[...]], axis=1)
     sent2[432:448, :] = jnp.broadcast_to(both, (16, 128))
 
@@ -138,9 +139,7 @@
     to_second[...] = mid[pl.ds(2 * odd, n)]
 
 
-def first_kernel(far3, k1, k2, b1, w1a, w1c, v2a, v2c, bias, k3, order, same, sem):
-    copy = pltpu.make_async_copy(far3, k3, sem)
-    copy.start()
+def first_kernel(k1, k2, b1, w1a, w1c, v2a, v2c, bias, order, same):
     row = lax.broadcasted_iota(jnp.int32, order.shape, 0)
     col = lax.broadcasted_iota(jnp.int32, order.shape, 1)
     source = 32 * (row // 32) + 16 * (row % 2) + row % 32 // 2
@@ -165,7 +164,6 @@
             v2c[0:64, lanes] = c
             v2c[64:128, lanes] = d
     bias[...] = jnp.broadcast_to(jnp.concatenate([b1[...].astype(F32)] * 4, axis=1), bias.shape)
-    copy.wait()
 
 
 def shifted(x, by):
@@ -221,9 +219,15 @@
             return jnp.concatenate([ref[par + dw, rows, :] for dw in range(3)], axis=1)
 
         cross = pair([pick(x34, par) for par in range(2)], w1c[:, 384 * dp : 384 * dp + 384])
+        weights = w1a[:, 768 * dp : 768 * dp + 768]
+        parts = [pick(q.at[f], par) for f in range(2) for par in range(2)]
+        if dp < 2:
+            together = pair(parts, weights)
+        else:
+            together = pair(parts[:2], weights) + pair(parts[2:], weights)
         sums = []
         for f in range(2):
-            ys = pair([pick(q.at[f], par) for par in range(2)], w1a[:, 768 * dp : 768 * dp + 768])
+            ys = together[2 * f : 2 * f + 2]
             for par in range(2):
                 low, high = ys[par][:, :128], ys[par][:, 128:]
                 if f == 0:
@@ -258,10 +262,9 @@
                 acc[f, par, FRAME * e : FRAME * e + FRAME, :] = add(terms)
 
 
-def one_kernel(rim_a, rim_b, w1a, w1c, b1, acc, skips, pd, q, x34):
+def halo_kernel(rim_a, rim_b, q, x34):
     layer, layers = lax.axis_index("slab") // LAYER, lax.axis_size("slab") // LAYER
     odd = layer % 2 == 1
-    left = lax.broadcasted_iota(jnp.int32, (1, 128), 1) < 64
 
     def run(v, f, rows):
         at = 2 * (v % 3) + f
@@ -270,6 +273,10 @@
         return jnp.where(outside, jnp.zeros_like(got), got)
 
     spread_runs(run, range(6), q, x34)
+
+
+def one_kernel(q, x34, w1a, w1c, b1, acc, skips, pd):
+    left = lax.broadcasted_iota(jnp.int32, (1, 128), 1) < 64
     sums = products(q, x34, w1a, w1c, 1)
     u = LAYER + 4
     targets = ((0, 1, 2, u - 1), (0, 1, u - 2, u - 1), (0, u - 3, u - 2, u - 1))
@@ -373,23 +380,23 @@
         rows = slice(32 * t, 32 * t + 32)
         return jnp.concatenate([k3[t], over[rows, :], beside[rows, :]], axis=0)
 
-    none = jnp.zeros((128, 128), BF)
-    straight, across = [[], []], [[], []]
+    straight, low, high = [[], []], [], []
     for dp, dw in TAPS:
         k0, k1, k2 = (third(9 * dp + 3 * dr + dw) for dr in range(3))
         straight[0] += [k1, k2]
         straight[1] += [k0, k1]
-        across[0] += [none, k2]
-        across[1] += [k0, none]
+        low.append(k0)
+        high.append(k2)
     w3a = jnp.concatenate([jnp.concatenate(rows, axis=1) for rows in straight], axis=0)
-    w3c = jnp.concatenate([jnp.concatenate(rows, axis=1) for rows in across], axis=0)
     both = jnp.concatenate(
         [jnp.concatenate(lanes_of(hd, m, 256 * a, 256 * a + 256), axis=1) for a in range(2)], axis=0
     )
     both = dot(both, w3a, NT)
-    mixed = dot(jnp.concatenate(lanes_of(hd, m, 128, 384), axis=1), w3c, NT)
-    t0, t1 = both[:m, :128], both[:m, 128:] + mixed[:, :128]
-    t2, t3 = both[m:, :128] + mixed[:, 128:], both[m:, 128:]
+    cat = lambda parts: jnp.concatenate(parts, axis=1)
+    up = dot(cat(lanes_of(hd, m, 256, 384)), cat(high), NT)
+    down = dot(cat(lanes_of(hd, m, 128, 256)), cat(low), NT)
+    t0, t1 = both[:m, :128], both[:m, 128:] + up
+    t2, t3 = both[m:, :128] + down, both[m:, 128:]
     t0, t1, t2, t3 = (jnp.maximum(t + b3[0:1, :], 0.0) for t in (t0, t1, t2, t3))
     r0, r1, r2, r3 = (pltpu.roll(t, 64, 1) for t in (t0, t1, t2, t3))
     first = jnp.concatenate([jnp.where(left, t0, r1), jnp.where(left, t2, r3)], axis=1)
@@ -453,7 +460,7 @@
         (
             pltpu.VMEM((peers, 2 * RUN, 256), BF),
             pltpu.VMEM((27, 32, 64), BF),
-            pltpu.VMEM((27, 32, 128), BF),
+            pltpu.VMEM(kernel_three.shape, BF),
             pltpu.VMEM((1, 64), BF),
             pltpu.VMEM((1, 64), BF),
         ),
@@ -470,7 +477,7 @@
     sent2, sent3 = call(send_kernel, halves_sent, *map(near, mine))
     over2 = lax.ppermute(sent2, "filt", [(0, 1), (1, 0)])
     over3 = lax.ppermute(sent3, "filt", [(0, 1), (1, 0)])
-    w1a, w1c, v2a, v2c, bias1, k3, order, same = call(
+    w1a, w1c, v2a, v2c, bias1, order, same = call(
         first_kernel,
         (
             pltpu.VMEM((256, 2304), BF),
@@ -478,16 +485,12 @@
             pltpu.VMEM((128, 1152), BF),
             pltpu.VMEM((128, 1152), BF),
             pltpu.VMEM((8, 256), F32),
-            pltpu.VMEM(kernel_three.shape, BF),
             pltpu.VMEM((256, 256), BF),
             pltpu.VMEM((256, 256), BF),
         ),
-        kernel_three,
         kernel_one,
         kernel_two,
         b1,
-        scratch=[pltpu.SemaphoreType.DMA],
-        far=1,
     )
     planes = pltpu.VMEM((2 * (LAYER - 1), 2 * RUN, 256), BF)
     to_first, to_second = call(rim_kernel, (planes, planes), near(mid))
@@ -524,11 +527,11 @@
         scratch=space(LAYER),
         limit=24,
     )
+    halo = call(halo_kernel, tuple(space(6)), near(rim_a), near(rim_b), limit=24)
     skips, pooled = call(
         one_kernel,
         (pltpu.VMEM((peers, 32, 256), BF), pltpu.VMEM((3, FRAME * (LAYER + 4), 256), BF)),
-        *map(near, (rim_a, rim_b, w1a, w1c, bias1, acc)),
-        scratch=space(6),
+        *map(near, (*halo, w1a, w1c, bias1, acc)),
         limit=24,
     )
     hidden = call(
@@ -540,7 +543,7 @@
     out = call(
         three_kernel,
         pltpu.VMEM((peers, 48, 256), BF),
-        *map(near, (hidden, k3, over3, beside3, bias3, skips)),
+        *map(near, (hidden, mine[1], over3, beside3, bias3, skips)),
         limit=24,
     )
     home = exchange(out)

time: 33.2 us -> 32.9 us (level)
  Pallas kernels: 8.26 us -> 7.22 us
  waiting for transfers between devices: 4.83 us -> 5.62 us
    pallas_call x10 -> x11, Pallas kernels: 8.26 us -> 7.22 us  [call(): pl.pallas_call(kernel, out_shape=outs, in_specs=[hbm] * far + [spec] * (l...]
    ppermute x1, waiting for transfers between devices: 0.74 us -> 1.53 us  [by_columns(): rim_a = lax.ppermute(to_first, 'slab', swaps(0))]
  transfers between devices with their start and end apart: 7 -> 7, of which waited for: 3 -> 3; matrix products, arithmetic and copies ran while one was open for 0% -> 0% of each run, Pallas kernels for 13% -> 10%
where the time goes in v7:
time: 32.9 us; the launch traced here: 32.6 us
  starting transfers between devices  10.2 us (31%)
  blocking collectives  8.74 us (27%)
  Pallas kernels  7.22 us (22%)
  waiting for transfers between devices  5.62 us (17%)
  between operations  0.77 us (2%)
    all_to_all x1, blocking collectives, by_columns(): home = exchange(out)  8.74 us
    pallas_call x11, Pallas kernels, call(): pl.pallas_call(kernel, out_shape=outs, in_specs=[hbm] * far + [spec] * (l...  7.22 us
    all_to_all x1, starting transfers between devices, by_columns(): mid = exchange(blocks)  4.25 us
    all_to_all x1, waiting for transfers between devices, by_columns(): mid = exchange(blocks)  3.03 us
    ppermute x1, waiting for transfers between devices, by_columns(): rim_a = lax.ppermute(to_first, 'slab', swaps(0))  1.53 us
    ppermute x1, starting transfers between devices, by_columns(): rim_a = lax.ppermute(to_first, 'slab', swaps(0))  1.36 us
    ppermute x1, starting transfers between devices, by_columns(): over2 = lax.ppermute(sent2, 'filt', [(0, 1), (1, 0)])  1.36 us
    ppermute x1, starting transfers between devices, by_columns(): over3 = lax.ppermute(sent3, 'filt', [(0, 1), (1, 0)])  1.3 us
  transfers between devices with their start and end apart: 7, of which 3 were waited for; matrix products, arithmetic and copies ran while one was open for 0% of the time, Pallas kernels for 10%

profile of v7, /device:TPU:17, one launch (start us, length us, event | category | flops | bytes accessed | tf_op | source)
XLA Modules:
  0.0 32.6 jit_solution(4311241334458727127)
XLA Ops:
  0.6 0.0 copy-start
  0.6 0.0 copy-start.1
  0.7 0.0 copy-start.4
  0.7 2.0 %shard_map.86 = (bf16[8,48,256]{2,1,0:T(8,128)(2,1)}, bf16[27,32,64]{2,1,0:T(8,128)(2,1)S(1)}, bf16[27,64,128]{2,1,0:T(8,128)(2,1)S(1)}, bf16[1,64]{1,0:T(2,128)(2,1)S(1)}, bf16[1,64]{1,0:T(2,128)(2,1)S(1)}) custom-call(bf16[256,256]{1,0:T(8,128)(2,1)} %bitcast.11, bf16[27,64,64]{2,1,0:T(8,128)(2,1)} %k2.1, bf16[27,64,128]{2,1,0:T(8,128)(2,1)} %far3.1, ...), custom_call_target="tpu_custom_call" | custom-call | tf_op jit(solution)/shard_map/pallas_call | solution.py:431
  2.6 0.1 shard_map.92
  2.7 1.3 %collective-permute-start.4 = (bf16[864,128]{1,0:T(8,128)(2,1)S(1)}, bf16[864,128]{1,0:T(8,128)(2,1)S(1)}, u32[]{:S(2)}, u32[]{:S(2)}) collective-permute-start(bf16[864,128]{1,0:T(8,128)(2,1)S(1)} %get-tuple-element.47), channel_id=1, source_target_pairs={{0,1},{1,0},{2,3},{3,2},{4,5},{5,4},{6,7},{7,6},{8,9},{9,8},{10,11... | collective-permute-start | bytes 663560 | tf_op jit(solution)/shard_map/ppermute | solution.py:479
  4.0 4.3 %all-to-all-start = ((bf16[8,48,256]{2,1,0:T(8,128)(2,1)}), bf16[8,48,256]{2,1,0:T(8,128)(2,1)S(1)}, u32[]{:S(2)}, u32[]{:S(2)}) async-start(bf16[8,48,256]{2,1,0:T(8,128)(2,1)} %get-tuple-element.28), calls=%async_computation | async-start | bytes 393216 | tf_op jit(solution)/shard_map/all_to_all | solution.py:475
  8.3 1.4 %collective-permute-start.2 = (bf16[448,128]{1,0:T(8,128)(2,1)S(1)}, bf16[448,128]{1,0:T(8,128)(2,1)S(1)}, u32[]{:S(2)}, u32[]{:S(2)}) collective-permute-start(bf16[448,128]{1,0:T(8,128)(2,1)S(1)} %get-tuple-element.43), channel_id=1, source_target_pairs={{0,1},{1,0},{2,3},{3,2},{4,5},{5,4},{6,7},{7,6},{8,9},{9,8},{10,11... | collective-permute-start | bytes 344072 | tf_op jit(solution)/shard_map/ppermute | solution.py:478
  9.7 0.0 collective-permute-done.4.over
  9.7 1.0 %collective-permute-start.5 = (bf16[864,128]{1,0:T(8,128)(2,1)S(1)}, bf16[864,128]{1,0:T(8,128)(2,1)S(1)}, u32[]{:S(2)}, u32[]{:S(2)}) collective-permute-start(bf16[864,128]{1,0:T(8,128)(2,1)S(1)} %collective-permute-done.4.over), channel_id=1, source_target_pairs={{0,2},{2,0},{4,6},{6,4},{8,10},{10,8},{12,14},{14,12},{16,18},{18,... | collective-permute-start | bytes 663560 | tf_op jit(solution)/shard_map/ppermute | solution.py:507
  10.7 3.0 %all-to-all-done.mid = bf16[8,48,256]{2,1,0:T(8,128)(2,1)S(1)} async-done(((bf16[8,48,256]{2,1,0:T(8,128)(2,1)}), bf16[8,48,256]{2,1,0:T(8,128)(2,1)S(1)}, u32[]{:S(2)}, u32[]{:S(2)}) %all-to-all-start) | async-done | bytes 196640 | tf_op jit(solution)/shard_map/all_to_all | solution.py:475
  13.7 1.4 %collective-permute-start = (bf16[6,48,256]{2,1,0:T(8,128)(2,1)S(1)}, bf16[6,48,256]{2,1,0:T(8,128)(2,1)S(1)}, u32[]{:S(2)}, u32[]{:S(2)}) collective-permute-start(bf16[6,48,256]{2,1,0:T(8,128)(2,1)S(1)} %get-tuple-element.29), channel_id=1, source_target_pairs={{0,8},{2,10},{4,12},{6,14},{8,0},{10,2},{12,4},{14,6},{16,24},{18,... | collective-permute-start | bytes 442376 | tf_op jit(solution)/shard_map/ppermute | solution.py:503
  15.1 0.0 collective-permute-start.1
  15.1 0.0 collective-permute-done.2.over
  15.1 1.0 %collective-permute-start.3 = (bf16[448,128]{1,0:T(8,128)(2,1)S(1)}, bf16[448,128]{1,0:T(8,128)(2,1)S(1)}, u32[]{:S(2)}, u32[]{:S(2)}) collective-permute-start(bf16[448,128]{1,0:T(8,128)(2,1)S(1)} %collective-permute-done.2.over), channel_id=1, source_target_pairs={{0,2},{2,0},{4,6},{6,4},{8,10},{10,8},{12,14},{14,12},{16,18},{18,... | collective-permute-start | bytes 344072 | tf_op jit(solution)/shard_map/ppermute | solution.py:506
  16.1 0.0 copy-done
  16.1 0.0 copy-done.1
  16.1 0.0 copy-done.4
  16.1 0.4 %shard_map.89 = (bf16[256,2304]{1,0:T(8,128)(2,1)S(1)}, bf16[128,1152]{1,0:T(8,128)(2,1)S(1)}, bf16[128,1152]{1,0:T(8,128)(2,1)S(1)}, bf16[128,1152]{1,0:T(8,128...) custom-call(bf16[27,64,64]{2,1,0:T(8,128)(2,1)S(1)} %copy-done.1, ...), custom_call_target="tpu_custom_call" | custom-call | tf_op jit(solution)/shard_map/pallas_call | solution.py:431
  16.5 0.0 copy-start.2
  16.5 0.0 copy-start.3
  16.5 0.9 %shard_map.90.acc = f32[2,2,144,256]{3,2,1,0:T(8,128)S(1)} custom-call(bf16[8,48,256]{2,1,0:T(8,128)(2,1)S(1)} %all-to-all-done.mid, bf16[256,2304]{1,0:T(8,128)(2,1)S(1)} %get-tuple-element.33.w1a, bf16[128,1152]{1,0:T(8,128)(2,1)S(1)} %get-tuple-element.34.w1c), custom_call_target="tpu_custom_call" | custom-call | tf_op jit(solution)/shard_map/pallas_call | solution.py:431
  17.4 0.0 collective-permute-done.3.beside
  17.4 0.0 copy-done.2
  17.4 0.0 copy-done.3
  17.5 0.2 shard_map.93
  17.7 1.5 %collective-permute-done.rim_a = bf16[6,48,256]{2,1,0:T(8,128)(2,1)S(1)} collective-permute-done((bf16[6,48,256]{2,1,0:T(8,128)(2,1)S(1)}, bf16[6,48,256]{2,1,0:T(8,128)(2,1)S(1)}, u32[]{:S(2)}, u32[]{:S(2)}) %collective-permute-start) | collective-permute-done | bytes 147488 | tf_op jit(solution)/shard_map/ppermute | solution.py:503
  19.2 1.0 %collective-permute-done.1.rim_b = bf16[6,48,256]{2,1,0:T(8,128)(2,1)S(1)} collective-permute-done((bf16[6,48,256]{2,1,0:T(8,128)(2,1)S(1)}, bf16[6,48,256]{2,1,0:T(8,128)(2,1)S(1)}, u32[]{:S(2)}, u32[]{:S(2)}) %collective-permute-start.1) | collective-permute-done | bytes 147488 | tf_op jit(solution)/shard_map/ppermute | solution.py:504
  20.2 0.1 shard_map.88
  20.4 1.0 %shard_map.91 = (bf16[8,32,256]{2,1,0:T(8,128)(2,1)S(1)}, bf16[3,192,256]{2,1,0:T(8,128)(2,1)S(1)}) custom-call(bf16[2,4,144,256]{3,2,1,0:T(8,128)(2,1)S(1)} %get-tuple-element.31.q, bf16[4,144,128]{2,1,0:T(8,128)(2,1)S(1)} %get-tuple-element.32.x34, bf16[256,2304]{1,0:T(8,128)(2,1)S(1)} %get-tuple-element.33.w1a, ...), custom_call_target="tpu_custom_call" | custom-call | tf_op jit(solution)/shard_map/pallas_call | solution.py:431
  21.4 0.6 %shard_map.94.hd = bf16[3,144,512]{2,1,0:T(8,128)(2,1)S(1)} custom-call(bf16[3,192,256]{2,1,0:T(8,128)(2,1)S(1)} %get-tuple-element.36.pd, bf16[256,1152]{1,0:T(8,128)(2,1)S(1)} %get-tuple-element.44.w2a, bf16[256,1152]{1,0:T(8,128)(2,1)S(1)} %get-tuple-element.45.w2c, f32[8,128]{1,0:T(8,128)S(1)} %get-tuple-element.46.b2), custom_call_target="tpu_custom_call" | custom-call | tf_op jit(solution)/shard_map/pallas_call | solution.py:431
  21.9 0.0 collective-permute-done.5.beside
  22.0 0.8 %shard_map.95 = bf16[8,48,256]{2,1,0:T(8,128)(2,1)S(1)} custom-call(bf16[3,144,512]{2,1,0:T(8,128)(2,1)S(1)} %shard_map.94.hd, bf16[27,64,128]{2,1,0:T(8,128)(2,1)S(1)} %get-tuple-element.40.k3, bf16[864,128]{1,0:T(8,128)(2,1)S(1)} %collective-permute-done.4.over, bf16[864,128]{1,0:T(8,128)(2,1)S(1)} %collective-permute-done.5.beside, ...), custom_call_target="tpu_custom_call" | custom-call | tf_op jit(solution)/shard_map/pallas_call | solution.py:431
  22.8 8.7 %all_to_all.10.got = bf16[8,48,256]{2,1,0:T(8,128)(2,1)S(1)} all-to-all(bf16[8,48,256]{2,1,0:T(8,128)(2,1)S(1)} %shard_map.95), channel_id=1, replica_groups={{0,1,2,3,4,5,6,7},{8,9,10,11,12,13,14,15},{16,17,18,19,20,21,22,23},{24..., dimensions={0} | all-to-all | bytes 393216 | tf_op jit(solution)/shard_map/all_to_all | solution.py:549
  31.5 1.1 %shard_map.96 = (bf16[256,256]{1,0:T(8,128)(2,1)}, bf16[256,128]{1,0:T(8,128)(2,1)}) custom-call(bf16[8,48,256]{2,1,0:T(8,128)(2,1)S(1)} %all_to_all.10.got, bf16[256,256]{1,0:T(8,128)(2,1)S(1)} %get-tuple-element.50.order, bf16[256,256]{1,0:T(8,128)(2,1)S(1)} %get-tuple-element.51.same), custom_call_target="tpu_custom_call" | custom-call | tf_op jit(solution)/shard_map/pallas_call | solution.py:431
  (1 shorter events, 0.0 us)
Async XLA Ops:
  0.6 15.4 %copy-start = (bf16[27,64,64]{2,1,0:T(8,128)(2,1)S(1)}, bf16[27,64,64]{2,1,0:T(8,128)(2,1)}, u32[]{:S(2)}) copy-start(bf16[27,64,64]{2,1,0:T(8,128)(2,1)} %k2.1) | copy-start | bytes 663556
  0.6 15.4 %copy-start.1 = (bf16[27,64,64]{2,1,0:T(8,128)(2,1)S(1)}, bf16[27,64,64]{2,1,0:T(8,128)(2,1)}, u32[]{:S(2)}) copy-start(bf16[27,64,64]{2,1,0:T(8,128)(2,1)} %k1.1) | copy-start | bytes 663556
  0.7 15.4 %copy-start.4 = (bf16[64]{0:T(256)(128)(2,1)S(1)}, bf16[64]{0:T(256)(128)(2,1)}, u32[]{:S(2)}) copy-start(bf16[64]{0:T(256)(128)(2,1)} %param.9) | copy-start | bytes 388
  2.7 6.9 %collective-permute-start.4 = (bf16[864,128]{1,0:T(8,128)(2,1)S(1)}, bf16[864,128]{1,0:T(8,128)(2,1)S(1)}, u32[]{:S(2)}, u32[]{:S(2)}) collective-permute-start(bf16[864,128]{1,0:T(8,128)(2,1)S(1)} %get-tuple-element.47), channel_id=1, source_target_pairs={{0,1},{1,0},{2,3},{3,2},{4,5},{5,4},{6,7},{7,6},{8,9},{9,8},{10,11... | collective-permute-start | bytes 663560 | tf_op jit(solution)/shard_map/ppermute | solution.py:479
  4.0 9.6 %all-to-all-start = ((bf16[8,48,256]{2,1,0:T(8,128)(2,1)}), bf16[8,48,256]{2,1,0:T(8,128)(2,1)S(1)}, u32[]{:S(2)}, u32[]{:S(2)}) async-start(bf16[8,48,256]{2,1,0:T(8,128)(2,1)} %get-tuple-element.28), calls=%async_computation | async-start | bytes 393216 | tf_op jit(solution)/shard_map/all_to_all | solution.py:475
  8.3 6.8 %collective-permute-start.2 = (bf16[448,128]{1,0:T(8,128)(2,1)S(1)}, bf16[448,128]{1,0:T(8,128)(2,1)S(1)}, u32[]{:S(2)}, u32[]{:S(2)}) collective-permute-start(bf16[448,128]{1,0:T(8,128)(2,1)S(1)} %get-tuple-element.43), channel_id=1, source_target_pairs={{0,1},{1,0},{2,3},{3,2},{4,5},{5,4},{6,7},{7,6},{8,9},{9,8},{10,11... | collective-permute-start | bytes 344072 | tf_op jit(solution)/shard_map/ppermute | solution.py:478
  9.7 12.3 %collective-permute-start.5 = (bf16[864,128]{1,0:T(8,128)(2,1)S(1)}, bf16[864,128]{1,0:T(8,128)(2,1)S(1)}, u32[]{:S(2)}, u32[]{:S(2)}) collective-permute-start(bf16[864,128]{1,0:T(8,128)(2,1)S(1)} %collective-permute-done.4.over), channel_id=1, source_target_pairs={{0,2},{2,0},{4,6},{6,4},{8,10},{10,8},{12,14},{14,12},{16,18},{18,... | collective-permute-start | bytes 663560 | tf_op jit(solution)/shard_map/ppermute | solution.py:507
  13.7 5.5 %collective-permute-start = (bf16[6,48,256]{2,1,0:T(8,128)(2,1)S(1)}, bf16[6,48,256]{2,1,0:T(8,128)(2,1)S(1)}, u32[]{:S(2)}, u32[]{:S(2)}) collective-permute-start(bf16[6,48,256]{2,1,0:T(8,128)(2,1)S(1)} %get-tuple-element.29), channel_id=1, source_target_pairs={{0,8},{2,10},{4,12},{6,14},{8,0},{10,2},{12,4},{14,6},{16,24},{18,... | collective-permute-start | bytes 442376 | tf_op jit(solution)/shard_map/ppermute | solution.py:503
  15.1 5.2 %collective-permute-start.1 = (bf16[6,48,256]{2,1,0:T(8,128)(2,1)S(1)}, bf16[6,48,256]{2,1,0:T(8,128)(2,1)S(1)}, u32[]{:S(2)}, u32[]{:S(2)}) collective-permute-start(bf16[6,48,256]{2,1,0:T(8,128)(2,1)S(1)} %get-tuple-element.30), channel_id=1, source_target_pairs={{0,2},{2,0},{4,6},{6,4},{8,16},{10,18},{12,20},{14,22},{16,8},{18,... | collective-permute-start | bytes 442376 | tf_op jit(solution)/shard_map/ppermute | solution.py:504
  15.1 2.3 %collective-permute-start.3 = (bf16[448,128]{1,0:T(8,128)(2,1)S(1)}, bf16[448,128]{1,0:T(8,128)(2,1)S(1)}, u32[]{:S(2)}, u32[]{:S(2)}) collective-permute-start(bf16[448,128]{1,0:T(8,128)(2,1)S(1)} %collective-permute-done.2.over), channel_id=1, source_target_pairs={{0,2},{2,0},{4,6},{6,4},{8,10},{10,8},{12,14},{14,12},{16,18},{18,... | collective-permute-start | bytes 344072 | tf_op jit(solution)/shard_map/ppermute | solution.py:506
  16.5 0.9 %copy-start.2 = (bf16[64]{0:T(256)(128)(2,1)S(1)}, bf16[64]{0:T(256)(128)(2,1)}, u32[]{:S(2)}) copy-start(bf16[64]{0:T(256)(128)(2,1)} %param.11) | copy-start | bytes 388
  16.5 0.9 %copy-start.3 = (bf16[64]{0:T(256)(128)(2,1)S(1)}, bf16[64]{0:T(256)(128)(2,1)}, u32[]{:S(2)}) copy-start(bf16[64]{0:T(256)(128)(2,1)} %param.13) | copy-start | bytes 388

commit v8 on v7

--- a/solution.py
+++ b/solution.py
@@ -97,12 +97,17 @@
     for copy in copies:
         copy.start()
     count, width = blocks.shape[0], volume.shape[1]
-    shape = (count * 2 * RUN, width)
-    row = lax.broadcasted_iota(jnp.int32, shape, 0)
-    col = lax.broadcasted_iota(jnp.int32, shape, 1)
-    peer, rest = row // (2 * RUN), row % (2 * RUN)
-    wanted = (width // count) * peer + 2 * (rest % RUN - LEAD) + rest // RUN
-    chosen = jnp.where(wanted == col, 1.0, 0.0).astype(BF)
+    row = lax.broadcasted_iota(jnp.int32, (RUN, width), 0)
+    col = lax.broadcasted_iota(jnp.int32, (RUN, width), 1)
+    ahead = 2 * (row - LEAD) - col
+    chosen = jnp.concatenate(
+        [
+            jnp.where(ahead == -(width // count) * peer - par, 1.0, 0.0)
+            for peer in range(count)
+            for par in range(2)
+        ],
+        axis=0,
+    ).astype(BF)
     copies[0].wait()
     blocks[...] = dot(chosen, volume[...], NT).astype(BF).reshape(blocks.shape)
     for copy in copies[1:]:
@@ -180,7 +185,8 @@
     row = lax.broadcasted_iota(jnp.int32, (planes * FRAME, 1), 0)
     col = 16 * group - LEAD + row % FRAME
     plane = LAYER * layer + first + row // FRAME
-    return (plane >= 0) & (plane < LAYER * layers) & (col >= 0) & (col < 128)
+    within = (plane >= 0) & (plane < LAYER * layers) & (col >= 0) & (col < 128)
+    return jnp.broadcast_to(jnp.where(within, 1.0, 0.0), (planes * FRAME, 128))
 
 
 def pair(parts, weights):
@@ -248,7 +254,9 @@
     return functools.reduce(jnp.add, terms)
 
 
-def inner_kernel(mid, w1a, w1c, acc, q, x34):
+def inner_kernel(mid, w1a, w1c, acc, within1, within2, q, x34):
+    within1[...] = inside(-2, LAYER + 4)
+    within2[...] = inside(-1, LAYER + 2)
     spread_runs(lambda v, f, rows: mid[2 * v + f, rows, :], range(LAYER), q, x34)
     sums = products(q, x34, w1a, w1c, 0)
     for f in range(2):
@@ -275,13 +283,12 @@
     spread_runs(run, range(6), q, x34)
 
 
-def one_kernel(q, x34, w1a, w1c, b1, acc, skips, pd):
+def one_kernel(q, x34, w1a, w1c, b1, acc, within, skips, pd):
     left = lax.broadcasted_iota(jnp.int32, (1, 128), 1) < 64
     sums = products(q, x34, w1a, w1c, 1)
     u = LAYER + 4
     targets = ((0, 1, 2, u - 1), (0, 1, u - 2, u - 1), (0, u - 3, u - 2, u - 1))
     bias = b1[0:1, :]
-    within = inside(-2, u)
     tiles = []
     for f in range(2):
         ys = []
@@ -306,7 +313,7 @@
         y0 = jnp.maximum(y0, pltpu.roll(y0, 64, 1))
         y1 = jnp.maximum(y1, pltpu.roll(y1, 64, 1))
         y = jnp.maximum(jnp.where(left, y0, y1) + bias[:, :128], 0.0)
-        tiles.append(jnp.where(within, y, 0.0))
+        tiles.append(jnp.where(within[...] > 0.0, y, 0.0))
     pooled = jnp.concatenate(tiles, axis=1)
     for dw in range(3):
         pd[dw] = shifted(pooled, dw - 1).astype(BF)
@@ -345,7 +352,7 @@
     bias3[...] = jnp.broadcast_to(order3, bias3.shape)
 
 
-def two_kernel(pd, w2a, w2c, b2, hd):
+def two_kernel(pd, w2a, w2c, b2, within, hd):
     left = lax.broadcasted_iota(jnp.int32, (1, 128), 1) < 64
     m = (LAYER + 2) * FRAME
     pairs = pair(
@@ -364,7 +371,8 @@
         axis=1,
     )
     bias = jnp.concatenate([b2[0:1, :]] * 4, axis=1)
-    hidden = jnp.where(inside(-1, LAYER + 2), jnp.maximum(hidden + bias, 0.0), 0.0).astype(BF).astype(F32)
+    within = jnp.concatenate([within[...]] * 4, axis=1)
+    hidden = jnp.where(within > 0.0, jnp.maximum(hidden + bias, 0.0), 0.0).astype(BF).astype(F32)
     for dw in range(3):
         hd[dw] = shifted(hidden, dw - 1).astype(BF)
 
@@ -520,9 +528,13 @@
         rows = FRAME * planes
         return [pltpu.VMEM((2, 4, rows, 256), BF), pltpu.VMEM((4, rows, 128), BF)]
 
-    acc = call(
+    acc, within1, within2 = call(
         inner_kernel,
-        pltpu.VMEM((2, 2, FRAME * (LAYER + 2), 256), F32),
+        (
+            pltpu.VMEM((2, 2, FRAME * (LAYER + 2), 256), F32),
+            pltpu.VMEM((FRAME * (LAYER + 4), 128), F32),
+            pltpu.VMEM((FRAME * (LAYER + 2), 128), F32),
+        ),
         *map(near, (mid, w1a, w1c)),
         scratch=space(LAYER),
         limit=24,
@@ -531,13 +543,13 @@
     skips, pooled = call(
         one_kernel,
         (pltpu.VMEM((peers, 32, 256), BF), pltpu.VMEM((3, FRAME * (LAYER + 4), 256), BF)),
-        *map(near, (*halo, w1a, w1c, bias1, acc)),
+        *map(near, (*halo, w1a, w1c, bias1, acc, within1)),
         limit=24,
     )
     hidden = call(
         two_kernel,
         pltpu.VMEM((3, FRAME * (LAYER + 2), 512), BF),
-        *map(near, (pooled, w2a, w2c, bias2)),
+        *map(near, (pooled, w2a, w2c, bias2, within2)),
         limit=24,
     )
     out = call(

time: 32.9 us -> 32.9 us (level)
  no operation moved by 1% of the time
where the time goes in v8:
time: 32.9 us; the launch traced here: 32.6 us
  starting transfers between devices  10.2 us (31%)
  blocking collectives  8.74 us (27%)
  Pallas kernels  7.3 us (22%)
  waiting for transfers between devices  5.55 us (17%)
  between operations  0.76 us (2%)
    all_to_all x1, blocking collectives, by_columns(): home = exchange(out)  8.74 us
    pallas_call x11, Pallas kernels, call(): pl.pallas_call(kernel, out_shape=outs, in_specs=[hbm] * far + [spec] * (l...  7.3 us
    all_to_all x1, starting transfers between devices, by_columns(): mid = exchange(blocks)  4.25 us
    all_to_all x1, waiting for transfers between devices, by_columns(): mid = exchange(blocks)  3.03 us
    ppermute x1, waiting for transfers between devices, by_columns(): rim_a = lax.ppermute(to_first, 'slab', swaps(0))  1.46 us
    ppermute x1, starting transfers between devices, by_columns(): rim_a = lax.ppermute(to_first, 'slab', swaps(0))  1.36 us
    ppermute x1, starting transfers between devices, by_columns(): over2 = lax.ppermute(sent2, 'filt', [(0, 1), (1, 0)])  1.36 us
    ppermute x1, starting transfers between devices, by_columns(): over3 = lax.ppermute(sent3, 'filt', [(0, 1), (1, 0)])  1.3 us
  transfers between devices with their start and end apart: 7, of which 3 were waited for; matrix products, arithmetic and copies ran while one was open for 0% of the time, Pallas kernels for 10%

profile of v8, /device:TPU:17, one launch (start us, length us, event | category | flops | bytes accessed | tf_op | source)
XLA Modules:
  0.0 32.6 jit_solution(3023101645518347154)
XLA Ops:
  0.6 0.0 copy-start
  0.6 0.0 copy-start.1
  0.7 0.0 copy-start.4
  0.7 2.0 %shard_map.86 = (bf16[8,48,256]{2,1,0:T(8,128)(2,1)}, bf16[27,32,64]{2,1,0:T(8,128)(2,1)S(1)}, bf16[27,64,128]{2,1,0:T(8,128)(2,1)S(1)}, bf16[1,64]{1,0:T(2,128)(2,1)S(1)}, bf16[1,64]{1,0:T(2,128)(2,1)S(1)}) custom-call(bf16[256,256]{1,0:T(8,128)(2,1)} %bitcast.11, bf16[27,64,64]{2,1,0:T(8,128)(2,1)} %k2.1, bf16[27,64,128]{2,1,0:T(8,128)(2,1)} %far3.1, ...), custom_call_target="tpu_custom_call" | custom-call | tf_op jit(solution)/shard_map/pallas_call | solution.py:439
  2.6 0.1 shard_map.92
  2.7 1.3 %collective-permute-start.4 = (bf16[864,128]{1,0:T(8,128)(2,1)S(1)}, bf16[864,128]{1,0:T(8,128)(2,1)S(1)}, u32[]{:S(2)}, u32[]{:S(2)}) collective-permute-start(bf16[864,128]{1,0:T(8,128)(2,1)S(1)} %get-tuple-element.53), channel_id=1, source_target_pairs={{0,1},{1,0},{2,3},{3,2},{4,5},{5,4},{6,7},{7,6},{8,9},{9,8},{10,11... | collective-permute-start | bytes 663560 | tf_op jit(solution)/shard_map/ppermute | solution.py:487
  4.0 4.3 %all-to-all-start = ((bf16[8,48,256]{2,1,0:T(8,128)(2,1)}), bf16[8,48,256]{2,1,0:T(8,128)(2,1)S(1)}, u32[]{:S(2)}, u32[]{:S(2)}) async-start(bf16[8,48,256]{2,1,0:T(8,128)(2,1)} %get-tuple-element.31), calls=%async_computation | async-start | bytes 393216 | tf_op jit(solution)/shard_map/all_to_all | solution.py:483
  8.3 1.4 %collective-permute-start.2 = (bf16[448,128]{1,0:T(8,128)(2,1)S(1)}, bf16[448,128]{1,0:T(8,128)(2,1)S(1)}, u32[]{:S(2)}, u32[]{:S(2)}) collective-permute-start(bf16[448,128]{1,0:T(8,128)(2,1)S(1)} %get-tuple-element.48), channel_id=1, source_target_pairs={{0,1},{1,0},{2,3},{3,2},{4,5},{5,4},{6,7},{7,6},{8,9},{9,8},{10,11... | collective-permute-start | bytes 344072 | tf_op jit(solution)/shard_map/ppermute | solution.py:486
  9.7 0.0 collective-permute-done.4.over
  9.7 1.0 %collective-permute-start.5 = (bf16[864,128]{1,0:T(8,128)(2,1)S(1)}, bf16[864,128]{1,0:T(8,128)(2,1)S(1)}, u32[]{:S(2)}, u32[]{:S(2)}) collective-permute-start(bf16[864,128]{1,0:T(8,128)(2,1)S(1)} %collective-permute-done.4.over), channel_id=1, source_target_pairs={{0,2},{2,0},{4,6},{6,4},{8,10},{10,8},{12,14},{14,12},{16,18},{18,... | collective-permute-start | bytes 663560 | tf_op jit(solution)/shard_map/ppermute | solution.py:515
  10.6 3.0 %all-to-all-done.mid = bf16[8,48,256]{2,1,0:T(8,128)(2,1)S(1)} async-done(((bf16[8,48,256]{2,1,0:T(8,128)(2,1)}), bf16[8,48,256]{2,1,0:T(8,128)(2,1)S(1)}, u32[]{:S(2)}, u32[]{:S(2)}) %all-to-all-start) | async-done | bytes 196640 | tf_op jit(solution)/shard_map/all_to_all | solution.py:483
  13.7 1.4 %collective-permute-start = (bf16[6,48,256]{2,1,0:T(8,128)(2,1)S(1)}, bf16[6,48,256]{2,1,0:T(8,128)(2,1)S(1)}, u32[]{:S(2)}, u32[]{:S(2)}) collective-permute-start(bf16[6,48,256]{2,1,0:T(8,128)(2,1)S(1)} %get-tuple-element.32), channel_id=1, source_target_pairs={{0,8},{2,10},{4,12},{6,14},{8,0},{10,2},{12,4},{14,6},{16,24},{18,... | collective-permute-start | bytes 442376 | tf_op jit(solution)/shard_map/ppermute | solution.py:511
  15.1 0.0 collective-permute-start.1
  15.1 0.0 collective-permute-done.2.over
  15.1 1.0 %collective-permute-start.3 = (bf16[448,128]{1,0:T(8,128)(2,1)S(1)}, bf16[448,128]{1,0:T(8,128)(2,1)S(1)}, u32[]{:S(2)}, u32[]{:S(2)}) collective-permute-start(bf16[448,128]{1,0:T(8,128)(2,1)S(1)} %collective-permute-done.2.over), channel_id=1, source_target_pairs={{0,2},{2,0},{4,6},{6,4},{8,10},{10,8},{12,14},{14,12},{16,18},{18,... | collective-permute-start | bytes 344072 | tf_op jit(solution)/shard_map/ppermute | solution.py:514
  16.1 0.0 copy-done
  16.1 0.0 copy-done.1
  16.1 0.0 copy-done.4
  16.1 0.0 copy-start.2
  16.1 0.0 copy-start.3
  16.1 0.4 %shard_map.89 = (bf16[256,2304]{1,0:T(8,128)(2,1)S(1)}, bf16[128,1152]{1,0:T(8,128)(2,1)S(1)}, bf16[128,1152]{1,0:T(8,128)(2,1)S(1)}, bf16[128,1152]{1,0:T(8,128...) custom-call(bf16[27,64,64]{2,1,0:T(8,128)(2,1)S(1)} %copy-done.1, ...), custom_call_target="tpu_custom_call" | custom-call | tf_op jit(solution)/shard_map/pallas_call | solution.py:439
  16.5 1.0 %shard_map.90 = (f32[2,2,144,256]{3,2,1,0:T(8,128)S(1)}, f32[192,128]{1,0:T(8,128)S(1)}, f32[144,128]{1,0:T(8,128)S(1)}) custom-call(bf16[8,48,256]{2,1,0:T(8,128)(2,1)S(1)} %all-to-all-done.mid, bf16[256,2304]{1,0:T(8,128)(2,1)S(1)} %get-tuple-element.36.w1a, bf16[128,1152]{1,0:T(8,128)(2,1)S(1)} %get-tuple-element.37.w1c), custom_call_target="tpu_custom_call" | custom-call | tf_op jit(solution)/shard_map/pallas_call | solution.py:439
  17.5 0.0 collective-permute-done.3.beside
  17.5 0.0 copy-done.2
  17.5 0.0 copy-done.3
  17.5 0.2 shard_map.93
  17.8 1.5 %collective-permute-done.rim_a = bf16[6,48,256]{2,1,0:T(8,128)(2,1)S(1)} collective-permute-done((bf16[6,48,256]{2,1,0:T(8,128)(2,1)S(1)}, bf16[6,48,256]{2,1,0:T(8,128)(2,1)S(1)}, u32[]{:S(2)}, u32[]{:S(2)}) %collective-permute-start) | collective-permute-done | bytes 147488 | tf_op jit(solution)/shard_map/ppermute | solution.py:511
  19.2 1.0 %collective-permute-done.1.rim_b = bf16[6,48,256]{2,1,0:T(8,128)(2,1)S(1)} collective-permute-done((bf16[6,48,256]{2,1,0:T(8,128)(2,1)S(1)}, bf16[6,48,256]{2,1,0:T(8,128)(2,1)S(1)}, u32[]{:S(2)}, u32[]{:S(2)}) %collective-permute-start.1) | collective-permute-done | bytes 147488 | tf_op jit(solution)/shard_map/ppermute | solution.py:512
  20.2 0.1 shard_map.88
  20.4 1.0 %shard_map.91 = (bf16[8,32,256]{2,1,0:T(8,128)(2,1)S(1)}, bf16[3,192,256]{2,1,0:T(8,128)(2,1)S(1)}) custom-call(bf16[2,4,144,256]{3,2,1,0:T(8,128)(2,1)S(1)} %get-tuple-element.34.q, bf16[4,144,128]{2,1,0:T(8,128)(2,1)S(1)} %get-tuple-element.35.x34, bf16[256,2304]{1,0:T(8,128)(2,1)S(1)} %get-tuple-element.36.w1a, ...), custom_call_target="tpu_custom_call" | custom-call | tf_op jit(solution)/shard_map/pallas_call | solution.py:439
  21.4 0.6 %shard_map.94.hd = bf16[3,144,512]{2,1,0:T(8,128)(2,1)S(1)} custom-call(bf16[3,192,256]{2,1,0:T(8,128)(2,1)S(1)} %get-tuple-element.41.pd, bf16[256,1152]{1,0:T(8,128)(2,1)S(1)} %get-tuple-element.49.w2a, bf16[256,1152]{1,0:T(8,128)(2,1)S(1)} %get-tuple-element.50.w2c, f32[8,128]{1,0:T(8,128)S(1)} %get-tuple-element.51.b2, ...), custom_call_target="tpu_custom_call" | custom-call | tf_op jit(solution)/shard_map/pallas_call | solution.py:439
  21.9 0.0 collective-permute-done.5.beside
  22.0 0.8 %shard_map.95 = bf16[8,48,256]{2,1,0:T(8,128)(2,1)S(1)} custom-call(bf16[3,144,512]{2,1,0:T(8,128)(2,1)S(1)} %shard_map.94.hd, bf16[27,64,128]{2,1,0:T(8,128)(2,1)S(1)} %get-tuple-element.45.k3, bf16[864,128]{1,0:T(8,128)(2,1)S(1)} %collective-permute-done.4.over, bf16[864,128]{1,0:T(8,128)(2,1)S(1)} %collective-permute-done.5.beside, ...), custom_call_target="tpu_custom_call" | custom-call | tf_op jit(solution)/shard_map/pallas_call | solution.py:439
  22.8 8.7 %all_to_all.10.got = bf16[8,48,256]{2,1,0:T(8,128)(2,1)S(1)} all-to-all(bf16[8,48,256]{2,1,0:T(8,128)(2,1)S(1)} %shard_map.95), channel_id=1, replica_groups={{0,1,2,3,4,5,6,7},{8,9,10,11,12,13,14,15},{16,17,18,19,20,21,22,23},{24..., dimensions={0} | all-to-all | bytes 393216 | tf_op jit(solution)/shard_map/all_to_all | solution.py:561
  31.5 1.1 %shard_map.96 = (bf16[256,256]{1,0:T(8,128)(2,1)}, bf16[256,128]{1,0:T(8,128)(2,1)}) custom-call(bf16[8,48,256]{2,1,0:T(8,128)(2,1)S(1)} %all_to_all.10.got, bf16[256,256]{1,0:T(8,128)(2,1)S(1)} %get-tuple-element.56.order, bf16[256,256]{1,0:T(8,128)(2,1)S(1)} %get-tuple-element.57.same), custom_call_target="tpu_custom_call" | custom-call | tf_op jit(solution)/shard_map/pallas_call | solution.py:439
  (1 shorter events, 0.0 us)
Async XLA Ops:
  0.6 15.4 %copy-start = (bf16[27,64,64]{2,1,0:T(8,128)(2,1)S(1)}, bf16[27,64,64]{2,1,0:T(8,128)(2,1)}, u32[]{:S(2)}) copy-start(bf16[27,64,64]{2,1,0:T(8,128)(2,1)} %k2.1) | copy-start | bytes 663556
  0.6 15.4 %copy-start.1 = (bf16[27,64,64]{2,1,0:T(8,128)(2,1)S(1)}, bf16[27,64,64]{2,1,0:T(8,128)(2,1)}, u32[]{:S(2)}) copy-start(bf16[27,64,64]{2,1,0:T(8,128)(2,1)} %k1.1) | copy-start | bytes 663556
  0.7 15.4 %copy-start.4 = (bf16[64]{0:T(256)(128)(2,1)S(1)}, bf16[64]{0:T(256)(128)(2,1)}, u32[]{:S(2)}) copy-start(bf16[64]{0:T(256)(128)(2,1)} %param.9) | copy-start | bytes 388
  2.7 6.9 %collective-permute-start.4 = (bf16[864,128]{1,0:T(8,128)(2,1)S(1)}, bf16[864,128]{1,0:T(8,128)(2,1)S(1)}, u32[]{:S(2)}, u32[]{:S(2)}) collective-permute-start(bf16[864,128]{1,0:T(8,128)(2,1)S(1)} %get-tuple-element.53), channel_id=1, source_target_pairs={{0,1},{1,0},{2,3},{3,2},{4,5},{5,4},{6,7},{7,6},{8,9},{9,8},{10,11... | collective-permute-start | bytes 663560 | tf_op jit(solution)/shard_map/ppermute | solution.py:487
  4.0 9.6 %all-to-all-start = ((bf16[8,48,256]{2,1,0:T(8,128)(2,1)}), bf16[8,48,256]{2,1,0:T(8,128)(2,1)S(1)}, u32[]{:S(2)}, u32[]{:S(2)}) async-start(bf16[8,48,256]{2,1,0:T(8,128)(2,1)} %get-tuple-element.31), calls=%async_computation | async-start | bytes 393216 | tf_op jit(solution)/shard_map/all_to_all | solution.py:483
  8.3 6.8 %collective-permute-start.2 = (bf16[448,128]{1,0:T(8,128)(2,1)S(1)}, bf16[448,128]{1,0:T(8,128)(2,1)S(1)}, u32[]{:S(2)}, u32[]{:S(2)}) collective-permute-start(bf16[448,128]{1,0:T(8,128)(2,1)S(1)} %get-tuple-element.48), channel_id=1, source_target_pairs={{0,1},{1,0},{2,3},{3,2},{4,5},{5,4},{6,7},{7,6},{8,9},{9,8},{10,11... | collective-permute-start | bytes 344072 | tf_op jit(solution)/shard_map/ppermute | solution.py:486
  9.7 12.3 %collective-permute-start.5 = (bf16[864,128]{1,0:T(8,128)(2,1)S(1)}, bf16[864,128]{1,0:T(8,128)(2,1)S(1)}, u32[]{:S(2)}, u32[]{:S(2)}) collective-permute-start(bf16[864,128]{1,0:T(8,128)(2,1)S(1)} %collective-permute-done.4.over), channel_id=1, source_target_pairs={{0,2},{2,0},{4,6},{6,4},{8,10},{10,8},{12,14},{14,12},{16,18},{18,... | collective-permute-start | bytes 663560 | tf_op jit(solution)/shard_map/ppermute | solution.py:515
  13.7 5.5 %collective-permute-start = (bf16[6,48,256]{2,1,0:T(8,128)(2,1)S(1)}, bf16[6,48,256]{2,1,0:T(8,128)(2,1)S(1)}, u32[]{:S(2)}, u32[]{:S(2)}) collective-permute-start(bf16[6,48,256]{2,1,0:T(8,128)(2,1)S(1)} %get-tuple-element.32), channel_id=1, source_target_pairs={{0,8},{2,10},{4,12},{6,14},{8,0},{10,2},{12,4},{14,6},{16,24},{18,... | collective-permute-start | bytes 442376 | tf_op jit(solution)/shard_map/ppermute | solution.py:511
  15.1 5.2 %collective-permute-start.1 = (bf16[6,48,256]{2,1,0:T(8,128)(2,1)S(1)}, bf16[6,48,256]{2,1,0:T(8,128)(2,1)S(1)}, u32[]{:S(2)}, u32[]{:S(2)}) collective-permute-start(bf16[6,48,256]{2,1,0:T(8,128)(2,1)S(1)} %get-tuple-element.33), channel_id=1, source_target_pairs={{0,2},{2,0},{4,6},{6,4},{8,16},{10,18},{12,20},{14,22},{16,8},{18,... | collective-permute-start | bytes 442376 | tf_op jit(solution)/shard_map/ppermute | solution.py:512
  15.1 2.4 %collective-permute-start.3 = (bf16[448,128]{1,0:T(8,128)(2,1)S(1)}, bf16[448,128]{1,0:T(8,128)(2,1)S(1)}, u32[]{:S(2)}, u32[]{:S(2)}) collective-permute-start(bf16[448,128]{1,0:T(8,128)(2,1)S(1)} %collective-permute-done.2.over), channel_id=1, source_target_pairs={{0,2},{2,0},{4,6},{6,4},{8,10},{10,8},{12,14},{14,12},{16,18},{18,... | collective-permute-start | bytes 344072 | tf_op jit(solution)/shard_map/ppermute | solution.py:514
  16.1 1.4 %copy-start.2 = (bf16[64]{0:T(256)(128)(2,1)S(1)}, bf16[64]{0:T(256)(128)(2,1)}, u32[]{:S(2)}) copy-start(bf16[64]{0:T(256)(128)(2,1)} %param.11) | copy-start | bytes 388
  16.1 1.4 %copy-start.3 = (bf16[64]{0:T(256)(128)(2,1)S(1)}, bf16[64]{0:T(256)(128)(2,1)}, u32[]{:S(2)}) copy-start(bf16[64]{0:T(256)(128)(2,1)} %param.13) | copy-start | bytes 388

commit v9 on v8

--- a/solution.py
+++ b/solution.py
@@ -381,7 +381,6 @@
     half, core = lax.axis_index("filt"), lax.axis_index("slab") % 2
     lane = lax.broadcasted_iota(jnp.int32, (1, 128), 1)
     left = lane < 64
-    out[:, 0:32, :] = skips[...]
     m = LAYER * FRAME
 
     def third(t):
@@ -431,7 +430,7 @@
     return jax.ShapeDtypeStruct(dims, BF)
 
 
-def call(kernel, outs, *operands, scratch=(), limit=8, far=0):
+def call(kernel, outs, *operands, scratch=(), limit=8, far=0, aliases={}):
     spec = pl.BlockSpec(memory_space=pltpu.VMEM)
     hbm = pl.BlockSpec(memory_space=pltpu.HBM)
     there = [pltpu.with_memory_space_constraint(x, pltpu.HBM) for x in operands[:far]]
@@ -442,6 +441,7 @@
         in_specs=[hbm] * far + [spec] * (len(operands) - far),
         out_specs=jax.tree.map(lambda _: spec, outs),
         scratch_shapes=scratch,
+        input_output_aliases=aliases,
         compiler_params=pltpu.CompilerParams(vmem_limit_bytes=limit << 20),
     )(*operands)
 
@@ -542,7 +542,7 @@
     halo = call(halo_kernel, tuple(space(6)), near(rim_a), near(rim_b), limit=24)
     skips, pooled = call(
         one_kernel,
-        (pltpu.VMEM((peers, 32, 256), BF), pltpu.VMEM((3, FRAME * (LAYER + 4), 256), BF)),
+        (pltpu.VMEM((peers, 48, 256), BF), pltpu.VMEM((3, FRAME * (LAYER + 4), 256), BF)),
         *map(near, (*halo, w1a, w1c, bias1, acc, within1)),
         limit=24,
     )
@@ -556,6 +556,7 @@
         three_kernel,
         pltpu.VMEM((peers, 48, 256), BF),
         *map(near, (hidden, mine[1], over3, beside3, bias3, skips)),
+        aliases={5: 0},
         limit=24,
     )
     home = exchange(out)

time: 32.9 us -> 32.9 us (level)
  no operation moved by 1% of the time
where the time goes in v9:
time: 32.9 us; the launch traced here: 32.6 us
  starting transfers between devices  10.2 us (31%)
  blocking collectives  8.74 us (27%)
  Pallas kernels  7.31 us (22%)
  waiting for transfers between devices  5.55 us (17%)
  between operations  0.76 us (2%)
    all_to_all x1, blocking collectives, by_columns(): home = exchange(out)  8.74 us
    pallas_call x11, Pallas kernels, call(): pl.pallas_call(kernel, out_shape=outs, in_specs=[hbm] * far + [spec] * (l...  7.31 us
    all_to_all x1, starting transfers between devices, by_columns(): mid = exchange(blocks)  4.25 us
    all_to_all x1, waiting for transfers between devices, by_columns(): mid = exchange(blocks)  3.03 us
    ppermute x1, waiting for transfers between devices, by_columns(): rim_a = lax.ppermute(to_first, 'slab', swaps(0))  1.46 us
    ppermute x1, starting transfers between devices, by_columns(): rim_a = lax.ppermute(to_first, 'slab', swaps(0))  1.36 us
    ppermute x1, starting transfers between devices, by_columns(): over2 = lax.ppermute(sent2, 'filt', [(0, 1), (1, 0)])  1.36 us
    ppermute x1, starting transfers between devices, by_columns(): over3 = lax.ppermute(sent3, 'filt', [(0, 1), (1, 0)])  1.3 us
  transfers between devices with their start and end apart: 7, of which 3 were waited for; matrix products, arithmetic and copies ran while one was open for 0% of the time, Pallas kernels for 10%

profile of v9, /device:TPU:17, one launch (start us, length us, event | category | flops | bytes accessed | tf_op | source)
XLA Modules:
  0.0 32.6 jit_solution(18163480550083432749)
XLA Ops:
  0.6 0.0 copy-start
  0.6 0.0 copy-start.1
  0.7 0.0 copy-start.4
  0.7 2.0 %shard_map.86 = (bf16[8,48,256]{2,1,0:T(8,128)(2,1)}, bf16[27,32,64]{2,1,0:T(8,128)(2,1)S(1)}, bf16[27,64,128]{2,1,0:T(8,128)(2,1)S(1)}, bf16[1,64]{1,0:T(2,128)(2,1)S(1)}, bf16[1,64]{1,0:T(2,128)(2,1)S(1)}) custom-call(bf16[256,256]{1,0:T(8,128)(2,1)} %bitcast.11, bf16[27,64,64]{2,1,0:T(8,128)(2,1)} %k2.1, bf16[27,64,128]{2,1,0:T(8,128)(2,1)} %far3.1, ...), custom_call_target="tpu_custom_call" | custom-call | tf_op jit(solution)/shard_map/pallas_call | solution.py:438
  2.6 0.1 shard_map.92
  2.7 1.3 %collective-permute-start.4 = (bf16[864,128]{1,0:T(8,128)(2,1)S(1)}, bf16[864,128]{1,0:T(8,128)(2,1)S(1)}, u32[]{:S(2)}, u32[]{:S(2)}) collective-permute-start(bf16[864,128]{1,0:T(8,128)(2,1)S(1)} %get-tuple-element.53), channel_id=1, source_target_pairs={{0,1},{1,0},{2,3},{3,2},{4,5},{5,4},{6,7},{7,6},{8,9},{9,8},{10,11... | collective-permute-start | bytes 663560 | tf_op jit(solution)/shard_map/ppermute | solution.py:487
  4.0 4.3 %all-to-all-start = ((bf16[8,48,256]{2,1,0:T(8,128)(2,1)}), bf16[8,48,256]{2,1,0:T(8,128)(2,1)S(1)}, u32[]{:S(2)}, u32[]{:S(2)}) async-start(bf16[8,48,256]{2,1,0:T(8,128)(2,1)} %get-tuple-element.31), calls=%async_computation | async-start | bytes 393216 | tf_op jit(solution)/shard_map/all_to_all | solution.py:483
  8.3 1.4 %collective-permute-start.2 = (bf16[448,128]{1,0:T(8,128)(2,1)S(1)}, bf16[448,128]{1,0:T(8,128)(2,1)S(1)}, u32[]{:S(2)}, u32[]{:S(2)}) collective-permute-start(bf16[448,128]{1,0:T(8,128)(2,1)S(1)} %get-tuple-element.48), channel_id=1, source_target_pairs={{0,1},{1,0},{2,3},{3,2},{4,5},{5,4},{6,7},{7,6},{8,9},{9,8},{10,11... | collective-permute-start | bytes 344072 | tf_op jit(solution)/shard_map/ppermute | solution.py:486
  9.7 0.0 collective-permute-done.4.over
  9.7 1.0 %collective-permute-start.5 = (bf16[864,128]{1,0:T(8,128)(2,1)S(1)}, bf16[864,128]{1,0:T(8,128)(2,1)S(1)}, u32[]{:S(2)}, u32[]{:S(2)}) collective-permute-start(bf16[864,128]{1,0:T(8,128)(2,1)S(1)} %collective-permute-done.4.over), channel_id=1, source_target_pairs={{0,2},{2,0},{4,6},{6,4},{8,10},{10,8},{12,14},{14,12},{16,18},{18,... | collective-permute-start | bytes 663560 | tf_op jit(solution)/shard_map/ppermute | solution.py:515
  10.6 3.0 %all-to-all-done.mid = bf16[8,48,256]{2,1,0:T(8,128)(2,1)S(1)} async-done(((bf16[8,48,256]{2,1,0:T(8,128)(2,1)}), bf16[8,48,256]{2,1,0:T(8,128)(2,1)S(1)}, u32[]{:S(2)}, u32[]{:S(2)}) %all-to-all-start) | async-done | bytes 196640 | tf_op jit(solution)/shard_map/all_to_all | solution.py:483
  13.7 1.4 %collective-permute-start = (bf16[6,48,256]{2,1,0:T(8,128)(2,1)S(1)}, bf16[6,48,256]{2,1,0:T(8,128)(2,1)S(1)}, u32[]{:S(2)}, u32[]{:S(2)}) collective-permute-start(bf16[6,48,256]{2,1,0:T(8,128)(2,1)S(1)} %get-tuple-element.32), channel_id=1, source_target_pairs={{0,8},{2,10},{4,12},{6,14},{8,0},{10,2},{12,4},{14,6},{16,24},{18,... | collective-permute-start | bytes 442376 | tf_op jit(solution)/shard_map/ppermute | solution.py:511
  15.1 0.0 collective-permute-start.1
  15.1 0.0 collective-permute-done.2.over
  15.1 1.0 %collective-permute-start.3 = (bf16[448,128]{1,0:T(8,128)(2,1)S(1)}, bf16[448,128]{1,0:T(8,128)(2,1)S(1)}, u32[]{:S(2)}, u32[]{:S(2)}) collective-permute-start(bf16[448,128]{1,0:T(8,128)(2,1)S(1)} %collective-permute-done.2.over), channel_id=1, source_target_pairs={{0,2},{2,0},{4,6},{6,4},{8,10},{10,8},{12,14},{14,12},{16,18},{18,... | collective-permute-start | bytes 344072 | tf_op jit(solution)/shard_map/ppermute | solution.py:514
  16.1 0.0 copy-done
  16.1 0.0 copy-done.1
  16.1 0.0 copy-done.4
  16.1 0.0 copy-start.2
  16.1 0.0 copy-start.3
  16.1 0.4 %shard_map.89 = (bf16[256,2304]{1,0:T(8,128)(2,1)S(1)}, bf16[128,1152]{1,0:T(8,128)(2,1)S(1)}, bf16[128,1152]{1,0:T(8,128)(2,1)S(1)}, bf16[128,1152]{1,0:T(8,128...) custom-call(bf16[27,64,64]{2,1,0:T(8,128)(2,1)S(1)} %copy-done.1, ...), custom_call_target="tpu_custom_call" | custom-call | tf_op jit(solution)/shard_map/pallas_call | solution.py:438
  16.5 1.0 %shard_map.90 = (f32[2,2,144,256]{3,2,1,0:T(8,128)S(1)}, f32[192,128]{1,0:T(8,128)S(1)}, f32[144,128]{1,0:T(8,128)S(1)}) custom-call(bf16[8,48,256]{2,1,0:T(8,128)(2,1)S(1)} %all-to-all-done.mid, bf16[256,2304]{1,0:T(8,128)(2,1)S(1)} %get-tuple-element.36.w1a, bf16[128,1152]{1,0:T(8,128)(2,1)S(1)} %get-tuple-element.37.w1c), custom_call_target="tpu_custom_call" | custom-call | tf_op jit(solution)/shard_map/pallas_call | solution.py:438
  17.5 0.0 collective-permute-done.3.beside
  17.5 0.0 copy-done.2
  17.5 0.0 copy-done.3
  17.5 0.2 shard_map.93
  17.8 1.5 %collective-permute-done.rim_a = bf16[6,48,256]{2,1,0:T(8,128)(2,1)S(1)} collective-permute-done((bf16[6,48,256]{2,1,0:T(8,128)(2,1)S(1)}, bf16[6,48,256]{2,1,0:T(8,128)(2,1)S(1)}, u32[]{:S(2)}, u32[]{:S(2)}) %collective-permute-start) | collective-permute-done | bytes 147488 | tf_op jit(solution)/shard_map/ppermute | solution.py:511
  19.2 1.0 %collective-permute-done.1.rim_b = bf16[6,48,256]{2,1,0:T(8,128)(2,1)S(1)} collective-permute-done((bf16[6,48,256]{2,1,0:T(8,128)(2,1)S(1)}, bf16[6,48,256]{2,1,0:T(8,128)(2,1)S(1)}, u32[]{:S(2)}, u32[]{:S(2)}) %collective-permute-start.1) | collective-permute-done | bytes 147488 | tf_op jit(solution)/shard_map/ppermute | solution.py:512
  20.2 0.1 shard_map.88
  20.4 1.0 %shard_map.91 = (bf16[8,48,256]{2,1,0:T(8,128)(2,1)S(1)}, bf16[3,192,256]{2,1,0:T(8,128)(2,1)S(1)}) custom-call(bf16[2,4,144,256]{3,2,1,0:T(8,128)(2,1)S(1)} %get-tuple-element.34.q, bf16[4,144,128]{2,1,0:T(8,128)(2,1)S(1)} %get-tuple-element.35.x34, bf16[256,2304]{1,0:T(8,128)(2,1)S(1)} %get-tuple-element.36.w1a, ...), custom_call_target="tpu_custom_call" | custom-call | tf_op jit(solution)/shard_map/pallas_call | solution.py:438
  21.4 0.6 %shard_map.94.hd = bf16[3,144,512]{2,1,0:T(8,128)(2,1)S(1)} custom-call(bf16[3,192,256]{2,1,0:T(8,128)(2,1)S(1)} %get-tuple-element.41.pd, bf16[256,1152]{1,0:T(8,128)(2,1)S(1)} %get-tuple-element.49.w2a, bf16[256,1152]{1,0:T(8,128)(2,1)S(1)} %get-tuple-element.50.w2c, f32[8,128]{1,0:T(8,128)S(1)} %get-tuple-element.51.b2, ...), custom_call_target="tpu_custom_call" | custom-call | tf_op jit(solution)/shard_map/pallas_call | solution.py:438
  21.9 0.0 collective-permute-done.5.beside
  22.0 0.8 %shard_map.95 = bf16[8,48,256]{2,1,0:T(8,128)(2,1)S(1)} custom-call(bf16[3,144,512]{2,1,0:T(8,128)(2,1)S(1)} %shard_map.94.hd, bf16[27,64,128]{2,1,0:T(8,128)(2,1)S(1)} %get-tuple-element.45.k3, bf16[864,128]{1,0:T(8,128)(2,1)S(1)} %collective-permute-done.4.over, ...), custom_call_target="tpu_custom_call", output_to_operand_aliasing={{}: (5, {})} | custom-call | tf_op jit(solution)/shard_map/pallas_call | solution.py:438
  22.8 8.7 %all_to_all.10.got = bf16[8,48,256]{2,1,0:T(8,128)(2,1)S(1)} all-to-all(bf16[8,48,256]{2,1,0:T(8,128)(2,1)S(1)} %shard_map.95), channel_id=1, replica_groups={{0,1,2,3,4,5,6,7},{8,9,10,11,12,13,14,15},{16,17,18,19,20,21,22,23},{24..., dimensions={0} | all-to-all | bytes 393216 | tf_op jit(solution)/shard_map/all_to_all | solution.py:562
  31.5 1.1 %shard_map.96 = (bf16[256,256]{1,0:T(8,128)(2,1)}, bf16[256,128]{1,0:T(8,128)(2,1)}) custom-call(bf16[8,48,256]{2,1,0:T(8,128)(2,1)S(1)} %all_to_all.10.got, bf16[256,256]{1,0:T(8,128)(2,1)S(1)} %get-tuple-element.56.order, bf16[256,256]{1,0:T(8,128)(2,1)S(1)} %get-tuple-element.57.same), custom_call_target="tpu_custom_call" | custom-call | tf_op jit(solution)/shard_map/pallas_call | solution.py:438
  (1 shorter events, 0.0 us)
Async XLA Ops:
  0.6 15.4 %copy-start = (bf16[27,64,64]{2,1,0:T(8,128)(2,1)S(1)}, bf16[27,64,64]{2,1,0:T(8,128)(2,1)}, u32[]{:S(2)}) copy-start(bf16[27,64,64]{2,1,0:T(8,128)(2,1)} %k2.1) | copy-start | bytes 663556
  0.6 15.4 %copy-start.1 = (bf16[27,64,64]{2,1,0:T(8,128)(2,1)S(1)}, bf16[27,64,64]{2,1,0:T(8,128)(2,1)}, u32[]{:S(2)}) copy-start(bf16[27,64,64]{2,1,0:T(8,128)(2,1)} %k1.1) | copy-start | bytes 663556
  0.7 15.4 %copy-start.4 = (bf16[64]{0:T(256)(128)(2,1)S(1)}, bf16[64]{0:T(256)(128)(2,1)}, u32[]{:S(2)}) copy-start(bf16[64]{0:T(256)(128)(2,1)} %param.9) | copy-start | bytes 388
  2.7 6.9 %collective-permute-start.4 = (bf16[864,128]{1,0:T(8,128)(2,1)S(1)}, bf16[864,128]{1,0:T(8,128)(2,1)S(1)}, u32[]{:S(2)}, u32[]{:S(2)}) collective-permute-start(bf16[864,128]{1,0:T(8,128)(2,1)S(1)} %get-tuple-element.53), channel_id=1, source_target_pairs={{0,1},{1,0},{2,3},{3,2},{4,5},{5,4},{6,7},{7,6},{8,9},{9,8},{10,11... | collective-permute-start | bytes 663560 | tf_op jit(solution)/shard_map/ppermute | solution.py:487
  4.0 9.6 %all-to-all-start = ((bf16[8,48,256]{2,1,0:T(8,128)(2,1)}), bf16[8,48,256]{2,1,0:T(8,128)(2,1)S(1)}, u32[]{:S(2)}, u32[]{:S(2)}) async-start(bf16[8,48,256]{2,1,0:T(8,128)(2,1)} %get-tuple-element.31), calls=%async_computation | async-start | bytes 393216 | tf_op jit(solution)/shard_map/all_to_all | solution.py:483
  8.3 6.8 %collective-permute-start.2 = (bf16[448,128]{1,0:T(8,128)(2,1)S(1)}, bf16[448,128]{1,0:T(8,128)(2,1)S(1)}, u32[]{:S(2)}, u32[]{:S(2)}) collective-permute-start(bf16[448,128]{1,0:T(8,128)(2,1)S(1)} %get-tuple-element.48), channel_id=1, source_target_pairs={{0,1},{1,0},{2,3},{3,2},{4,5},{5,4},{6,7},{7,6},{8,9},{9,8},{10,11... | collective-permute-start | bytes 344072 | tf_op jit(solution)/shard_map/ppermute | solution.py:486
  9.7 12.3 %collective-permute-start.5 = (bf16[864,128]{1,0:T(8,128)(2,1)S(1)}, bf16[864,128]{1,0:T(8,128)(2,1)S(1)}, u32[]{:S(2)}, u32[]{:S(2)}) collective-permute-start(bf16[864,128]{1,0:T(8,128)(2,1)S(1)} %collective-permute-done.4.over), channel_id=1, source_target_pairs={{0,2},{2,0},{4,6},{6,4},{8,10},{10,8},{12,14},{14,12},{16,18},{18,... | collective-permute-start | bytes 663560 | tf_op jit(solution)/shard_map/ppermute | solution.py:515
  13.7 5.5 %collective-permute-start = (bf16[6,48,256]{2,1,0:T(8,128)(2,1)S(1)}, bf16[6,48,256]{2,1,0:T(8,128)(2,1)S(1)}, u32[]{:S(2)}, u32[]{:S(2)}) collective-permute-start(bf16[6,48,256]{2,1,0:T(8,128)(2,1)S(1)} %get-tuple-element.32), channel_id=1, source_target_pairs={{0,8},{2,10},{4,12},{6,14},{8,0},{10,2},{12,4},{14,6},{16,24},{18,... | collective-permute-start | bytes 442376 | tf_op jit(solution)/shard_map/ppermute | solution.py:511
  15.1 5.2 %collective-permute-start.1 = (bf16[6,48,256]{2,1,0:T(8,128)(2,1)S(1)}, bf16[6,48,256]{2,1,0:T(8,128)(2,1)S(1)}, u32[]{:S(2)}, u32[]{:S(2)}) collective-permute-start(bf16[6,48,256]{2,1,0:T(8,128)(2,1)S(1)} %get-tuple-element.33), channel_id=1, source_target_pairs={{0,2},{2,0},{4,6},{6,4},{8,16},{10,18},{12,20},{14,22},{16,8},{18,... | collective-permute-start | bytes 442376 | tf_op jit(solution)/shard_map/ppermute | solution.py:512
  15.1 2.4 %collective-permute-start.3 = (bf16[448,128]{1,0:T(8,128)(2,1)S(1)}, bf16[448,128]{1,0:T(8,128)(2,1)S(1)}, u32[]{:S(2)}, u32[]{:S(2)}) collective-permute-start(bf16[448,128]{1,0:T(8,128)(2,1)S(1)} %collective-permute-done.2.over), channel_id=1, source_target_pairs={{0,2},{2,0},{4,6},{6,4},{8,10},{10,8},{12,14},{14,12},{16,18},{18,... | collective-permute-start | bytes 344072 | tf_op jit(solution)/shard_map/ppermute | solution.py:514
  16.1 1.4 %copy-start.2 = (bf16[64]{0:T(256)(128)(2,1)S(1)}, bf16[64]{0:T(256)(128)(2,1)}, u32[]{:S(2)}) copy-start(bf16[64]{0:T(256)(128)(2,1)} %param.11) | copy-start | bytes 388
  16.1 1.4 %copy-start.3 = (bf16[64]{0:T(256)(128)(2,1)S(1)}, bf16[64]{0:T(256)(128)(2,1)}, u32[]{:S(2)}) copy-start(bf16[64]{0:T(256)(128)(2,1)} %param.13) | copy-start | bytes 388
